TPU v7x, 32 devices: a whole 2x2x4 slice. The times are simulated.
32 devices in a mesh: seq: 8 (over y, x, core), hid: 4 (over z).
Axes of the slice: x: 2, y: 2, z: 4, core: 2. Of those that a mesh axis runs over, the one named last changes fastest.
Arguments:
- tokens: bfloat16 [2048, 768], P('seq'), may hold values from -6 to 6
- query_weight: bfloat16 [768, 768], P(None, 'hid'), may hold values from -0.21875 to 0.21875
- query_shift: float32 [768], P('hid'), may hold values from -3 to 3
- key_weight: bfloat16 [768, 768], P(None, 'hid'), may hold values from -0.21875 to 0.21875
- key_shift: float32 [768], P('hid'), may hold values from -3 to 3
- value_weight: bfloat16 [768, 768], P(None, 'hid'), may hold values from -0.21875 to 0.21875
- value_shift: float32 [768], P('hid'), may hold values from -3 to 3
- mixer_weight: bfloat16 [768, 768], P('hid'), may hold values from -0.875 to 0.875
- mixer_shift: float32 [768], replicated, may hold values from -3 to 3
- conv_taps: float32 [12, 35], P('hid'), may hold values from -0.18 to 0.18
- first_gain: float32 [768], replicated, may hold values from 0.5 to 1.5
- first_shift: float32 [768], replicated, may hold values from -1.75 to 1.75
- up_weight: bfloat16 [768, 3072], P(None, 'hid'), may hold values from -0.21875 to 0.21875
- up_shift: float32 [3072], P('hid'), may hold values from -3 to 3
- down_weight: bfloat16 [3072, 768], P('hid'), may hold values from -0.109375 to 0.109375
- down_shift: float32 [768], replicated, may hold values from -1.75 to 1.75
- second_gain: float32 [768], replicated, may hold values from 0.5 to 1.5
- second_shift: float32 [768], replicated, may hold values from -1.75 to 1.75
- hyperplanes: float32 [32, 64], replicated, may hold values from -6 to 6
- plane_choice: int32 [4, 8], replicated, may hold values from 0 to 31
- doc_lengths: int32 [2], replicated, may hold values from 1 to 1536, 2048 in all
- out_grad: float32 [2048, 768], P('seq'), may hold values from -6 to 6
Outputs:
- layer_out: bfloat16 [2048, 768], P('seq')
- tokens_grad: float32 [2048, 768], P('seq')
- query_grad: float32 [768, 768], P(None, 'hid')
- query_offsets: float32 [768], P('hid')
- key_grad: float32 [768, 768], P(None, 'hid')
- key_offsets: float32 [768], P('hid')
- value_grad: float32 [768, 768], P(None, 'hid')
- value_offsets: float32 [768], P('hid')
- mixer_grad: float32 [768, 768], P('hid')
- mixer_offsets: float32 [768], replicated
- taps_grad: float32 [12, 35], P('hid')
- first_gains: float32 [768], replicated
- first_shifts: float32 [768], replicated
- up_grad: float32 [768, 3072], P(None, 'hid')
- up_offsets: float32 [3072], P('hid')
- down_grad: float32 [3072, 768], P('hid')
- down_offsets: float32 [768], replicated
- second_gains: float32 [768], replicated
- second_shifts: float32 [768], replicated
Inputs may be any that keep to these rules, and one draw needn't show every extreme that they name: `doc_lengths`: the item holds 2 documents one after another; the longest has at most 1536 tokens.
All inputs are finite; a program needn't handle non-finite values.
Results may differ from a plain program's by a relative error of at most 0.034.
Values may be sent and summed in bfloat16 or wider, within the bound.
No kernel may reach another device: no remote copies, remote signals or barrier semaphores. Data moves between devices by JAX's collectives and lax.ppermute only.
A program may use at most 128 MiB of HBM per device.

v0:
```python
import math

import jax
import jax.numpy as jnp
from jax import lax
from jax.sharding import PartitionSpec as P

D = 768
H = 12
BITS = 8
PLANES = 32
HASH_ROUNDS = 4
CONV = 35


SHARP = 2.0
NORM_EPS = 1e-05
UNIT_EPS = 1e-06
UPPER_PRECISION = lax.Precision.HIGHEST
BLOCK_LIMIT = 512


def with_halo(value, sides, width):
    for axis, dim in sides:
        peers, length = (lax.axis_size(axis), value.shape[dim])
        up = [(i, (i + 1) % peers) for i in range(peers - 1)]
        down = [(j, i) for i, j in up]
        last = lax.slice_in_dim(value, length - width, length, axis=dim)
        first = lax.slice_in_dim(value, 0, width, axis=dim)
        before = lax.ppermute(last, axis, up)
        after = lax.ppermute(first, axis, down)
        value = jnp.concatenate([before, value, after], axis=dim)
    return value


def doc_index(positions, doc_lengths):
    starts = jnp.cumsum(doc_lengths) - doc_lengths
    inside = (positions >= 0) & (positions < jnp.sum(doc_lengths))
    found = jnp.sum((positions[:, None] >= starts[None, :]).astype(jnp.int32), axis=1) - 1
    return jnp.where(inside, found, -1)


def feature_tree(picked):
    lead = picked.shape[:-1]
    parts = picked.reshape(lead + (HASH_ROUNDS, BITS))
    features = jnp.ones(lead + (HASH_ROUNDS, 1), jnp.float32)
    for bit in range(BITS):
        features = jnp.concatenate([features, features * parts[..., bit : bit + 1]], axis=-1)
    return (features * 2.0 ** (-0.5 * BITS)).reshape(lead + (HASH_ROUNDS * 2**BITS,))


def expand_codes(codes, chooser):
    picked = jnp.einsum("rhp,pc->rhc", codes, chooser, preferred_element_type=jnp.float32)
    return feature_tree(picked).astype(jnp.bfloat16)


def codes_back(codes, feature_grad, chooser_wide):
    picked = jnp.einsum(
        "rhp,pc->rhc", codes.astype(jnp.float32), chooser_wide, precision=UPPER_PRECISION
    )
    unused, pull = jax.vjp(feature_tree, picked)
    picked_grad = pull(feature_grad)[0]
    return jnp.einsum("rhc,pc->rhp", picked_grad, chooser_wide, precision=UPPER_PRECISION)


def unit_back(code_grad, tanh_value, raw, scale, hyperplanes):
    pre_grad = code_grad * SHARP * (1.0 - tanh_value * tanh_value)
    unit_grad = jnp.einsum("rhp,pd->rhd", pre_grad, hyperplanes, precision=UPPER_PRECISION)
    inner = jnp.sum(raw * unit_grad, axis=-1, keepdims=True)
    return unit_grad * scale - raw * (scale * scale * scale) * inner


def norm_forward(rows, gain, shift):
    center = rows - jnp.mean(rows, axis=-1, keepdims=True)
    inverse = lax.rsqrt(jnp.mean(center * center, axis=-1, keepdims=True) + NORM_EPS)
    normed = center * inverse
    return (normed * gain + shift, normed, inverse)


def norm_backward(grad, normed, inverse, gain):
    scaled = grad * gain
    rows_grad = inverse * (
        scaled
        - jnp.mean(scaled, axis=-1, keepdims=True)
        - normed * jnp.mean(scaled * normed, axis=-1, keepdims=True)
    )
    return (rows_grad, jnp.sum(grad * normed, axis=0), jnp.sum(grad, axis=0))


def masked_scores(query_feature_rows, key_feature_rows, same):
    collision_scores = (
        jnp.einsum(
            "rbl,jbl->brj", query_feature_rows, key_feature_rows, preferred_element_type=jnp.float32
        )
        / HASH_ROUNDS
    )
    return jnp.where(same[None], collision_scores, 0.0)


def mix_gradient(weighted_grad, total_grad, block_values, same):
    mixing = jnp.einsum(
        "qhe,khe->hqk", weighted_grad, block_values, preferred_element_type=jnp.float32
    )
    mixing = mixing + total_grad.T[:, :, None]
    return jnp.where(same[None], mixing, 0.0).astype(jnp.bfloat16)


def on_device(
    tokens,
    query_weight,
    query_shift,
    key_weight,
    key_shift,
    value_weight,
    value_shift,
    mixer_weight,
    mixer_shift,
    conv_taps,
    first_gain,
    first_shift,
    up_weight,
    up_shift,
    down_weight,
    down_shift,
    second_gain,
    second_shift,
    hyperplanes,
    plane_choice,
    doc_lengths,
    out_grad,
):
    count = tokens.shape[0]
    place = lax.axis_index("seq")
    head_size = D // H
    heads = query_weight.shape[1] // head_size
    radius = (CONV - 1) // 2
    first_row = place * count
    segment = doc_index(first_row + jnp.arange(count, dtype=jnp.int32), doc_lengths)
    chooser_wide = (
        jnp.arange(PLANES, dtype=jnp.int32)[:, None] == plane_choice.reshape(1, -1)
    ).astype(jnp.float32)
    chooser = chooser_wide.astype(jnp.bfloat16)
    feature_width = HASH_ROUNDS * 2**BITS

    def project(weight, shift):
        return (jnp.dot(tokens, weight, preferred_element_type=jnp.float32) + shift).reshape(
            count, heads, head_size
        )

    query = project(query_weight, query_shift)
    keys = project(key_weight, key_shift)
    values = project(value_weight, value_shift)
    query_scale = lax.rsqrt(jnp.sum(query * query, axis=-1, keepdims=True) + UNIT_EPS)
    key_scale = lax.rsqrt(jnp.sum(keys * keys, axis=-1, keepdims=True) + UNIT_EPS)
    query_tanh = jnp.tanh(
        SHARP
        * jnp.einsum("rhd,pd->rhp", query * query_scale, hyperplanes, precision=UPPER_PRECISION)
    )
    key_tanh = jnp.tanh(
        SHARP * jnp.einsum("rhd,pd->rhp", keys * key_scale, hyperplanes, precision=UPPER_PRECISION)
    )
    query_codes = query_tanh.astype(jnp.bfloat16)
    key_codes = key_tanh.astype(jnp.bfloat16)
    value_low = values.astype(jnp.bfloat16)
    query_feature_rows = expand_codes(query_codes, chooser)
    key_pack = jnp.concatenate([key_codes, value_low], axis=-1)
    piece = lax.all_gather(key_pack, "seq", axis=0, tiled=True)
    step_rows = math.gcd(piece.shape[0], BLOCK_LIMIT)

    def one_block(turn, inner):
        offset = turn * step_rows
        block = lax.dynamic_slice_in_dim(piece, offset, step_rows, 0)
        key_segment = doc_index(offset + jnp.arange(step_rows, dtype=jnp.int32), doc_lengths)

        def compute(state):
            same = segment[:, None] == key_segment[None, :]
            weights = masked_scores(
                query_feature_rows, expand_codes(block[..., :PLANES], chooser), same
            )
            weighted = state[0] + jnp.einsum(
                "hqk,khe->qhe",
                weights.astype(jnp.bfloat16),
                block[..., PLANES:],
                preferred_element_type=jnp.float32,
            )
            return (weighted, state[1] + jnp.sum(weights, axis=-1).T)

        return compute(inner)

    weighted, total = lax.fori_loop(
        0,
        piece.shape[0] // step_rows,
        one_block,
        (jnp.zeros((count, heads, head_size), jnp.float32), jnp.zeros((count, heads), jnp.float32)),
    )
    total = total + 1.0
    flat_values = value_low.reshape(count, heads * head_size)
    padded = with_halo(flat_values, (("seq", 0),), radius)
    padded_segment = doc_index(
        first_row - radius + jnp.arange(count + 2 * radius, dtype=jnp.int32), doc_lengths
    )
    conv_out = jnp.zeros((count, heads, head_size), jnp.float32)
    shifted_list = []
    for tap in range(CONV):
        same = (padded_segment[tap : tap + count] == segment).astype(jnp.float32)
        shifted = (
            padded[tap : tap + count].reshape(count, heads, head_size).astype(jnp.float32)
            * same[:, None, None]
        )
        shifted_list.append(shifted)
        conv_out = conv_out + conv_taps[:, tap][None, :, None] * shifted
    context = (
        (weighted / total[:, :, None] + conv_out)
        .reshape(count, heads * head_size)
        .astype(jnp.bfloat16)
    )
    mixed = (
        lax.psum(jnp.dot(context, mixer_weight, preferred_element_type=jnp.float32), "hid")
        + mixer_shift
    )
    first_out, first_normed, first_inverse = norm_forward(
        tokens.astype(jnp.float32) + mixed, first_gain, first_shift
    )
    first_low = first_out.astype(jnp.bfloat16)
    upward = jnp.dot(first_low, up_weight, preferred_element_type=jnp.float32) + up_shift
    hidden = jax.nn.gelu(upward, approximate=False).astype(jnp.bfloat16)
    downward = (
        lax.psum(jnp.dot(hidden, down_weight, preferred_element_type=jnp.float32), "hid")
        + down_shift
    )
    second_out, second_normed, second_inverse = norm_forward(
        first_out + downward, second_gain, second_shift
    )
    layer_out = second_out.astype(jnp.bfloat16)
    second_grad, second_gains, second_shifts = norm_backward(
        out_grad, second_normed, second_inverse, second_gain
    )
    down_low = second_grad.astype(jnp.bfloat16)
    down_grad = jnp.einsum("rf,rd->fd", hidden, down_low, preferred_element_type=jnp.float32)
    down_offsets = jnp.sum(down_low.astype(jnp.float32), axis=0)
    hidden_grad = jnp.einsum("rd,fd->rf", down_low, down_weight, preferred_element_type=jnp.float32)
    unused, gelu_pull = jax.vjp(
        lambda inner_value: jax.nn.gelu(inner_value, approximate=False), upward
    )
    up_low = gelu_pull(hidden_grad)[0].astype(jnp.bfloat16)
    up_grad = jnp.einsum("rd,rf->df", first_low, up_low, preferred_element_type=jnp.float32)
    up_offsets = jnp.sum(up_low.astype(jnp.float32), axis=0)
    first_back = (
        lax.psum(
            jnp.einsum("rf,df->rd", up_low, up_weight, preferred_element_type=jnp.float32), "hid"
        )
        + second_grad
    )
    first_grad, first_gains, first_shifts = norm_backward(
        first_back, first_normed, first_inverse, first_gain
    )
    mixed_low = first_grad.astype(jnp.bfloat16)
    mixer_grad = jnp.einsum("rc,rd->cd", context, mixed_low, preferred_element_type=jnp.float32)
    mixer_offsets = jnp.sum(mixed_low.astype(jnp.float32), axis=0)
    context_grad = jnp.einsum(
        "rd,cd->rc", mixed_low, mixer_weight, preferred_element_type=jnp.float32
    ).reshape(count, heads, head_size)
    weighted_grad = (context_grad / total[:, :, None]).astype(jnp.bfloat16)
    total_grad = -jnp.sum(context_grad * weighted, axis=-1) / (total * total)
    padded_grad = with_halo(
        context_grad.reshape(count, heads * head_size).astype(jnp.bfloat16), (("seq", 0),), radius
    ).astype(jnp.float32)
    conv_value_grad = jnp.zeros((count, heads, head_size), jnp.float32)
    taps_columns = []
    for tap in range(CONV):
        offset = CONV - 1 - tap
        same = (padded_segment[offset : offset + count] == segment).astype(jnp.float32)
        moved = (
            padded_grad[offset : offset + count].reshape(count, heads, head_size)
            * same[:, None, None]
        )
        conv_value_grad = conv_value_grad + conv_taps[:, tap][None, :, None] * moved
        taps_columns.append(jnp.sum(context_grad * shifted_list[tap], axis=(0, 2)))
    taps_grad = jnp.stack(taps_columns, axis=1)
    fold_piece = lax.all_gather(key_pack, "seq", axis=0, tiled=True)
    fold_step_rows = math.gcd(fold_piece.shape[0], BLOCK_LIMIT)

    def one_block(turn, inner):
        offset = turn * fold_step_rows
        block = lax.dynamic_slice_in_dim(fold_piece, offset, fold_step_rows, 0)
        key_segment = doc_index(offset + jnp.arange(fold_step_rows, dtype=jnp.int32), doc_lengths)

        def compute(state):
            same = segment[:, None] == key_segment[None, :]
            block_feature_rows = expand_codes(block[..., :PLANES], chooser)
            mixing_reduced = mix_gradient(weighted_grad, total_grad, block[..., PLANES:], same)
            return state + jnp.einsum(
                "bvp,pbt->vbt",
                mixing_reduced,
                block_feature_rows,
                preferred_element_type=jnp.float32,
            )

        return compute(inner)

    query_feature_grad = lax.fori_loop(
        0,
        fold_piece.shape[0] // fold_step_rows,
        one_block,
        jnp.zeros((count, heads, feature_width), jnp.float32),
    )
    key_feature_rows = expand_codes(key_codes, chooser)
    query_pack = jnp.concatenate([query_codes, weighted_grad], axis=-1).astype(jnp.float32)

    def fold_queries(summed, pieces):
        packs, totals = pieces
        step_rows = math.gcd(packs.shape[0], BLOCK_LIMIT)

        def one_block(turn, inner):
            offset = turn * step_rows
            block = lax.dynamic_slice_in_dim(packs, offset, step_rows, 0)
            block_totals = lax.dynamic_slice_in_dim(totals, offset, step_rows, 0)
            query_segment = doc_index(offset + jnp.arange(step_rows, dtype=jnp.int32), doc_lengths)

            def compute(state):
                same = query_segment[:, None] == segment[None, :]
                block_feature_rows = expand_codes(block[..., :PLANES].astype(jnp.bfloat16), chooser)
                block_grad = block[..., PLANES:].astype(jnp.bfloat16)
                weights = masked_scores(block_feature_rows, key_feature_rows, same)
                mixing_reduced = mix_gradient(block_grad, block_totals, value_low, same)
                feature_sum = state[0] + jnp.einsum(
                    "ain,iam->nam",
                    mixing_reduced,
                    block_feature_rows,
                    preferred_element_type=jnp.float32,
                )
                value_sum = state[1] + jnp.einsum(
                    "hqk,qhe->khe",
                    weights.astype(jnp.bfloat16),
                    block_grad,
                    preferred_element_type=jnp.float32,
                )
                return (feature_sum, value_sum)

            return compute(inner)

        return lax.fori_loop(0, packs.shape[0] // step_rows, one_block, summed)

    key_feature_grad, value_attn_grad = fold_queries(
        (
            jnp.zeros((count, heads, feature_width), jnp.float32),
            jnp.zeros((count, heads, head_size), jnp.float32),
        ),
        (
            lax.all_gather(query_pack.astype(jnp.bfloat16), "seq", axis=0, tiled=True).astype(
                jnp.float32
            ),
            lax.all_gather(total_grad.astype(jnp.bfloat16), "seq", axis=0, tiled=True).astype(
                jnp.float32
            ),
        ),
    )
    key_code_grad = codes_back(key_codes, key_feature_grad / HASH_ROUNDS, chooser_wide)
    query_code_grad = codes_back(query_codes, query_feature_grad / HASH_ROUNDS, chooser_wide)
    query_low = (
        unit_back(query_code_grad, query_tanh, query, query_scale, hyperplanes)
        .reshape(count, heads * head_size)
        .astype(jnp.bfloat16)
    )
    key_low = (
        unit_back(key_code_grad, key_tanh, keys, key_scale, hyperplanes)
        .reshape(count, heads * head_size)
        .astype(jnp.bfloat16)
    )
    value_grad_low = (
        (value_attn_grad + conv_value_grad).reshape(count, heads * head_size).astype(jnp.bfloat16)
    )

    def weight_grad(grad_low):
        return jnp.einsum("rd,rc->dc", tokens, grad_low, preferred_element_type=jnp.float32)

    def back_input(grad_low, weight):
        return jnp.einsum("rc,dc->rd", grad_low, weight, preferred_element_type=jnp.float32)

    tokens_grad = (
        lax.psum(
            (
                back_input(query_low, query_weight)
                + back_input(key_low, key_weight)
                + back_input(value_grad_low, value_weight)
            ).astype(jnp.bfloat16),
            "hid",
        ).astype(jnp.float32)
        + first_grad
    )
    summed = (
        lax.psum(weight_grad(query_low).astype(jnp.bfloat16), "seq").astype(jnp.float32),
        lax.psum(jnp.sum(query_low.astype(jnp.float32), axis=0).astype(jnp.bfloat16), "seq").astype(
            jnp.float32
        ),
        lax.psum(weight_grad(key_low).astype(jnp.bfloat16), "seq").astype(jnp.float32),
        lax.psum(jnp.sum(key_low.astype(jnp.float32), axis=0).astype(jnp.bfloat16), "seq").astype(
            jnp.float32
        ),
        lax.psum(weight_grad(value_grad_low).astype(jnp.bfloat16), "seq").astype(jnp.float32),
        lax.psum(
            jnp.sum(value_grad_low.astype(jnp.float32), axis=0).astype(jnp.bfloat16), "seq"
        ).astype(jnp.float32),
        lax.psum(mixer_grad.astype(jnp.bfloat16), "seq").astype(jnp.float32),
        lax.psum(mixer_offsets.astype(jnp.bfloat16), "seq").astype(jnp.float32),
        lax.psum(taps_grad.astype(jnp.bfloat16), "seq").astype(jnp.float32),
        lax.psum(first_gains.astype(jnp.bfloat16), "seq").astype(jnp.float32),
        lax.psum(first_shifts.astype(jnp.bfloat16), "seq").astype(jnp.float32),
        lax.psum(up_grad.astype(jnp.bfloat16), "seq").astype(jnp.float32),
        lax.psum(up_offsets.astype(jnp.bfloat16), "seq").astype(jnp.float32),
        lax.psum(down_grad.astype(jnp.bfloat16), "seq").astype(jnp.float32),
        lax.psum(down_offsets.astype(jnp.bfloat16), "seq").astype(jnp.float32),
        lax.psum(second_gains.astype(jnp.bfloat16), "seq").astype(jnp.float32),
        lax.psum(second_shifts.astype(jnp.bfloat16), "seq").astype(jnp.float32),
    )
    return (
        layer_out,
        tokens_grad,
        summed[0],
        summed[1],
        summed[2],
        summed[3],
        summed[4],
        summed[5],
        summed[6],
        summed[7],
        summed[8],
        summed[9],
        summed[10],
        summed[11],
        summed[12],
        summed[13],
        summed[14],
        summed[15],
        summed[16],
    )


def solution(mesh):
    placed = (
        P("seq", None),
        P(None, "hid"),
        P("hid"),
        P(None, "hid"),
        P("hid"),
        P(None, "hid"),
        P("hid"),
        P("hid", None),
        P(),
        P("hid", None),
        P(),
        P(),
        P(None, "hid"),
        P("hid"),
        P("hid", None),
        P(),
        P(),
        P(),
        P(),
        P(),
        P(),
        P("seq", None),
    )
    return jax.shard_map(
        on_device,
        mesh=mesh,
        in_specs=placed,
        out_specs=(
            P("seq", None),
            P("seq", None),
            P(None, "hid"),
            P("hid"),
            P(None, "hid"),
            P("hid"),
            P(None, "hid"),
            P("hid"),
            P("hid", None),
            P(),
            P("hid", None),
            P(),
            P(),
            P(None, "hid"),
            P("hid"),
            P("hid", None),
            P(),
            P(),
            P(),
        ),
        check_vma=False,
    )
```

profile of v0, /device:TPU:0, one launch (start us, length us, event | category | flops | bytes accessed | tf_op | source)
XLA Modules:
  0.0 1006.9 jit_solution(6511966222402936166)
XLA Ops:
  41.0 8.9 concatenate.418
  79.0 9.7 concatenate.443
  100.1 193.8 %while.52 = (s32[]{:T(128)}, f32[256,3,64]{0,2,1:T(8,128)}, f32[256,3]{0,1:T(4,128)}, bf16[2048,3,96]{0,2,1:T(8,128)(2,1)}, s32[256]{0:T(256)S(1)}, /*index=5*/s...) while((s32[]{:T(128)}, f32[256,3,64]{0,2,1:T(8,128)}, ...), condition=%wide.region_8.9_spmd.clone, body=%wide.region_5.8_spmd.clone.sunk | while | flops 865498880 | bytes 65906848 | solution.py:190
  110.5 9.0 concatenate.504
  123.4 16.9 %concatenate.505 = f32[512,3,4,256]{0,3,2,1:T(8,128)} concatenate(f32[512,3,4,1]{0,3,2,1:T(1,128)} %copy-done.7, f32[512,3,4,1]{0,3,2,1:T(1,128)} %copy-done.6, f32[512,3,4,2]{0,3,2,1:T(2,128)} %copy-done.5, f32[512,3,4,4]{0,3,2,1:T(4,128)} %copy-done.4, f32[512,3,4,8]{0,3,2,1:T(8,128)} %copy-done.3, f32[512,3,4,16]{0,3,2,1:T(8,128)} %copy-done.2, ...), dimensions={3} | concatenate | bytes 12582912 | tf_op jit(solution)/shard_map/while/body/eval_jaxpr/concatenate | solution.py:48
  158.9 9.0 concatenate.504
  171.8 16.9 %concatenate.505 = f32[512,3,4,256]{0,3,2,1:T(8,128)} concatenate(f32[512,3,4,1]{0,3,2,1:T(1,128)} %copy-done.7, f32[512,3,4,1]{0,3,2,1:T(1,128)} %copy-done.6, f32[512,3,4,2]{0,3,2,1:T(2,128)} %copy-done.5, f32[512,3,4,4]{0,3,2,1:T(4,128)} %copy-done.4, f32[512,3,4,8]{0,3,2,1:T(8,128)} %copy-done.3, f32[512,3,4,16]{0,3,2,1:T(8,128)} %copy-done.2, ...), dimensions={3} | concatenate | bytes 12582912 | tf_op jit(solution)/shard_map/while/body/eval_jaxpr/concatenate | solution.py:48
  207.2 9.0 concatenate.504
  220.1 16.9 %concatenate.505 = f32[512,3,4,256]{0,3,2,1:T(8,128)} concatenate(f32[512,3,4,1]{0,3,2,1:T(1,128)} %copy-done.7, f32[512,3,4,1]{0,3,2,1:T(1,128)} %copy-done.6, f32[512,3,4,2]{0,3,2,1:T(2,128)} %copy-done.5, f32[512,3,4,4]{0,3,2,1:T(4,128)} %copy-done.4, f32[512,3,4,8]{0,3,2,1:T(8,128)} %copy-done.3, f32[512,3,4,16]{0,3,2,1:T(8,128)} %copy-done.2, ...), dimensions={3} | concatenate | bytes 12582912 | tf_op jit(solution)/shard_map/while/body/eval_jaxpr/concatenate | solution.py:48
  255.5 9.0 concatenate.504
  268.4 16.9 %concatenate.505 = f32[512,3,4,256]{0,3,2,1:T(8,128)} concatenate(f32[512,3,4,1]{0,3,2,1:T(1,128)} %copy-done.7, f32[512,3,4,1]{0,3,2,1:T(1,128)} %copy-done.6, f32[512,3,4,2]{0,3,2,1:T(2,128)} %copy-done.5, f32[512,3,4,4]{0,3,2,1:T(4,128)} %copy-done.4, f32[512,3,4,8]{0,3,2,1:T(8,128)} %copy-done.3, f32[512,3,4,16]{0,3,2,1:T(8,128)} %copy-done.2, ...), dimensions={3} | concatenate | bytes 12582912 | tf_op jit(solution)/shard_map/while/body/eval_jaxpr/concatenate | solution.py:48
  306.2 41.1 %all-reduce.31.cloned.1.call-done = f32[256,768]{1,0:T(8,128)} async-done(((f32[256,768]{1,0:T(8,128)}), f32[256,768]{1,0:T(8,128)}) %all-reduce.31.cloned.1.call-update) | async-done | bytes 786448 | tf_op jit(solution)/shard_map/psum | solution.py:218
  355.0 9.3 concatenate.434
  373.7 23.1 %all-reduce.33.cloned.1.call-done = f32[256,768]{1,0:T(8,128)} async-done(((f32[256,768]{1,0:T(8,128)}), f32[256,768]{1,0:T(8,128)}) %all-reduce.33.cloned.1.call-update) | async-done | bytes 786448 | tf_op jit(solution)/shard_map/psum | solution.py:228
  416.4 32.4 %all-reduce.35.cloned.1.call-done = f32[256,768]{1,0:T(8,128)} async-done(((f32[256,768]{1,0:T(8,128)}), f32[256,768]{1,0:T(8,128)}) %all-reduce.35.cloned.1.call-update) | async-done | bytes 786448 | tf_op jit(solution)/shard_map/psum | solution.py:249
  455.8 176.6 %while.53 = (s32[]{:T(128)}, f32[256,3,1024]{0,2,1:T(8,128)}, bf16[2048,3,96]{0,2,1:T(8,128)(2,1)}, s32[256]{0:T(256)S(1)}, s32[]{:T(128)}, /*index=5*/s32[1,2]{...) while((s32[]{:T(128)}, f32[256,3,1024]{0,2,1:T(8,128)}, ...), condition=%wide.region_24.25_spmd.clone, body=%wide.region_22.24_spmd.clone.sunk | while | flops 866579456 | bytes 57516792 | solution.py:301
  463.9 6.3 concatenate.510
  474.1 14.1 %concatenate.511 = f32[512,3,4,256]{0,3,2,1:T(8,128)} concatenate(f32[512,3,4,1]{0,3,2,1:T(1,128)S(1)} %broadcast.981, f32[512,3,4,1]{0,3,2,1:T(1,128)S(1)} %get-tuple-element.1588, f32[512,3,4,2]{0,3,2,1:T(2,128)S(1)} %pad_multiply_fusion.13, f32[512,3,4,4]{0,3,2,1:T(4,128)S(1)} %maximum_multiply_fusion.14, f32[512,3,4,8]{0,3,2,1:T(8,128)S(1)} %maximum_multiply_fusion.15, ...), dimensions={3} | concatenate | bytes 12582912 | tf_op jit(solution)/shard_map/while/body/eval_jaxpr/concatenate | solution.py:48
  507.2 6.3 concatenate.510
  517.4 14.1 %concatenate.511 = f32[512,3,4,256]{0,3,2,1:T(8,128)} concatenate(f32[512,3,4,1]{0,3,2,1:T(1,128)S(1)} %broadcast.981, f32[512,3,4,1]{0,3,2,1:T(1,128)S(1)} %get-tuple-element.1588, f32[512,3,4,2]{0,3,2,1:T(2,128)S(1)} %pad_multiply_fusion.13, f32[512,3,4,4]{0,3,2,1:T(4,128)S(1)} %maximum_multiply_fusion.14, f32[512,3,4,8]{0,3,2,1:T(8,128)S(1)} %maximum_multiply_fusion.15, ...), dimensions={3} | concatenate | bytes 12582912 | tf_op jit(solution)/shard_map/while/body/eval_jaxpr/concatenate | solution.py:48
  551.5 6.3 concatenate.510
  561.8 14.1 %concatenate.511 = f32[512,3,4,256]{0,3,2,1:T(8,128)} concatenate(f32[512,3,4,1]{0,3,2,1:T(1,128)S(1)} %broadcast.981, f32[512,3,4,1]{0,3,2,1:T(1,128)S(1)} %get-tuple-element.1588, f32[512,3,4,2]{0,3,2,1:T(2,128)S(1)} %pad_multiply_fusion.13, f32[512,3,4,4]{0,3,2,1:T(4,128)S(1)} %maximum_multiply_fusion.14, f32[512,3,4,8]{0,3,2,1:T(8,128)S(1)} %maximum_multiply_fusion.15, ...), dimensions={3} | concatenate | bytes 12582912 | tf_op jit(solution)/shard_map/while/body/eval_jaxpr/concatenate | solution.py:48
  595.9 6.3 concatenate.510
  606.1 14.1 %concatenate.511 = f32[512,3,4,256]{0,3,2,1:T(8,128)} concatenate(f32[512,3,4,1]{0,3,2,1:T(1,128)S(1)} %broadcast.981, f32[512,3,4,1]{0,3,2,1:T(1,128)S(1)} %get-tuple-element.1588, f32[512,3,4,2]{0,3,2,1:T(2,128)S(1)} %pad_multiply_fusion.13, f32[512,3,4,4]{0,3,2,1:T(4,128)S(1)} %maximum_multiply_fusion.14, f32[512,3,4,8]{0,3,2,1:T(8,128)S(1)} %maximum_multiply_fusion.15, ...), dimensions={3} | concatenate | bytes 12582912 | tf_op jit(solution)/shard_map/while/body/eval_jaxpr/concatenate | solution.py:48
  643.1 8.9 all_gather.12
  660.5 200.4 %while.54 = (s32[]{:T(128)}, f32[256,3,1024]{0,2,1:T(8,128)}, f32[256,3,64]{0,2,1:T(8,128)}, bf16[2048,3,96]{0,2,1:T(8,128)(2,1)}, s32[]{:T(128)}, /*index=5*/s3...) while((s32[]{:T(128)}, f32[256,3,1024]{0,2,1:T(8,128)}, ...), condition=%wide.region_35.36_spmd.clone, body=%wide.region_33.35_spmd.clone.sunk | while | flops 1723495424 | bytes 71427520 | solution.py:342
  680.0 14.1 %concatenate.517 = f32[512,3,4,256]{0,3,2,1:T(8,128)} concatenate(f32[512,3,4,1]{0,3,2,1:T(1,128)S(1)} %broadcast.990, f32[512,3,4,1]{0,3,2,1:T(1,128)S(1)} %get-tuple-element.1613, f32[512,3,4,2]{0,3,2,1:T(2,128)S(1)} %pad_multiply_fusion.14, f32[512,3,4,4]{0,3,2,1:T(4,128)S(1)} %maximum_multiply_fusion.16, f32[512,3,4,8]{0,3,2,1:T(8,128)S(1)} %maximum_multiply_fusion.17, ...), dimensions={3} | concatenate | bytes 12582912 | tf_op jit(solution)/shard_map/while/body/eval_jaxpr/concatenate | solution.py:48
  729.3 14.1 %concatenate.517 = f32[512,3,4,256]{0,3,2,1:T(8,128)} concatenate(f32[512,3,4,1]{0,3,2,1:T(1,128)S(1)} %broadcast.990, f32[512,3,4,1]{0,3,2,1:T(1,128)S(1)} %get-tuple-element.1613, f32[512,3,4,2]{0,3,2,1:T(2,128)S(1)} %pad_multiply_fusion.14, f32[512,3,4,4]{0,3,2,1:T(4,128)S(1)} %maximum_multiply_fusion.16, f32[512,3,4,8]{0,3,2,1:T(8,128)S(1)} %maximum_multiply_fusion.17, ...), dimensions={3} | concatenate | bytes 12582912 | tf_op jit(solution)/shard_map/while/body/eval_jaxpr/concatenate | solution.py:48
  779.6 14.1 %concatenate.517 = f32[512,3,4,256]{0,3,2,1:T(8,128)} concatenate(f32[512,3,4,1]{0,3,2,1:T(1,128)S(1)} %broadcast.990, f32[512,3,4,1]{0,3,2,1:T(1,128)S(1)} %get-tuple-element.1613, f32[512,3,4,2]{0,3,2,1:T(2,128)S(1)} %pad_multiply_fusion.14, f32[512,3,4,4]{0,3,2,1:T(4,128)S(1)} %maximum_multiply_fusion.16, f32[512,3,4,8]{0,3,2,1:T(8,128)S(1)} %maximum_multiply_fusion.17, ...), dimensions={3} | concatenate | bytes 12582912 | tf_op jit(solution)/shard_map/while/body/eval_jaxpr/concatenate | solution.py:48
  829.8 14.1 %concatenate.517 = f32[512,3,4,256]{0,3,2,1:T(8,128)} concatenate(f32[512,3,4,1]{0,3,2,1:T(1,128)S(1)} %broadcast.990, f32[512,3,4,1]{0,3,2,1:T(1,128)S(1)} %get-tuple-element.1613, f32[512,3,4,2]{0,3,2,1:T(2,128)S(1)} %pad_multiply_fusion.14, f32[512,3,4,4]{0,3,2,1:T(4,128)S(1)} %maximum_multiply_fusion.16, f32[512,3,4,8]{0,3,2,1:T(8,128)S(1)} %maximum_multiply_fusion.17, ...), dimensions={3} | concatenate | bytes 12582912 | tf_op jit(solution)/shard_map/while/body/eval_jaxpr/concatenate | solution.py:48
  900.2 24.0 %all-reduce.23 = (bf16[192]{0:T(256)(128)(2,1)S(1)}, bf16[192]{0:T(256)(128)(2,1)S(1)}, bf16[192]{0:T(256)(128)(2,1)S(1)}, bf16[768]{0:T(1024)(128)(2,1)S(1)}, b...) all-reduce(bf16[192]{0:T(256)(128)(2,1)S(1)} %reduce_sum.1073, ...), channel_id=1, replica_groups=mesh['seq'=8,'hid'=4] {'seq'}, use_global_device_ids=true, to_apply=%region_47.48 | all-reduce | flops 6057 | bytes 24228 | tf_op jit(solution)/shard_map/psum | solution.py:393
  932.6 58.5 %all-reduce.39.cloned.1.call-done = (bf16[768,192]{0,1:T(8,128)(2,1)}, bf16[768,192]{0,1:T(8,128)(2,1)}, bf16[768,192]{0,1:T(8,128)(2,1)}, bf16[192,768]{1,0:T(8...) async-done(((bf16[768,192]{0,1:T(8,128)(2,1)}, bf16[768,192]{0,1:T(8,128)(2,1)}, bf16[768,192]{0,1:T(8,128)(2,1)}, bf16[192,768]{1,0:T(8,128)(2,1)}, ...) | async-done | bytes 3538960 | tf_op jit(solution)/shard_map/psum | solution.py:392
  (1289 shorter events, 528.3 us)
Async XLA Ops:
  7.2 341.8 %copy-start = (bf16[768,768]{1,0:T(8,128)(2,1)S(1)}, bf16[768,768]{1,0:T(8,128)(2,1)}, u32[]{:S(2)}) copy-start(bf16[768,768]{1,0:T(8,128)(2,1)} %param.40) | copy-start | bytes 3538948
  7.3 92.8 %all-gather.3.cloned.1.call-start = ((), (), s32[]{:S(2)}) async-start(), calls=%async_computation | async-start | bytes 1327104 | tf_op jit(solution)/shard_map/all_gather | solution.py:167
  8.8 88.3 %copy-start.8 = (bf16[256,192]{0,1:T(8,128)(2,1)}, bf16[256,192]{0,1:T(8,128)(2,1)S(1)}, u32[]{:S(2)}) copy-start(bf16[256,192]{0,1:T(8,128)(2,1)S(1)} %fusion.61) | copy-start | bytes 294916
  9.6 79.2 %collective-permute-start.1 = (bf16[17,192]{0,1:T(8,128)(2,1)}, bf16[17,192]{0,1:T(8,128)(2,1)}, u32[]{:S(2)}, u32[]{:S(2)}) collective-permute-start(bf16[17,192]{0,1:T(8,128)(2,1)} %get-tuple-element.1266), channel_id=1, source_target_pairs={{4,0},{8,4},{12,8},{16,12},{20,16},{24,20},{28,24},{5,1},{9,5},{13... | collective-permute-start | bytes 19592 | tf_op jit(solution)/shard_map/ppermute | solution.py:31
  10.8 80.6 %collective-permute-start = (bf16[17,192]{0,1:T(8,128)(2,1)}, bf16[17,192]{0,1:T(8,128)(2,1)}, u32[]{:S(2)}, u32[]{:S(2)}) collective-permute-start(bf16[17,192]{0,1:T(8,128)(2,1)} %get-tuple-element.1265), channel_id=1, source_target_pairs={{0,4},{4,8},{8,12},{12,16},{16,20},{20,24},{24,28},{1,5},{5,9},{9,... | collective-permute-start | bytes 19592 | tf_op jit(solution)/shard_map/ppermute | solution.py:30
  18.2 329.2 %all-reduce.31.cloned.1.call-start = ((), (), s32[]{:S(2)}) async-start(), calls=%async_computation.1 | async-start | bytes 1572864 | tf_op jit(solution)/shard_map/psum | solution.py:218
  30.4 376.8 %copy-start.18 = (f32[256,3,4,1]{0,3,2,1:T(1,128)}, f32[256,3,4,1]{0,3,2,1:T(1,128)S(1)}, u32[]{:S(2)}) copy-start(f32[256,3,4,1]{0,3,2,1:T(1,128)S(1)} %broadcast.727) | copy-start | bytes 36868
  300.5 96.3 %all-reduce.33.cloned.1.call-start = ((), (), s32[]{:S(2)}) async-start(), calls=%async_computation.2 | async-start | bytes 1572864 | tf_op jit(solution)/shard_map/psum | solution.py:228
  302.8 44.6 %copy-start.12 = (bf16[256,768]{1,0:T(8,128)(2,1)S(1)}, bf16[256,768]{1,0:T(8,128)(2,1)}, u32[]{:S(2)}) copy-start(bf16[256,768]{1,0:T(8,128)(2,1)} %param.28) | copy-start | bytes 1179652
  302.8 44.6 %copy-start.262 = (f32[768]{0:T(1024)S(1)}, f32[768]{0:T(1024)}, u32[]{:S(2)}) copy-start(f32[768]{0:T(1024)} %param.36) | copy-start | bytes 9220
  353.6 95.1 %all-reduce.35.cloned.1.call-start = ((), (), s32[]{:S(2)}) async-start(), calls=%async_computation.3 | async-start | bytes 1572864 | tf_op jit(solution)/shard_map/psum | solution.py:249
  372.1 26.4 %copy-start.37 = (f32[256,3,4,32]{0,3,2,1:T(8,128)}, f32[256,3,4,32]{0,3,2,1:T(8,128)S(1)}, u32[]{:S(2)}) copy-start(f32[256,3,4,32]{0,3,2,1:T(8,128)S(1)} %broadcast_multiply_fusion.22) | copy-start | bytes 1179652
  372.3 33.2 %copy-start.22 = (f32[256,3,4,64]{0,3,2,1:T(8,128)}, f32[256,3,4,64]{0,3,2,1:T(8,128)S(1)}, u32[]{:S(2)}) copy-start(f32[256,3,4,64]{0,3,2,1:T(8,128)S(1)} %concatenate.426) | copy-start | bytes 2359300
  373.7 25.0 %copy-start.211 = (f32[768]{0:T(1024)S(1)}, f32[768]{0:T(1024)}, u32[]{:S(2)}) copy-start(f32[768]{0:T(1024)} %param.44) | copy-start | bytes 9220
  373.7 25.0 %copy-start.263 = (f32[768]{0:T(1024)S(1)}, f32[768]{0:T(1024)}, u32[]{:S(2)}) copy-start(f32[768]{0:T(1024)} %param.45) | copy-start | bytes 9220
  405.4 255.0 %all-gather.5.cloned.1.call-start = ((), (), s32[]{:S(2)}) async-start(), calls=%async_computation.4 | async-start | bytes 1327104 | tf_op jit(solution)/shard_map/all_gather | solution.py:350
  455.7 474.9 %all-reduce.37.cloned.1.call-start = ((), (), s32[]{:S(2)}) async-start(), calls=%async_computation.5 | async-start | bytes 786432 | tf_op jit(solution)/shard_map/psum | solution.py:381
  634.7 20.3 %collective-permute-start.3 = (bf16[17,192]{0,1:T(8,128)(2,1)S(1)}, bf16[17,192]{0,1:T(8,128)(2,1)S(1)}, u32[]{:S(2)}, u32[]{:S(2)}) collective-permute-start(bf16[17,192]{0,1:T(8,128)(2,1)S(1)} %get-tuple-element.1230), channel_id=1, source_target_pairs={{4,0},{8,4},{12,8},{16,12},{20,16},{24,20},{28,24},{5,1},{9,5},{13... | collective-permute-start | bytes 19592 | tf_op jit(solution)/shard_map/ppermute | solution.py:31
  636.0 19.0 %collective-permute-start.2 = (bf16[17,192]{0,1:T(8,128)(2,1)S(1)}, bf16[17,192]{0,1:T(8,128)(2,1)S(1)}, u32[]{:S(2)}, u32[]{:S(2)}) collective-permute-start(bf16[17,192]{0,1:T(8,128)(2,1)S(1)} %get-tuple-element.1229), channel_id=1, source_target_pairs={{0,4},{4,8},{8,12},{12,16},{16,20},{20,24},{24,28},{1,5},{5,9},{9,... | collective-permute-start | bytes 19592 | tf_op jit(solution)/shard_map/ppermute | solution.py:30
  877.1 114.0 %all-reduce.39.cloned.1.call-start = ((), (), s32[]{:S(2)}) async-start(), calls=%async_computation.6 | async-start | bytes 7077888 | tf_op jit(solution)/shard_map/psum | solution.py:392
  880.3 18.2 %copy-start.270 = (f32[192]{0:T(256)S(1)}, f32[192]{0:T(256)}, u32[]{:S(2)}) copy-start(f32[192]{0:T(256)} %get-tuple-element.931) | copy-start | bytes 2308
  880.3 18.5 %copy-start.269 = (f32[192]{0:T(256)S(1)}, f32[192]{0:T(256)}, u32[]{:S(2)}) copy-start(f32[192]{0:T(256)} %get-tuple-element.930) | copy-start | bytes 2308
  880.3 18.8 %copy-start.268 = (f32[192]{0:T(256)S(1)}, f32[192]{0:T(256)}, u32[]{:S(2)}) copy-start(f32[192]{0:T(256)} %get-tuple-element.929) | copy-start | bytes 2308
  880.3 19.1 %copy-start.267 = (f32[192]{0:T(256)S(1)}, f32[192]{0:T(256)}, u32[]{:S(2)}) copy-start(f32[192]{0:T(256)} %get-tuple-element.928) | copy-start | bytes 2308
  880.3 19.8 %copy-start.255 = (bf16[768]{0:T(1024)(128)(2,1)S(1)}, bf16[768]{0:T(1024)(128)(2,1)}, u32[]{:S(2)}) copy-start(bf16[768]{0:T(1024)(128)(2,1)} %get-tuple-element.922) | copy-start | bytes 4612
  880.3 19.8 %copy-start.256 = (bf16[768]{0:T(1024)(128)(2,1)S(1)}, bf16[768]{0:T(1024)(128)(2,1)}, u32[]{:S(2)}) copy-start(bf16[768]{0:T(1024)(128)(2,1)} %get-tuple-element.927) | copy-start | bytes 4612
  880.4 19.8 %copy-start.258 = (bf16[768]{0:T(1024)(128)(2,1)S(1)}, bf16[768]{0:T(1024)(128)(2,1)}, u32[]{:S(2)}) copy-start(bf16[768]{0:T(1024)(128)(2,1)} %get-tuple-element.920) | copy-start | bytes 4612
  880.4 19.8 %copy-start.259 = (bf16[768]{0:T(1024)(128)(2,1)S(1)}, bf16[768]{0:T(1024)(128)(2,1)}, u32[]{:S(2)}) copy-start(bf16[768]{0:T(1024)(128)(2,1)} %get-tuple-element.926) | copy-start | bytes 4612
  880.4 19.8 %copy-start.260 = (bf16[768]{0:T(1024)(128)(2,1)S(1)}, bf16[768]{0:T(1024)(128)(2,1)}, u32[]{:S(2)}) copy-start(bf16[768]{0:T(1024)(128)(2,1)} %get-tuple-element.1077) | copy-start | bytes 4612
  880.4 19.8 %copy-start.261 = (bf16[768]{0:T(1024)(128)(2,1)S(1)}, bf16[768]{0:T(1024)(128)(2,1)}, u32[]{:S(2)}) copy-start(bf16[768]{0:T(1024)(128)(2,1)} %get-tuple-element.1079) | copy-start | bytes 4612
  880.4 19.8 %copy-start.265 = (bf16[768]{0:T(1024)(128)(2,1)S(1)}, bf16[768]{0:T(1024)(128)(2,1)}, u32[]{:S(2)}) copy-start(bf16[768]{0:T(1024)(128)(2,1)} %get-tuple-element.1330) | copy-start | bytes 4612
  880.4 50.2 %copy-start.26 = (f32[256,768]{1,0:T(8,128)S(1)}, f32[256,768]{1,0:T(8,128)}, u32[]{:S(2)}) copy-start(f32[256,768]{1,0:T(8,128)} %copy-done.24) | copy-start | bytes 2359300
  (308 other events, 1152.9 us)
Sparse Core Ops, SparseCore 0:
  18.3 26.8 all-gather.2
  300.6 46.6 all-reduce.30
  353.7 43.0 all-reduce.32
  405.6 43.1 all-reduce.34
  455.8 23.2 all-gather.4
  877.2 35.5 all-reduce.36
  917.4 73.5 all-reduce.38
where the time goes:
time: 1020 us; the launch traced here: 1010 us
  local copies, waits for them, and re-layouts  440 us (43%)
  other arithmetic  237 us (23%)
  waiting for transfers between devices  155 us (15%)
  matrix products  111 us (11%)
  blocking collectives  32.9 us (3%)
  between operations  17.8 us (2%)
    concatenate x78, local copies, waits for them, and re-layouts, feature_tree(): jnp.concatenate([features, features * parts[..., bit:bit + 1]], axis=-1)  374 us
    mul x103, other arithmetic, feature_tree(): features * parts[..., bit:bit + 1]  88.3 us
    convert_element_type x14, other arithmetic, expand_codes(): return feature_tree(picked).astype(jnp.bfloat16)  63 us
    psum x1, waiting for transfers between devices, on_device(): lax.psum(weight_grad(query_low).astype(jnp.bfloat16), 'seq')  58.5 us
    psum x1, waiting for transfers between devices, on_device(): lax.psum(jnp.dot(context, mixer_weight, preferred_element_type=jnp.float3...  41.1 us
    psum x1, waiting for transfers between devices, on_device(): lax.psum(jnp.einsum('rf,df->rd', up_low, up_weight, preferred_element_typ...  32.4 us
    psum x1, blocking collectives, on_device(): lax.psum(jnp.sum(query_low.astype(jnp.float32), axis=0).astype(jnp.bfloat...  24 us
    psum x1, waiting for transfers between devices, on_device(): lax.psum(jnp.dot(hidden, down_weight, preferred_element_type=jnp.float32)...  23.1 us
  transfers between devices with their start and end apart: 11, of which 4 were waited for; matrix products, arithmetic and copies ran while one was open for 34% of the time, Pallas kernels for 0%

commit v1 on v0

v1 whole, which is shorter than its diff:
```python
import functools
import math

import jax
import jax.numpy as jnp
from jax import lax
from jax.experimental import pallas as pl
from jax.experimental.pallas import tpu as pltpu
from jax.sharding import PartitionSpec as P

D = 768
H = 12
HS = 64
BITS = 8
PLANES = 32
HASHES = 4
CONV = 35
RADIUS = 17
FEATS = HASHES * 2**BITS
SHARP = 2.0
NORM_EPS = 1e-05
UNIT_EPS = 1e-06
EXACT = lax.Precision.HIGHEST
F32 = jnp.float32
BF16 = jnp.bfloat16
ROWS = 256
HEADS = 3
TAP_LANE = 111
VMEM = pl.BlockSpec(memory_space=pltpu.VMEM)
SMEM = pl.BlockSpec(memory_space=pltpu.SMEM)
LIMIT = 60 * 1024 * 1024


def dot(a, b):
    return lax.dot_general(a, b, (((1,), (0,)), ((), ())), preferred_element_type=F32)


def dot_nt(a, b):
    return lax.dot_general(a, b, (((1,), (1,)), ((), ())), preferred_element_type=F32)


def dot_exact(a, b):
    return lax.dot_general(
        a, b, (((1,), (0,)), ((), ())), precision=EXACT, preferred_element_type=F32
    )


def doc_count(pos, lengths):
    start = jnp.int32(0)
    found = jnp.zeros_like(pos)
    for d in range(lengths.shape[0]):
        found = found + (pos >= start).astype(jnp.int32)
        start = start + lengths[d]
    return found + (pos >= start).astype(jnp.int32)


def blocks_meet(mine, other, lengths):
    a0 = doc_count(mine * ROWS, lengths)
    a1 = doc_count(mine * ROWS + (ROWS - 1), lengths)
    b0 = doc_count(other * ROWS, lengths)
    b1 = doc_count(other * ROWS + (ROWS - 1), lengths)
    return jnp.logical_and(a0 <= b1, b0 <= a1)


def same_doc(row_start, rows, col_start, cols, lengths, reverse=False):
    rid = row_start + lax.broadcasted_iota(jnp.int32, (rows, 1), 0)
    cid = lax.broadcasted_iota(jnp.int32, (1, cols), 1)
    cid = col_start + ((cols - 1) - cid if reverse else cid)
    return doc_count(rid, lengths) == doc_count(cid, lengths)


def hash_base(picks, m, lanes):
    bit = lax.broadcasted_iota(jnp.int32, (8, lanes), 0)
    factors = []
    for b in range(3):
        on = (bit & (1 << b)) != 0
        row = jnp.broadcast_to(picks[m * BITS + b : m * BITS + b + 1, :], (8, lanes))
        factors.append((on, jnp.where(on, row, 1.0)))
    return factors


def hash_feats(picks, m, lanes):
    factors = hash_base(picks, m, lanes)
    scale = 2.0 ** (-0.5 * BITS)
    feats = [(factors[0][1] * scale) * (factors[1][1] * factors[2][1])]
    rows = {}
    for b in range(3, BITS):
        rows[b] = jnp.broadcast_to(picks[m * BITS + b : m * BITS + b + 1, :], (8, lanes))
        feats = feats + [f * rows[b] for f in feats]
    return feats, rows, factors


def expand(picks, phi_ref):
    lanes = picks.shape[1]
    for m in range(HASHES):
        feats = hash_feats(picks, m, lanes)[0]
        for i in range(0, len(feats), 2):
            both = jnp.concatenate([feats[i], feats[i + 1]], axis=0)
            phi_ref[m * 256 + i * 8 : m * 256 + i * 8 + 16, :] = both.astype(BF16)


def expand_back(picks, dphi_ref, lane0, lanes):
    out = []
    scale = 2.0 ** (-0.5 * BITS)
    for m in range(HASHES):
        feats, rows, factors = hash_feats(picks, m, lanes)
        grads = [
            dphi_ref[m * 256 + i * 8 : m * 256 + i * 8 + 8, lane0 : lane0 + lanes]
            for i in range(32)
        ]
        found = {}
        for b in range(BITS - 1, 2, -1):
            half = len(grads) // 2
            total = grads[half] * feats[0]
            for i in range(1, half):
                total = total + grads[half + i] * feats[i]
            found[b] = jnp.sum(total, axis=0, keepdims=True)
            grads = [grads[i] + grads[half + i] * rows[b] for i in range(half)]
        g = grads[0] * scale
        (on0, f0), (on1, f1), (on2, f2) = factors
        found[0] = jnp.sum(jnp.where(on0, g * (f1 * f2), 0.0), axis=0, keepdims=True)
        found[1] = jnp.sum(jnp.where(on1, g * (f0 * f2), 0.0), axis=0, keepdims=True)
        found[2] = jnp.sum(jnp.where(on2, g * (f0 * f1), 0.0), axis=0, keepdims=True)
        out.extend(found[b] for b in range(BITS))
    return jnp.concatenate(out, axis=0)


def heads_on_lanes(rows):
    turned = rows.T
    return jnp.concatenate([turned[h * HS : (h + 1) * HS] for h in range(HEADS)], axis=1)


def heads_on_rows(turned):
    return jnp.concatenate(
        [turned[:, h * ROWS : (h + 1) * ROWS] for h in range(HEADS)], axis=0
    ).T


def project_body(
    tokens, wq, bq, wk, bk, wv, bv, planes, choose, raw_q, raw_k, tan_q, tan_k, pick_q, pack
):
    x = tokens[...]

    def codes(w, b, raw_ref, tan_ref):
        raw = heads_on_lanes(dot(x, w[...]) + b[...])
        raw_ref[...] = raw
        unit = raw * lax.rsqrt(jnp.sum(raw * raw, axis=0, keepdims=True) + UNIT_EPS)
        tan = jnp.tanh(SHARP * dot_exact(planes[...], unit))
        tan_ref[...] = tan
        return dot(choose[...], tan.astype(BF16)).astype(BF16)

    pack[0:PLANES, :] = codes(wk, bk, raw_k, tan_k)
    values = heads_on_lanes(dot(x, wv[...]) + bv[...])
    pack[PLANES : PLANES + HS, :] = values.astype(BF16)
    pick_q[...] = codes(wq, bq, raw_q, tan_q)


def project(tokens, wq, bq, wk, bk, wv, bv, planes, choose):
    wide = HEADS * ROWS
    shapes = (
        jax.ShapeDtypeStruct((HS, wide), F32),
        jax.ShapeDtypeStruct((HS, wide), F32),
        jax.ShapeDtypeStruct((PLANES, wide), F32),
        jax.ShapeDtypeStruct((PLANES, wide), F32),
        jax.ShapeDtypeStruct((PLANES, wide), BF16),
        jax.ShapeDtypeStruct((PLANES + HS, wide), BF16),
    )
    return pl.pallas_call(
        project_body,
        out_shape=shapes,
        in_specs=[VMEM] * 9,
        out_specs=tuple([VMEM] * 6),
        name="project",
        compiler_params=pltpu.CompilerParams(vmem_limit_bytes=LIMIT),
        cost_estimate=pl.CostEstimate(flops=300_000_000, bytes_accessed=3_000_000, transcendentals=0),
    )(tokens, wq, bq, wk, bk, wv, bv, planes, choose)


def local_feats_body(pick_q, pack, feat_q, feat_k, phi):
    for src, dst in ((pick_q, feat_q), (pack, feat_k)):
        for h in range(HEADS):
            picks = src[0:PLANES, h * ROWS : (h + 1) * ROWS].astype(F32)
            expand(picks, phi)
            dst[h] = phi[...].T


def local_feats(pick_q, pack):
    shape = jax.ShapeDtypeStruct((HEADS, ROWS, FEATS), BF16)
    return pl.pallas_call(
        local_feats_body,
        out_shape=(shape, shape),
        in_specs=[VMEM] * 2,
        out_specs=(VMEM, VMEM),
        scratch_shapes=[pltpu.VMEM((FEATS, ROWS), BF16)],
        name="local_feats",
        compiler_params=pltpu.CompilerParams(vmem_limit_bytes=LIMIT),
        cost_estimate=pl.CostEstimate(flops=100_000_000, bytes_accessed=6_000_000, transcendentals=0),
    )(pick_q, pack)


def window(packs, mine, low, high, n):
    def at(h):
        before = jnp.bitwise_xor(mine, jnp.maximum(mine - 1, 0))
        after = jnp.bitwise_xor(mine, jnp.minimum(mine + 1, n - 1))
        lane = h * ROWS
        return jnp.concatenate(
            [
                packs[before, low:high, lane + 128 : lane + 256],
                packs[0, low:high, lane : lane + 256],
                packs[after, low:high, lane : lane + 128],
            ],
            axis=1,
        )

    return at


def band(row):
    return pltpu.roll(jnp.broadcast_to(row, (ROWS, 512)), 0, 1, stride=1, stride_axis=0)


def split_dot(a, b, mul):
    high = a.astype(BF16)
    low = (a - high.astype(F32)).astype(BF16)
    return mul(high, b) + mul(low, b)


def forward_body(n, lengths, place, feat_q, taps, *refs):
    pack_in, (context, weighted, total_out) = refs[:n], refs[n : n + 3]
    packs, phi0, phi1, phi2, acc, tot = refs[n + 3 :]
    phis = (phi0, phi1, phi2)
    mine = place[0]
    for k in range(n):
        packs[k] = pack_in[k][...]
    acc[...] = jnp.zeros_like(acc)
    tot[...] = jnp.zeros_like(tot)

    def block(k, carry):
        other = jnp.bitwise_xor(mine, k)

        @pl.when(blocks_meet(mine, other, lengths))
        def _():
            same = same_doc(mine * ROWS, ROWS, other * ROWS, ROWS, lengths)
            for h in range(HEADS):
                lane = h * ROWS
                expand(packs[k, 0:PLANES, lane : lane + ROWS].astype(F32), phis[h])
                score = dot(feat_q[h], phis[h][...])
                w = jnp.where(same, score * (1.0 / HASHES), 0.0)
                tot[h] += w[:, :128] + w[:, 128:]
                acc[h] += dot_nt(w.astype(BF16), packs[k, PLANES : PLANES + HS, lane : lane + ROWS])

        return carry

    lax.fori_loop(0, n, block, 0)
    near = same_doc(mine * ROWS, ROWS, mine * ROWS - 128, 512, lengths)
    ext = window(packs, mine, PLANES, PLANES + HS, n)
    outs, sums, parts = [], [], []
    for h in range(HEADS):
        total = 1.0 + jnp.sum(tot[h], axis=1, keepdims=True)
        taps_band = jnp.where(near, band(taps[h : h + 1, :]), 0.0)
        conv = split_dot(taps_band, ext(h), dot_nt)
        sums.append(jnp.broadcast_to(total, (ROWS, HS)))
        parts.append(acc[h])
        outs.append(acc[h] / total + conv)
    context[...] = jnp.concatenate(outs, axis=1).astype(BF16)
    weighted[...] = jnp.concatenate(parts, axis=1)
    total_out[...] = jnp.concatenate(sums, axis=1)


def forward(lengths, place, feat_q, taps, packs):
    n = len(packs)
    wide = HEADS * HS
    return pl.pallas_call(
        functools.partial(forward_body, n),
        out_shape=(
            jax.ShapeDtypeStruct((ROWS, wide), BF16),
            jax.ShapeDtypeStruct((ROWS, wide), F32),
            jax.ShapeDtypeStruct((ROWS, wide), F32),
        ),
        in_specs=[SMEM, SMEM] + [VMEM] * (n + 2),
        out_specs=(VMEM, VMEM, VMEM),
        scratch_shapes=[
            pltpu.VMEM((n, PLANES + HS, HEADS * ROWS), BF16),
            pltpu.VMEM((FEATS, ROWS), BF16),
            pltpu.VMEM((FEATS, ROWS), BF16),
            pltpu.VMEM((FEATS, ROWS), BF16),
            pltpu.VMEM((HEADS, ROWS, HS), F32),
            pltpu.VMEM((HEADS, ROWS, 128), F32),
        ],
        name="attend",
        compiler_params=pltpu.CompilerParams(vmem_limit_bytes=LIMIT),
        cost_estimate=pl.CostEstimate(
            flops=n * 400_000_000, bytes_accessed=4_000_000, transcendentals=0
        ),
    )(lengths, place, feat_q, taps, *packs)


def unit_back(code_grad, tan, raw, planes_t):
    scale = lax.rsqrt(jnp.sum(raw * raw, axis=0, keepdims=True) + UNIT_EPS)
    unit_grad = dot_exact(planes_t, code_grad * (SHARP * (1.0 - tan * tan)))
    inner = jnp.sum(raw * unit_grad, axis=0, keepdims=True)
    return unit_grad * scale - raw * (scale * scale * scale) * inner


def codes_to_raw(dphi, picks, tan, raw, choose_back, planes_t):
    parts = []
    for h in range(HEADS):
        for u in range(2):
            lane = h * ROWS + u * 128
            parts.append(
                expand_back(picks[0:PLANES, lane : lane + 128].astype(F32), dphi.at[h], u * 128, 128)
            )
    pick_grad = jnp.concatenate(parts, axis=1) * (1.0 / HASHES)
    code_grad = dot_exact(choose_back[...], pick_grad)
    return unit_back(code_grad, tan[...], raw[...], planes_t[...])


def query_back_body(
    n, lengths, place, grads, row_totals, pick_q, tan, raw, choose_back, planes_t, *refs
):
    pack_in, (grad_out,) = refs[:n], refs[n : n + 1]
    packs, phi0, phi1, phi2, dphi = refs[n + 1 :]
    phis = (phi0, phi1, phi2)
    mine = place[0]
    for k in range(n):
        packs[k] = pack_in[k][...]
    dphi[...] = jnp.zeros_like(dphi)

    def block(k, carry):
        other = jnp.bitwise_xor(mine, k)

        @pl.when(blocks_meet(mine, other, lengths))
        def _():
            same = same_doc(other * ROWS, ROWS, mine * ROWS, ROWS, lengths)
            for h in range(HEADS):
                lane = h * ROWS
                expand(packs[k, 0:PLANES, lane : lane + ROWS].astype(F32), phis[h])
                values = packs[k, PLANES : PLANES + HS, lane : lane + ROWS].T
                dw = dot_nt(values, grads[:, h * HS : (h + 1) * HS]) + row_totals[h : h + 1, :]
                dw = jnp.where(same, dw, 0.0).astype(BF16)
                dphi[h] += dot(phis[h][...], dw)

        return carry

    lax.fori_loop(0, n, block, 0)
    raw_grad = codes_to_raw(dphi, pick_q, tan, raw, choose_back, planes_t)
    grad_out[...] = heads_on_rows(raw_grad).astype(BF16)


def query_back(lengths, place, grads, row_totals, pick_q, tan, raw, choose_back, planes_t, packs):
    n = len(packs)
    return pl.pallas_call(
        functools.partial(query_back_body, n),
        out_shape=(jax.ShapeDtypeStruct((ROWS, HEADS * HS), BF16),),
        in_specs=[SMEM, SMEM] + [VMEM] * (n + 7),
        out_specs=(VMEM,),
        scratch_shapes=[
            pltpu.VMEM((n, PLANES + HS, HEADS * ROWS), BF16),
            pltpu.VMEM((FEATS, ROWS), BF16),
            pltpu.VMEM((FEATS, ROWS), BF16),
            pltpu.VMEM((FEATS, ROWS), BF16),
            pltpu.VMEM((HEADS, FEATS, ROWS), F32),
        ],
        name="query_back",
        compiler_params=pltpu.CompilerParams(vmem_limit_bytes=LIMIT),
        cost_estimate=pl.CostEstimate(
            flops=n * 400_000_000, bytes_accessed=4_000_000, transcendentals=0
        ),
    )(lengths, place, grads, row_totals, pick_q, tan, raw, choose_back, planes_t, *packs)[0]


def key_back_body(
    n, lengths, place, feat_k, pack, tan, raw, taps_back, choose_back, planes_t, *refs
):
    pick_in, grad_in = refs[:n], refs[n : 2 * n]
    key_out, value_out, taps_out = refs[2 * n : 2 * n + 3]
    picks, grads, phi0, phi1, phi2, dphi, acc = refs[2 * n + 3 :]
    phis = (phi0, phi1, phi2)
    mine = place[0]
    for k in range(n):
        picks[k] = pick_in[k][...]
        grads[k] = grad_in[k][...]
    dphi[...] = jnp.zeros_like(dphi)
    acc[...] = jnp.zeros_like(acc)

    def block(k, carry):
        other = jnp.bitwise_xor(mine, k)

        @pl.when(blocks_meet(mine, other, lengths))
        def _():
            same = same_doc(mine * ROWS, ROWS, other * ROWS, ROWS, lengths)
            same_t = same_doc(other * ROWS, ROWS, mine * ROWS, ROWS, lengths)
            for h in range(HEADS):
                lane = h * ROWS
                expand(picks[k, :, lane : lane + ROWS].astype(F32), phis[h])
                score = dot(feat_k[h], phis[h][...])
                w = jnp.where(same, score * (1.0 / HASHES), 0.0).astype(BF16)
                grad = grads[k, :, h * HS : (h + 1) * HS]
                acc[h] += dot(w, grad)
                values_t = pack[PLANES : PLANES + HS, lane : lane + ROWS]
                side = grads[k, :, 3 * HS : 4 * HS].astype(F32)
                row_total = side[:, h : h + 1] + side[:, 2 * HEADS + h : 2 * HEADS + h + 1]
                dw = dot(grad, values_t) + row_total
                dw = jnp.where(same_t, dw, 0.0).astype(BF16)
                dphi[h] += dot(phis[h][...], dw)

        return carry

    lax.fori_loop(0, n, block, 0)
    raw_grad = codes_to_raw(dphi, pack, tan, raw, choose_back, planes_t)
    key_out[...] = heads_on_rows(raw_grad).astype(BF16)

    before = jnp.bitwise_xor(mine, jnp.maximum(mine - 1, 0))
    after = jnp.bitwise_xor(mine, jnp.minimum(mine + 1, n - 1))
    near = same_doc(mine * ROWS, ROWS, mine * ROWS - 128, 512, lengths)
    ext = jnp.concatenate([grads[before, 128:, :], grads[0], grads[after, :128, :]], axis=0)
    side = ext[:, 3 * HS : 4 * HS].astype(F32)
    near_rev = same_doc(mine * ROWS, ROWS, mine * ROWS - 128, 512, lengths, reverse=True)
    turn = lax.broadcasted_iota(jnp.int32, (512, 512), 0) + lax.broadcasted_iota(
        jnp.int32, (512, 512), 1
    )
    flip = (turn == 511).astype(BF16)
    outs, tap_rows = [], []
    for h in range(HEADS):
        total = side[:, HEADS + h : HEADS + h + 1]
        context_grad = (ext[:, h * HS : (h + 1) * HS].astype(F32) * total).astype(BF16)
        taps_band = jnp.where(near, band(taps_back[h : h + 1, :]), 0.0)
        outs.append(acc[h] + split_dot(taps_band, context_grad, dot))
        flipped = dot(flip, context_grad).astype(BF16)
        values = pack[PLANES : PLANES + HS, h * ROWS : (h + 1) * ROWS].T
        cross = jnp.where(near_rev, dot_nt(values, flipped), 0.0)
        cross = pltpu.roll(cross, 0, 1, stride=1, stride_axis=0)
        tap_rows.append(jnp.sum(cross, axis=0, keepdims=True))
    value_out[...] = jnp.concatenate(outs, axis=1).astype(BF16)
    taps_out[...] = jnp.concatenate(tap_rows + [jnp.zeros((5, 512), F32)], axis=0)


def key_back(lengths, place, feat_k, pack, tan, raw, taps_back, choose_back, planes_t, picks, grads):
    n = len(picks)
    shape = jax.ShapeDtypeStruct((ROWS, HEADS * HS), BF16)
    return pl.pallas_call(
        functools.partial(key_back_body, n),
        out_shape=(shape, shape, jax.ShapeDtypeStruct((8, 512), F32)),
        in_specs=[SMEM, SMEM] + [VMEM] * (2 * n + 7),
        out_specs=(VMEM, VMEM, VMEM),
        scratch_shapes=[
            pltpu.VMEM((n, PLANES, HEADS * ROWS), BF16),
            pltpu.VMEM((n, ROWS, 4 * HS), BF16),
            pltpu.VMEM((FEATS, ROWS), BF16),
            pltpu.VMEM((FEATS, ROWS), BF16),
            pltpu.VMEM((FEATS, ROWS), BF16),
            pltpu.VMEM((HEADS, FEATS, ROWS), F32),
            pltpu.VMEM((HEADS, ROWS, HS), F32),
        ],
        name="key_back",
        compiler_params=pltpu.CompilerParams(vmem_limit_bytes=LIMIT),
        cost_estimate=pl.CostEstimate(
            flops=n * 800_000_000, bytes_accessed=6_000_000, transcendentals=0
        ),
    )(lengths, place, feat_k, pack, tan, raw, taps_back, choose_back, planes_t, *picks, *grads)


def to_all(value, axis):
    n = lax.axis_size(axis)
    return [value] + [
        lax.ppermute(value, axis, [(i, i ^ k) for i in range(n)]) for k in range(1, n)
    ]


def norm_forward(rows, gain, shift):
    center = rows - jnp.mean(rows, axis=-1, keepdims=True)
    inverse = lax.rsqrt(jnp.mean(center * center, axis=-1, keepdims=True) + NORM_EPS)
    normed = center * inverse
    return (normed * gain + shift, normed, inverse)


def norm_backward(grad, normed, inverse, gain):
    scaled = grad * gain
    rows_grad = inverse * (
        scaled
        - jnp.mean(scaled, axis=-1, keepdims=True)
        - normed * jnp.mean(scaled * normed, axis=-1, keepdims=True)
    )
    return (rows_grad, jnp.sum(grad * normed, axis=0), jnp.sum(grad, axis=0))


def on_device(
    tokens,
    query_weight,
    query_shift,
    key_weight,
    key_shift,
    value_weight,
    value_shift,
    mixer_weight,
    mixer_shift,
    conv_taps,
    first_gain,
    first_shift,
    up_weight,
    up_shift,
    down_weight,
    down_shift,
    second_gain,
    second_shift,
    hyperplanes,
    plane_choice,
    doc_lengths,
    out_grad,
):
    place = lax.axis_index("seq").reshape(1).astype(jnp.int32)
    hot = plane_choice.reshape(-1, 1) == jnp.arange(PLANES, dtype=jnp.int32)
    choose = hot.astype(BF16)
    choose_back = hot.astype(F32).T
    planes_t = hyperplanes.T
    raw_q, raw_k, tan_q, tan_k, pick_q, pack = project(
        tokens,
        query_weight,
        query_shift.reshape(1, -1),
        key_weight,
        key_shift.reshape(1, -1),
        value_weight,
        value_shift.reshape(1, -1),
        hyperplanes,
        choose,
    )
    packs = to_all(pack, "seq")
    picks = to_all(pick_q, "seq")
    feat_q, feat_k = local_feats(pick_q, pack)
    side = (TAP_LANE, 512 - TAP_LANE - CONV)
    taps = jnp.pad(conv_taps, ((0, 5), side))
    taps_back = jnp.pad(conv_taps[:, ::-1], ((0, 5), side))
    context, weighted, total = forward(doc_lengths, place, feat_q, taps, packs)
    mixed = (
        lax.psum(jnp.dot(context, mixer_weight, preferred_element_type=jnp.float32), "hid")
        + mixer_shift
    )
    first_out, first_normed, first_inverse = norm_forward(
        tokens.astype(jnp.float32) + mixed, first_gain, first_shift
    )
    first_low = first_out.astype(jnp.bfloat16)
    upward = jnp.dot(first_low, up_weight, preferred_element_type=jnp.float32) + up_shift
    hidden = jax.nn.gelu(upward, approximate=False).astype(jnp.bfloat16)
    downward = (
        lax.psum(jnp.dot(hidden, down_weight, preferred_element_type=jnp.float32), "hid")
        + down_shift
    )
    second_out, second_normed, second_inverse = norm_forward(
        first_out + downward, second_gain, second_shift
    )
    layer_out = second_out.astype(jnp.bfloat16)
    second_grad, second_gains, second_shifts = norm_backward(
        out_grad, second_normed, second_inverse, second_gain
    )
    down_low = second_grad.astype(jnp.bfloat16)
    down_grad = jnp.einsum("rf,rd->fd", hidden, down_low, preferred_element_type=jnp.float32)
    down_offsets = jnp.sum(down_low.astype(jnp.float32), axis=0)
    hidden_grad = jnp.einsum("rd,fd->rf", down_low, down_weight, preferred_element_type=jnp.float32)
    unused, gelu_pull = jax.vjp(
        lambda inner_value: jax.nn.gelu(inner_value, approximate=False), upward
    )
    up_low = gelu_pull(hidden_grad)[0].astype(jnp.bfloat16)
    up_grad = jnp.einsum("rd,rf->df", first_low, up_low, preferred_element_type=jnp.float32)
    up_offsets = jnp.sum(up_low.astype(jnp.float32), axis=0)
    first_back = (
        lax.psum(
            jnp.einsum("rf,df->rd", up_low, up_weight, preferred_element_type=jnp.float32), "hid"
        )
        + second_grad
    )
    first_grad, first_gains, first_shifts = norm_backward(
        first_back, first_normed, first_inverse, first_gain
    )
    mixed_low = first_grad.astype(jnp.bfloat16)
    mixer_grad = jnp.einsum("rc,rd->cd", context, mixed_low, preferred_element_type=jnp.float32)
    mixer_offsets = jnp.sum(mixed_low.astype(jnp.float32), axis=0)
    context_grad = jnp.einsum(
        "rd,cd->rc", mixed_low, mixer_weight, preferred_element_type=jnp.float32
    )
    weighted_grad = (context_grad / total).astype(BF16)
    total3 = total.reshape(ROWS, HEADS, HS)[:, :, 0]
    total_grad = -jnp.sum((context_grad * weighted).reshape(ROWS, HEADS, HS), axis=-1) / (
        total3 * total3
    )
    grad_high = total_grad.astype(BF16)
    grad_low = (total_grad - grad_high.astype(F32)).astype(BF16)
    grad_pack = jnp.concatenate(
        [weighted_grad, grad_high, total3.astype(BF16), grad_low, jnp.zeros((ROWS, 55), BF16)], axis=1
    )
    grad_packs = to_all(grad_pack, "seq")
    query_low = query_back(
        doc_lengths,
        place,
        weighted_grad,
        jnp.pad(total_grad.T, ((0, 5), (0, 0))),
        pick_q,
        tan_q,
        raw_q,
        choose_back,
        planes_t,
        packs,
    )
    key_low, value_grad_low, tap_rows = key_back(
        doc_lengths, place, feat_k, pack, tan_k, raw_k, taps_back, choose_back, planes_t, picks, grad_packs
    )
    taps_grad = tap_rows[:HEADS, 366 : 366 + CONV]

    def weight_grad(grad_low):
        return jnp.einsum("rd,rc->dc", tokens, grad_low, preferred_element_type=jnp.float32)

    def back_input(grad_low, weight):
        return jnp.einsum("rc,dc->rd", grad_low, weight, preferred_element_type=jnp.float32)

    tokens_grad = (
        lax.psum(
            (
                back_input(query_low, query_weight)
                + back_input(key_low, key_weight)
                + back_input(value_grad_low, value_weight)
            ).astype(jnp.bfloat16),
            "hid",
        ).astype(jnp.float32)
        + first_grad
    )
    summed = (
        lax.psum(weight_grad(query_low).astype(jnp.bfloat16), "seq").astype(jnp.float32),
        lax.psum(jnp.sum(query_low.astype(jnp.float32), axis=0).astype(jnp.bfloat16), "seq").astype(
            jnp.float32
        ),
        lax.psum(weight_grad(key_low).astype(jnp.bfloat16), "seq").astype(jnp.float32),
        lax.psum(jnp.sum(key_low.astype(jnp.float32), axis=0).astype(jnp.bfloat16), "seq").astype(
            jnp.float32
        ),
        lax.psum(weight_grad(value_grad_low).astype(jnp.bfloat16), "seq").astype(jnp.float32),
        lax.psum(
            jnp.sum(value_grad_low.astype(jnp.float32), axis=0).astype(jnp.bfloat16), "seq"
        ).astype(jnp.float32),
        lax.psum(mixer_grad.astype(jnp.bfloat16), "seq").astype(jnp.float32),
        lax.psum(mixer_offsets.astype(jnp.bfloat16), "seq").astype(jnp.float32),
        lax.psum(taps_grad.astype(jnp.bfloat16), "seq").astype(jnp.float32),
        lax.psum(first_gains.astype(jnp.bfloat16), "seq").astype(jnp.float32),
        lax.psum(first_shifts.astype(jnp.bfloat16), "seq").astype(jnp.float32),
        lax.psum(up_grad.astype(jnp.bfloat16), "seq").astype(jnp.float32),
        lax.psum(up_offsets.astype(jnp.bfloat16), "seq").astype(jnp.float32),
        lax.psum(down_grad.astype(jnp.bfloat16), "seq").astype(jnp.float32),
        lax.psum(down_offsets.astype(jnp.bfloat16), "seq").astype(jnp.float32),
        lax.psum(second_gains.astype(jnp.bfloat16), "seq").astype(jnp.float32),
        lax.psum(second_shifts.astype(jnp.bfloat16), "seq").astype(jnp.float32),
    )
    return (
        layer_out,
        tokens_grad,
        summed[0],
        summed[1],
        summed[2],
        summed[3],
        summed[4],
        summed[5],
        summed[6],
        summed[7],
        summed[8],
        summed[9],
        summed[10],
        summed[11],
        summed[12],
        summed[13],
        summed[14],
        summed[15],
        summed[16],
    )


def solution(mesh):
    placed = (
        P("seq", None),
        P(None, "hid"),
        P("hid"),
        P(None, "hid"),
        P("hid"),
        P(None, "hid"),
        P("hid"),
        P("hid", None),
        P(),
        P("hid", None),
        P(),
        P(),
        P(None, "hid"),
        P("hid"),
        P("hid", None),
        P(),
        P(),
        P(),
        P(),
        P(),
        P(),
        P("seq", None),
    )
    return jax.shard_map(
        on_device,
        mesh=mesh,
        in_specs=placed,
        out_specs=(
            P("seq", None),
            P("seq", None),
            P(None, "hid"),
            P("hid"),
            P(None, "hid"),
            P("hid"),
            P(None, "hid"),
            P("hid"),
            P("hid", None),
            P(),
            P("hid", None),
            P(),
            P(),
            P(None, "hid"),
            P("hid"),
            P("hid", None),
            P(),
            P(),
            P(),
        ),
        check_vma=False,
    )
```

time: 1020 us -> 388 us (0.38); the launches traced: 1010 us -> 387 us
  local copies, waits for them, and re-layouts: 440 us -> 13.5 us
  other arithmetic: 237 us -> 28 us
  matrix products: 111 us -> 18.6 us
  waiting for transfers between devices: 155 us -> 220 us
  Pallas kernels: 0 us -> 32.5 us
  starting transfers between devices: 9.79 us -> 27.2 us
    concatenate x78 -> x1, local copies, waits for them, and re-layouts: 374 us -> 0.17 us  [on_device(): jnp.concatenate([weighted_grad, grad_high, total3.astype(BF16), grad_low,...]
    mul x109 -> x1, other arithmetic: 95 us -> 0.71 us  [on_device(): context_grad * weighted]
    dot_general x45 -> x0, matrix products: 91.8 us -> none  [the longest x4 22.9 us: compute(): jnp.einsum('ain,iam->nam', mixing_reduced, block_feature_rows, preferred_...]
    convert_element_type x25 -> x2, other arithmetic: 81.8 us -> 2.21 us  [the longest x1 1.54 us: on_device(): total3.astype(BF16)]
    pallas_call x0 -> x5, Pallas kernels: none -> 32.5 us  [the longest x1 12.1 us: key_back(): pl.pallas_call(functools.partial(key_back_body, n), out_shape=(shape, sha...]
    psum x1, waiting for transfers between devices: 58.5 us -> 76.8 us  [on_device(): lax.psum(weight_grad(query_low).astype(jnp.bfloat16), 'seq')]
    reduce_sum x70 -> x3, other arithmetic: 18.4 us -> 0.14 us  [the longest x1 0.06 us: on_device(): jnp.sum(query_low.astype(jnp.float32), axis=0).astype(jnp.bfloat16)]
    ppermute x4 -> x21, starting transfers between devices: 9.25 us -> 26.8 us  [to_all(): lax.ppermute(value, axis, [(i, i ^ k) for i in range(n)])]
  transfers between devices with their start and end apart: 11 -> 26, of which waited for: 4 -> 10; matrix products, arithmetic and copies ran while one was open for 34% -> 8% of each run, Pallas kernels for 0% -> 3%
where the time goes in v1:
time: 388 us; the launch traced here: 387 us
  waiting for transfers between devices  220 us (57%)
  Pallas kernels  32.5 us (8%)
  blocking collectives  32.5 us (8%)
  other arithmetic  28 us (7%)
  starting transfers between devices  27.2 us (7%)
  matrix products  18.6 us (5%)
  between operations  14.4 us (4%)
  local copies, waits for them, and re-layouts  13.5 us (3%)
    psum x1, waiting for transfers between devices, on_device(): lax.psum(weight_grad(query_low).astype(jnp.bfloat16), 'seq')  76.8 us
    psum x1, waiting for transfers between devices, on_device(): lax.psum(jnp.dot(context, mixer_weight, preferred_element_type=jnp.float3...  50.2 us
    psum x1, waiting for transfers between devices, on_device(): lax.psum(jnp.einsum('rf,df->rd', up_low, up_weight, preferred_element_typ...  38.3 us
    psum x1, waiting for transfers between devices, on_device(): lax.psum(jnp.dot(hidden, down_weight, preferred_element_type=jnp.float32)...  37.2 us
    psum x1, blocking collectives, on_device(): lax.psum(jnp.sum(query_low.astype(jnp.float32), axis=0).astype(jnp.bfloat...  32.5 us
    ppermute x21, starting transfers between devices, to_all(): lax.ppermute(value, axis, [(i, i ^ k) for i in range(n)])  26.8 us
    ppermute x21, waiting for transfers between devices, to_all(): lax.ppermute(value, axis, [(i, i ^ k) for i in range(n)])  13 us
    pallas_call x1, Pallas kernels, key_back(): pl.pallas_call(functools.partial(key_back_body, n), out_shape=(shape, sha...  12.1 us
  transfers between devices with their start and end apart: 26, of which 10 were waited for; matrix products, arithmetic and copies ran while one was open for 8% of the time, Pallas kernels for 3%

profile of v1, /device:TPU:0, one launch (start us, length us, event | category | flops | bytes accessed | tf_op | source)
XLA Modules:
  0.0 387.1 jit_solution(9829071882653011122)
XLA Ops:
  7.3 2.0 copy.69.wq
  9.3 1.9 copy.70.wk
  12.8 3.3 project.1
  16.6 2.5 collective-permute-start.1
  19.2 1.8 collective-permute-start.3
  21.0 2.6 collective-permute-start.5
  24.1 1.6 collective-permute-start.6
  26.4 3.1 local_feats.1
  29.5 4.9 %collective-permute-done.4.refs_5_ = bf16[96,768]{1,0:T(8,128)(2,1)S(1)} collective-permute-done((bf16[96,768]{1,0:T(8,128)(2,1)}, bf16[96,768]{1,0:T(8,128)(2,1)S(1)}, u32[]{:S(2)}, u32[]{:S(2)}) %collective-permute-start.4) | collective-permute-done | bytes 147488 | tf_op jit(solution)/shard_map/ppermute | solution.py:466
  35.1 7.1 %attend.1 = (bf16[256,192]{1,0:T(8,128)(2,1)}, f32[256,192]{1,0:T(8,128)}, f32[256,192]{1,0:T(8,128)}) custom-call(s32[2]{0:T(128)} %lengths.5, s32[1]{0:T(128)} %bitcast.place, bf16[3,256,1024]{2,1,0:T(8,128)(2,1)} %get-tuple-element.35.feat_q, f32[8,512]{1,0:T(8,128)} %pad.11.taps, bf16[96,768]{1,0:T(8,128)(2,1)} %get-tuple-element.34.pack.refs_0_, ...), custom_call_target="tpu_custom_call" | custom-call | flops 3200000000 | bytes 4000000 | tf_op jit(solution)/shard_map/attend/pallas_call | solution.py:273
  42.2 2.1 fusion.31
  44.5 50.2 %all-reduce.11.cloned.1.call-done = f32[256,768]{1,0:T(8,128)} async-done(((f32[256,768]{1,0:T(8,128)}), f32[256,768]{1,0:T(8,128)}) %all-reduce.11.cloned.1.call-update) | async-done | bytes 786448 | tf_op jit(solution)/shard_map/psum | solution.py:535
  96.3 3.2 multiply_convert_fusion
  107.0 37.2 %all-reduce.13.cloned.1.call-done = f32[256,768]{1,0:T(8,128)} async-done(((f32[256,768]{1,0:T(8,128)}), f32[256,768]{1,0:T(8,128)}) %all-reduce.13.cloned.1.call-update) | async-done | bytes 786448 | tf_op jit(solution)/shard_map/psum | solution.py:545
  146.0 1.8 multiply_reduce_fusion
  155.4 1.7 convolution_convert_fusion.1
  157.1 38.3 %all-reduce.15.cloned.1.call-done = f32[256,768]{1,0:T(8,128)} async-done(((f32[256,768]{1,0:T(8,128)}), f32[256,768]{1,0:T(8,128)}) %all-reduce.15.cloned.1.call-update) | async-done | bytes 786448 | tf_op jit(solution)/shard_map/psum | solution.py:566
  195.3 1.6 multiply_reduce_fusion.1
  200.0 7.0 %query_back.1 = bf16[256,192]{1,0:T(8,128)(2,1)} custom-call(s32[2]{0:T(128)} %lengths.5, s32[1]{0:T(128)} %bitcast.place, bf16[256,192]{1,0:T(8,128)(2,1)} %get-tuple-element.88.grads, f32[8,256]{1,0:T(8,128)} %pad.12.clone.row_totals, bf16[32,768]{1,0:T(8,128)(2,1)} %get-tuple-element.33.pick_q.refs_0_, f32[32,768]{1,0:T(8,128)} %get-tuple-element.39.tan, ...), custom_call_target="tpu_custom_call" | custom-call | flops 3200000000 | bytes 4000000 | tf_op jit(solution)/shard_map/query_back/pallas_call | solution.py:352
  207.2 5.4 %collective-permute-start.12 = (bf16[32,768]{1,0:T(8,128)(2,1)}, bf16[32,768]{1,0:T(8,128)(2,1)S(1)}, u32[]{:S(2)}, u32[]{:S(2)}) collective-permute-start(bf16[32,768]{1,0:T(8,128)(2,1)} %get-tuple-element.33.pick_q.refs_0_), channel_id=1, source_target_pairs={{0,24},{4,28},{8,16},{12,20},{16,8},{20,12},{24,0},{28,4},{1,25},{... | collective-permute-start | bytes 147464 | tf_op jit(solution)/shard_map/ppermute | solution.py:466
  212.9 3.9 %collective-permute-start.15 = (bf16[256,256]{1,0:T(8,128)(2,1)S(1)}, bf16[256,256]{1,0:T(8,128)(2,1)S(1)}, u32[]{:S(2)}, u32[]{:S(2)}) collective-permute-start(bf16[256,256]{1,0:T(8,128)(2,1)S(1)} %concatenate.3.refs_8_), channel_id=1, source_target_pairs={{0,8},{4,12},{8,0},{12,4},{16,24},{20,28},{24,16},{28,20},{1,9},{5... | collective-permute-start | bytes 393224 | tf_op jit(solution)/shard_map/ppermute | solution.py:466
  219.3 2.1 collective-permute-start.19
  224.1 5.8 %collective-permute-done.17.refs_12_ = bf16[256,256]{1,0:T(8,128)(2,1)S(1)} collective-permute-done((bf16[256,256]{1,0:T(8,128)(2,1)S(1)}, bf16[256,256]{1,0:T(8,128)(2,1)S(1)}, u32[]{:S(2)}, u32[]{:S(2)}) %collective-permute-start.17) | collective-permute-done | bytes 131104 | tf_op jit(solution)/shard_map/ppermute | solution.py:466
  231.6 12.1 %key_back.1 = (bf16[256,192]{1,0:T(8,128)(2,1)}, bf16[256,192]{1,0:T(8,128)(2,1)}, f32[8,512]{1,0:T(8,128)}) custom-call(s32[2]{0:T(128)} %lengths.5, s32[1]{0:T(128)} %bitcast.place, bf16[3,256,1024]{2,1,0:T(8,128)(2,1)} %get-tuple-element.41.feat_k, bf16[96,768]{1,0:T(8,128)(2,1)} %get-tuple-element.34.pack.refs_0_, f32[32,768]{1,0:T(8,128)} %get-tuple-element.42.tan, ...), custom_call_target="tpu_custom_call" | custom-call | flops 6400000000 | bytes 6000000 | tf_op jit(solution)/shard_map/key_back/pallas_call | solution.py:441
  249.2 32.5 %all-reduce.3 = (bf16[192]{0:T(256)(128)(2,1)S(1)}, bf16[192]{0:T(256)(128)(2,1)S(1)}, bf16[192]{0:T(256)(128)(2,1)S(1)}, bf16[768]{0:T(1024)(128)(2,1)S(1)}, bf...) all-reduce(bf16[192]{0:T(256)(128)(2,1)S(1)} %reduce_sum.198, ...), channel_id=1, replica_groups=mesh['seq'=8,'hid'=4] {'seq'}, use_global_device_ids=true, to_apply=%region_15.16 | all-reduce | flops 6057 | bytes 24228 | tf_op jit(solution)/shard_map/psum | solution.py:627
  288.2 4.9 %all-reduce.17.cloned.1.call-done = bf16[256,768]{1,0:T(8,128)(2,1)} async-done(((bf16[256,768]{1,0:T(8,128)(2,1)}), bf16[256,768]{1,0:T(8,128)(2,1)}) %all-reduce.17.cloned.1.call-update) | async-done | bytes 393232 | tf_op jit(solution)/shard_map/psum | solution.py:615
  293.1 1.9 convert_add_fusion
  295.0 76.8 %all-reduce.19.cloned.1.call-done = (bf16[768,192]{0,1:T(8,128)(2,1)}, bf16[768,192]{0,1:T(8,128)(2,1)}, bf16[768,192]{0,1:T(8,128)(2,1)}, bf16[192,768]{1,0:T(8...) async-done(((bf16[768,192]{0,1:T(8,128)(2,1)}, bf16[768,192]{0,1:T(8,128)(2,1)}, bf16[768,192]{0,1:T(8,128)(2,1)}, bf16[192,768]{1,0:T(8,128)(2,1)}, ...) | async-done | bytes 3538960 | tf_op jit(solution)/shard_map/psum | solution.py:626
  371.9 1.9 convert_element_type.179
  373.7 1.9 convert_element_type.183
  377.4 1.6 convert_element_type.198
  379.0 1.6 convert_element_type.201
  (226 shorter events, 46.5 us)
Async XLA Ops:
  7.2 89.1 %copy-start = (bf16[768,768]{1,0:T(8,128)(2,1)S(1)}, bf16[768,768]{1,0:T(8,128)(2,1)}, u32[]{:S(2)}) copy-start(bf16[768,768]{1,0:T(8,128)(2,1)} %param.34) | copy-start | bytes 3538948
  7.2 87.5 %all-reduce.11.cloned.1.call-start = ((), (), s32[]{:S(2)}) async-start(), calls=%async_computation | async-start | bytes 1572864 | tf_op jit(solution)/shard_map/psum | solution.py:535
  16.1 4.9 %collective-permute-start = (bf16[96,768]{1,0:T(8,128)(2,1)}, bf16[96,768]{1,0:T(8,128)(2,1)S(1)}, u32[]{:S(2)}, u32[]{:S(2)}) collective-permute-start(bf16[96,768]{1,0:T(8,128)(2,1)} %get-tuple-element.34.pack.refs_0_), channel_id=1, source_target_pairs={{0,4},{4,0},{8,12},{12,8},{16,20},{20,16},{24,28},{28,24},{1,5},{5... | collective-permute-start | bytes 442376 | tf_op jit(solution)/shard_map/ppermute | solution.py:466
  16.6 7.5 %collective-permute-start.1 = (bf16[96,768]{1,0:T(8,128)(2,1)}, bf16[96,768]{1,0:T(8,128)(2,1)S(1)}, u32[]{:S(2)}, u32[]{:S(2)}) collective-permute-start(bf16[96,768]{1,0:T(8,128)(2,1)} %get-tuple-element.34.pack.refs_0_), channel_id=1, source_target_pairs={{0,8},{4,12},{8,0},{12,4},{16,24},{20,28},{24,16},{28,20},{1,9},{5... | collective-permute-start | bytes 442376 | tf_op jit(solution)/shard_map/ppermute | solution.py:466
  19.1 10.3 %collective-permute-start.2 = (bf16[96,768]{1,0:T(8,128)(2,1)}, bf16[96,768]{1,0:T(8,128)(2,1)S(1)}, u32[]{:S(2)}, u32[]{:S(2)}) collective-permute-start(bf16[96,768]{1,0:T(8,128)(2,1)} %get-tuple-element.34.pack.refs_0_), channel_id=1, source_target_pairs={{0,12},{4,8},{8,4},{12,0},{16,28},{20,24},{24,20},{28,16},{1,13},{... | collective-permute-start | bytes 442376 | tf_op jit(solution)/shard_map/ppermute | solution.py:466
  19.2 10.3 %collective-permute-start.3 = (bf16[96,768]{1,0:T(8,128)(2,1)}, bf16[96,768]{1,0:T(8,128)(2,1)S(1)}, u32[]{:S(2)}, u32[]{:S(2)}) collective-permute-start(bf16[96,768]{1,0:T(8,128)(2,1)} %get-tuple-element.34.pack.refs_0_), channel_id=1, source_target_pairs={{0,16},{4,20},{8,24},{12,28},{16,0},{20,4},{24,8},{28,12},{1,17},{... | collective-permute-start | bytes 442376 | tf_op jit(solution)/shard_map/ppermute | solution.py:466
  21.0 13.4 %collective-permute-start.4 = (bf16[96,768]{1,0:T(8,128)(2,1)}, bf16[96,768]{1,0:T(8,128)(2,1)S(1)}, u32[]{:S(2)}, u32[]{:S(2)}) collective-permute-start(bf16[96,768]{1,0:T(8,128)(2,1)} %get-tuple-element.34.pack.refs_0_), channel_id=1, source_target_pairs={{0,20},{4,16},{8,28},{12,24},{16,4},{20,0},{24,12},{28,8},{1,21},{... | collective-permute-start | bytes 442376 | tf_op jit(solution)/shard_map/ppermute | solution.py:466
  21.0 13.4 %collective-permute-start.5 = (bf16[96,768]{1,0:T(8,128)(2,1)}, bf16[96,768]{1,0:T(8,128)(2,1)S(1)}, u32[]{:S(2)}, u32[]{:S(2)}) collective-permute-start(bf16[96,768]{1,0:T(8,128)(2,1)} %get-tuple-element.34.pack.refs_0_), channel_id=1, source_target_pairs={{0,24},{4,28},{8,16},{12,20},{16,8},{20,12},{24,0},{28,4},{1,25},{... | collective-permute-start | bytes 442376 | tf_op jit(solution)/shard_map/ppermute | solution.py:466
  24.1 10.3 %collective-permute-start.6 = (bf16[96,768]{1,0:T(8,128)(2,1)}, bf16[96,768]{1,0:T(8,128)(2,1)S(1)}, u32[]{:S(2)}, u32[]{:S(2)}) collective-permute-start(bf16[96,768]{1,0:T(8,128)(2,1)} %get-tuple-element.34.pack.refs_0_), channel_id=1, source_target_pairs={{0,28},{4,24},{8,20},{12,16},{16,12},{20,8},{24,4},{28,0},{1,29},{... | collective-permute-start | bytes 442376 | tf_op jit(solution)/shard_map/ppermute | solution.py:466
  42.2 52.5 %copy-start.1 = (bf16[256,768]{1,0:T(8,128)(2,1)S(1)}, bf16[256,768]{1,0:T(8,128)(2,1)}, u32[]{:S(2)}) copy-start(bf16[256,768]{1,0:T(8,128)(2,1)} %tokens.1) | copy-start | bytes 1179652
  42.2 52.5 %copy-start.38 = (f32[768]{0:T(1024)S(1)}, f32[768]{0:T(1024)}, u32[]{:S(2)}) copy-start(f32[768]{0:T(1024)} %param.30) | copy-start | bytes 9220
  44.4 51.9 %copy-start.29 = (f32[768]{0:T(1024)S(1)}, f32[768]{0:T(1024)}, u32[]{:S(2)}) copy-start(f32[768]{0:T(1024)} %param.32) | copy-start | bytes 9220
  44.4 51.9 %copy-start.32 = (f32[768]{0:T(1024)S(1)}, f32[768]{0:T(1024)}, u32[]{:S(2)}) copy-start(f32[768]{0:T(1024)} %param.33) | copy-start | bytes 9220
  44.4 51.9 %copy-start.57 = (f32[768]{0:T(1024)S(1)}, f32[768]{0:T(1024)}, u32[]{:S(2)}) copy-start(f32[768]{0:T(1024)} %param.35) | copy-start | bytes 9220
  44.4 99.8 %all-reduce.13.cloned.1.call-start = ((), (), s32[]{:S(2)}) async-start(), calls=%async_computation.1 | async-start | bytes 1572864 | tf_op jit(solution)/shard_map/psum | solution.py:545
  100.9 94.4 %all-reduce.15.cloned.1.call-start = ((), (), s32[]{:S(2)}) async-start(), calls=%async_computation.2 | async-start | bytes 1572864 | tf_op jit(solution)/shard_map/psum | solution.py:566
  100.9 106.3 %collective-permute-start.7 = (bf16[32,768]{1,0:T(8,128)(2,1)}, bf16[32,768]{1,0:T(8,128)(2,1)}, u32[]{:S(2)}, u32[]{:S(2)}) collective-permute-start(bf16[32,768]{1,0:T(8,128)(2,1)} %get-tuple-element.33.pick_q.refs_0_), channel_id=1, source_target_pairs={{0,4},{4,0},{8,12},{12,8},{16,20},{20,16},{24,28},{28,24},{1,5},{5... | collective-permute-start | bytes 147464 | tf_op jit(solution)/shard_map/ppermute | solution.py:466
  101.0 111.7 %collective-permute-start.8 = (bf16[32,768]{1,0:T(8,128)(2,1)}, bf16[32,768]{1,0:T(8,128)(2,1)}, u32[]{:S(2)}, u32[]{:S(2)}) collective-permute-start(bf16[32,768]{1,0:T(8,128)(2,1)} %get-tuple-element.33.pick_q.refs_0_), channel_id=1, source_target_pairs={{0,8},{4,12},{8,0},{12,4},{16,24},{20,28},{24,16},{28,20},{1,9},{5... | collective-permute-start | bytes 147464 | tf_op jit(solution)/shard_map/ppermute | solution.py:466
  102.5 110.1 %collective-permute-start.9 = (bf16[32,768]{1,0:T(8,128)(2,1)}, bf16[32,768]{1,0:T(8,128)(2,1)}, u32[]{:S(2)}, u32[]{:S(2)}) collective-permute-start(bf16[32,768]{1,0:T(8,128)(2,1)} %get-tuple-element.33.pick_q.refs_0_), channel_id=1, source_target_pairs={{0,12},{4,8},{8,4},{12,0},{16,28},{20,24},{24,20},{28,16},{1,13},{... | collective-permute-start | bytes 147464 | tf_op jit(solution)/shard_map/ppermute | solution.py:466
  102.9 110.0 %collective-permute-start.10 = (bf16[32,768]{1,0:T(8,128)(2,1)}, bf16[32,768]{1,0:T(8,128)(2,1)}, u32[]{:S(2)}, u32[]{:S(2)}) collective-permute-start(bf16[32,768]{1,0:T(8,128)(2,1)} %get-tuple-element.33.pick_q.refs_0_), channel_id=1, source_target_pairs={{0,16},{4,20},{8,24},{12,28},{16,0},{20,4},{24,8},{28,12},{1,17},{... | collective-permute-start | bytes 147464 | tf_op jit(solution)/shard_map/ppermute | solution.py:466
  104.3 113.5 %collective-permute-start.11 = (bf16[32,768]{1,0:T(8,128)(2,1)}, bf16[32,768]{1,0:T(8,128)(2,1)}, u32[]{:S(2)}, u32[]{:S(2)}) collective-permute-start(bf16[32,768]{1,0:T(8,128)(2,1)} %get-tuple-element.33.pick_q.refs_0_), channel_id=1, source_target_pairs={{0,20},{4,16},{8,28},{12,24},{16,4},{20,0},{24,12},{28,8},{1,21},{... | collective-permute-start | bytes 147464 | tf_op jit(solution)/shard_map/ppermute | solution.py:466
  152.1 141.0 %all-reduce.17.cloned.1.call-start = ((), (), s32[]{:S(2)}) async-start(), calls=%async_computation.3 | async-start | bytes 786432 | tf_op jit(solution)/shard_map/psum | solution.py:615
  207.2 10.6 %collective-permute-start.12 = (bf16[32,768]{1,0:T(8,128)(2,1)}, bf16[32,768]{1,0:T(8,128)(2,1)S(1)}, u32[]{:S(2)}, u32[]{:S(2)}) collective-permute-start(bf16[32,768]{1,0:T(8,128)(2,1)} %get-tuple-element.33.pick_q.refs_0_), channel_id=1, source_target_pairs={{0,24},{4,28},{8,16},{12,20},{16,8},{20,12},{24,0},{28,4},{1,25},{... | collective-permute-start | bytes 147464 | tf_op jit(solution)/shard_map/ppermute | solution.py:466
  212.7 5.5 %collective-permute-start.13 = (bf16[32,768]{1,0:T(8,128)(2,1)}, bf16[32,768]{1,0:T(8,128)(2,1)S(1)}, u32[]{:S(2)}, u32[]{:S(2)}) collective-permute-start(bf16[32,768]{1,0:T(8,128)(2,1)} %get-tuple-element.33.pick_q.refs_0_), channel_id=1, source_target_pairs={{0,28},{4,24},{8,20},{12,16},{16,12},{20,8},{24,4},{28,0},{1,29},{... | collective-permute-start | bytes 147464 | tf_op jit(solution)/shard_map/ppermute | solution.py:466
  212.7 6.6 %collective-permute-start.14 = (bf16[256,256]{1,0:T(8,128)(2,1)S(1)}, bf16[256,256]{1,0:T(8,128)(2,1)S(1)}, u32[]{:S(2)}, u32[]{:S(2)}) collective-permute-start(bf16[256,256]{1,0:T(8,128)(2,1)S(1)} %concatenate.3.refs_8_), channel_id=1, source_target_pairs={{0,4},{4,0},{8,12},{12,8},{16,20},{20,16},{24,28},{28,24},{1,5},{5... | collective-permute-start | bytes 393224 | tf_op jit(solution)/shard_map/ppermute | solution.py:466
  212.9 8.6 %collective-permute-start.15 = (bf16[256,256]{1,0:T(8,128)(2,1)S(1)}, bf16[256,256]{1,0:T(8,128)(2,1)S(1)}, u32[]{:S(2)}, u32[]{:S(2)}) collective-permute-start(bf16[256,256]{1,0:T(8,128)(2,1)S(1)} %concatenate.3.refs_8_), channel_id=1, source_target_pairs={{0,8},{4,12},{8,0},{12,4},{16,24},{20,28},{24,16},{28,20},{1,9},{5... | collective-permute-start | bytes 393224 | tf_op jit(solution)/shard_map/ppermute | solution.py:466
  217.8 6.2 %collective-permute-start.16 = (bf16[256,256]{1,0:T(8,128)(2,1)S(1)}, bf16[256,256]{1,0:T(8,128)(2,1)S(1)}, u32[]{:S(2)}, u32[]{:S(2)}) collective-permute-start(bf16[256,256]{1,0:T(8,128)(2,1)S(1)} %concatenate.3.refs_8_), channel_id=1, source_target_pairs={{0,12},{4,8},{8,4},{12,0},{16,28},{20,24},{24,20},{28,16},{1,13},{... | collective-permute-start | bytes 393224 | tf_op jit(solution)/shard_map/ppermute | solution.py:466
  217.8 12.1 %collective-permute-start.17 = (bf16[256,256]{1,0:T(8,128)(2,1)S(1)}, bf16[256,256]{1,0:T(8,128)(2,1)S(1)}, u32[]{:S(2)}, u32[]{:S(2)}) collective-permute-start(bf16[256,256]{1,0:T(8,128)(2,1)S(1)} %concatenate.3.refs_8_), channel_id=1, source_target_pairs={{0,16},{4,20},{8,24},{12,28},{16,0},{20,4},{24,8},{28,12},{1,17},{... | collective-permute-start | bytes 393224 | tf_op jit(solution)/shard_map/ppermute | solution.py:466
  218.2 12.7 %collective-permute-start.18 = (bf16[256,256]{1,0:T(8,128)(2,1)S(1)}, bf16[256,256]{1,0:T(8,128)(2,1)S(1)}, u32[]{:S(2)}, u32[]{:S(2)}) collective-permute-start(bf16[256,256]{1,0:T(8,128)(2,1)S(1)} %concatenate.3.refs_8_), channel_id=1, source_target_pairs={{0,20},{4,16},{8,28},{12,24},{16,4},{20,0},{24,12},{28,8},{1,21},{... | collective-permute-start | bytes 393224 | tf_op jit(solution)/shard_map/ppermute | solution.py:466
  219.3 11.5 %collective-permute-start.19 = (bf16[256,256]{1,0:T(8,128)(2,1)S(1)}, bf16[256,256]{1,0:T(8,128)(2,1)S(1)}, u32[]{:S(2)}, u32[]{:S(2)}) collective-permute-start(bf16[256,256]{1,0:T(8,128)(2,1)S(1)} %concatenate.3.refs_8_), channel_id=1, source_target_pairs={{0,24},{4,28},{8,16},{12,20},{16,8},{20,12},{24,0},{28,4},{1,25},{... | collective-permute-start | bytes 393224 | tf_op jit(solution)/shard_map/ppermute | solution.py:466
  221.5 9.4 %collective-permute-start.20 = (bf16[256,256]{1,0:T(8,128)(2,1)S(1)}, bf16[256,256]{1,0:T(8,128)(2,1)S(1)}, u32[]{:S(2)}, u32[]{:S(2)}) collective-permute-start(bf16[256,256]{1,0:T(8,128)(2,1)S(1)} %concatenate.3.refs_8_), channel_id=1, source_target_pairs={{0,28},{4,24},{8,20},{12,16},{16,12},{20,8},{24,4},{28,0},{1,29},{... | collective-permute-start | bytes 393224 | tf_op jit(solution)/shard_map/ppermute | solution.py:466
  246.3 125.6 %all-reduce.19.cloned.1.call-start = ((), (), s32[]{:S(2)}) async-start(), calls=%async_computation.4 | async-start | bytes 7077888 | tf_op jit(solution)/shard_map/psum | solution.py:626
  (54 other events, 336.7 us)
Sparse Core Ops, SparseCore 0:
  44.5 50.1 all-reduce.10
  101.0 43.1 all-reduce.12
  152.2 43.0 all-reduce.14
  246.4 46.6 all-reduce.16
  298.1 73.6 all-reduce.18

commit v2 on v1

v2 whole, which is shorter than its diff:
```python
import functools
import math

import jax
import jax.numpy as jnp
from jax import lax
from jax.experimental import pallas as pl
from jax.experimental.pallas import tpu as pltpu
from jax.sharding import PartitionSpec as P

D = 768
H = 12
HS = 64
BITS = 8
PLANES = 32
HASHES = 4
CONV = 35
RADIUS = 17
FEATS = HASHES * 2**BITS
SHARP = 2.0
NORM_EPS = 1e-05
UNIT_EPS = 1e-06
EXACT = lax.Precision.HIGHEST
F32 = jnp.float32
BF16 = jnp.bfloat16
ROWS = 256
HEADS = 3
TAP_LANE = 111
VMEM = pl.BlockSpec(memory_space=pltpu.VMEM)
SMEM = pl.BlockSpec(memory_space=pltpu.SMEM)
LIMIT = 60 * 1024 * 1024


def dot(a, b):
    return lax.dot_general(a, b, (((1,), (0,)), ((), ())), preferred_element_type=F32)


def dot_nt(a, b):
    return lax.dot_general(a, b, (((1,), (1,)), ((), ())), preferred_element_type=F32)


def dot_exact(a, b):
    return lax.dot_general(
        a, b, (((1,), (0,)), ((), ())), precision=EXACT, preferred_element_type=F32
    )


def doc_count(pos, lengths):
    start = jnp.int32(0)
    found = jnp.zeros_like(pos)
    for d in range(lengths.shape[0]):
        found = found + (pos >= start).astype(jnp.int32)
        start = start + lengths[d]
    return found + (pos >= start).astype(jnp.int32)


def blocks_meet(mine, other, lengths):
    a0 = doc_count(mine * ROWS, lengths)
    a1 = doc_count(mine * ROWS + (ROWS - 1), lengths)
    b0 = doc_count(other * ROWS, lengths)
    b1 = doc_count(other * ROWS + (ROWS - 1), lengths)
    return jnp.logical_and(a0 <= b1, b0 <= a1)


def same_doc(row_start, rows, col_start, cols, lengths, reverse=False):
    rid = row_start + lax.broadcasted_iota(jnp.int32, (rows, 1), 0)
    cid = lax.broadcasted_iota(jnp.int32, (1, cols), 1)
    cid = col_start + ((cols - 1) - cid if reverse else cid)
    return doc_count(rid, lengths) == doc_count(cid, lengths)


def hash_base(picks, m, lanes):
    bit = lax.broadcasted_iota(jnp.int32, (8, lanes), 0)
    factors = []
    for b in range(3):
        on = (bit & (1 << b)) != 0
        row = jnp.broadcast_to(picks[m * BITS + b : m * BITS + b + 1, :], (8, lanes))
        factors.append((on, jnp.where(on, row, 1.0)))
    return factors


def hash_feats(picks, m, lanes):
    factors = hash_base(picks, m, lanes)
    scale = 2.0 ** (-0.5 * BITS)
    feats = [(factors[0][1] * scale) * (factors[1][1] * factors[2][1])]
    rows = {}
    for b in range(3, BITS):
        rows[b] = jnp.broadcast_to(picks[m * BITS + b : m * BITS + b + 1, :], (8, lanes))
        feats = feats + [f * rows[b] for f in feats]
    return feats, rows, factors


def expand(picks, phi_ref):
    lanes = picks.shape[1]
    for m in range(HASHES):
        feats = hash_feats(picks, m, lanes)[0]
        for i in range(0, len(feats), 2):
            both = jnp.concatenate([feats[i], feats[i + 1]], axis=0)
            phi_ref[m * 256 + i * 8 : m * 256 + i * 8 + 16, :] = both.astype(BF16)


def expand_back(picks, dphi_ref, lane0, lanes):
    out = []
    scale = 2.0 ** (-0.5 * BITS)
    for m in range(HASHES):
        feats, rows, factors = hash_feats(picks, m, lanes)
        grads = [
            dphi_ref[m * 256 + i * 8 : m * 256 + i * 8 + 8, lane0 : lane0 + lanes]
            for i in range(32)
        ]
        found = {}
        for b in range(BITS - 1, 2, -1):
            half = len(grads) // 2
            total = grads[half] * feats[0]
            for i in range(1, half):
                total = total + grads[half + i] * feats[i]
            found[b] = jnp.sum(total, axis=0, keepdims=True)
            grads = [grads[i] + grads[half + i] * rows[b] for i in range(half)]
        g = grads[0] * scale
        (on0, f0), (on1, f1), (on2, f2) = factors
        found[0] = jnp.sum(jnp.where(on0, g * (f1 * f2), 0.0), axis=0, keepdims=True)
        found[1] = jnp.sum(jnp.where(on1, g * (f0 * f2), 0.0), axis=0, keepdims=True)
        found[2] = jnp.sum(jnp.where(on2, g * (f0 * f1), 0.0), axis=0, keepdims=True)
        out.extend(found[b] for b in range(BITS))
    return jnp.concatenate(out, axis=0)


def stacked(turned):
    return jnp.concatenate([turned[:, h * ROWS : (h + 1) * ROWS] for h in range(HEADS)], axis=0)


def column(row):
    n = row.shape[1]
    here = lax.broadcasted_iota(jnp.int32, (n, n), 0) == lax.broadcasted_iota(jnp.int32, (n, n), 1)
    return jnp.sum(jnp.where(here, row, 0.0), axis=1, keepdims=True)


def beside(rows):
    return jnp.concatenate([rows[h * HS : (h + 1) * HS] for h in range(HEADS)], axis=1)


def project_body(
    tokens, wq, bq, wk, bk, wv, bv, planes, choose, raw_q, raw_k, tan_q, tan_k, pick_q, pack
):
    x = tokens[...]

    def codes(w, b, raw_ref, tan_ref):
        raw = beside(dot_nt(w[...], x) + column(b[...].reshape(1, -1)))
        raw_ref[...] = raw
        unit = raw * lax.rsqrt(jnp.sum(raw * raw, axis=0, keepdims=True) + UNIT_EPS)
        tan = jnp.tanh(SHARP * dot_exact(planes[...], unit))
        tan_ref[...] = tan
        return dot(choose[...], tan.astype(BF16)).astype(BF16)

    pack[0:PLANES, :] = codes(wk, bk, raw_k, tan_k)
    values = beside(dot_nt(wv[...], x) + column(bv[...].reshape(1, -1)))
    pack[PLANES : PLANES + HS, :] = values.astype(BF16)
    pick_q[...] = codes(wq, bq, raw_q, tan_q)


def call(body, name, out_shape, ins, smem=0, scratch=(), us=2):
    single = not isinstance(out_shape, (tuple, list))
    outs = (out_shape,) if single else tuple(out_shape)
    got = pl.pallas_call(
        body,
        out_shape=outs,
        in_specs=[SMEM] * smem + [VMEM] * (len(ins) - smem),
        out_specs=tuple([VMEM] * len(outs)),
        scratch_shapes=list(scratch),
        name=name,
        compiler_params=pltpu.CompilerParams(vmem_limit_bytes=LIMIT),
        cost_estimate=pl.CostEstimate(
            flops=int(us * 1e9), bytes_accessed=100_000, transcendentals=0
        ),
    )(*ins)
    return got[0] if single else got


def f32(*shape):
    return jax.ShapeDtypeStruct(shape, F32)


def bf16(*shape):
    return jax.ShapeDtypeStruct(shape, BF16)


def project(*ins):
    wide = HEADS * ROWS
    return call(
        project_body,
        "project",
        (
            f32(HS, wide),
            f32(HS, wide),
            f32(PLANES, wide),
            f32(PLANES, wide),
            bf16(PLANES, wide),
            bf16(PLANES + HS, wide),
        ),
        ins,
        us=3,
    )


def local_feats_body(pick_q, pack, feat_q, feat_k, phi):
    for src, dst in ((pick_q, feat_q), (pack, feat_k)):
        for h in range(HEADS):
            picks = src[0:PLANES, h * ROWS : (h + 1) * ROWS].astype(F32)
            expand(picks, phi)
            dst[h] = phi[...].T


def local_feats(pick_q, pack):
    shape = bf16(HEADS, ROWS, FEATS)
    return call(
        local_feats_body,
        "local_feats",
        (shape, shape),
        (pick_q, pack),
        scratch=(pltpu.VMEM((FEATS, ROWS), BF16),),
        us=3,
    )


def window(packs, mine, low, high, n):
    def at(h):
        before = jnp.bitwise_xor(mine, jnp.maximum(mine - 1, 0))
        after = jnp.bitwise_xor(mine, jnp.minimum(mine + 1, n - 1))
        lane = h * ROWS
        return jnp.concatenate(
            [
                packs[before, low:high, lane + 128 : lane + 256],
                packs[0, low:high, lane : lane + 256],
                packs[after, low:high, lane : lane + 128],
            ],
            axis=1,
        )

    return at


def band(row):
    return pltpu.roll(jnp.broadcast_to(row, (ROWS, 512)), 0, 1, stride=1, stride_axis=0)


def split_dot(a, b, mul):
    high = a.astype(BF16)
    low = (a - high.astype(F32)).astype(BF16)
    return mul(high, b) + mul(low, b)


def forward_body(n, lengths, place, slot, feat_q, taps, *refs):
    pack_in, (context, near_half, far_half, weighted, total_out) = refs[:n], refs[n : n + 5]
    packs, phi0, phi1, phi2, acc, tot = refs[n + 5 :]
    phis = (phi0, phi1, phi2)
    mine = place[0]
    for k in range(n):
        packs[k] = pack_in[k][...]
    acc[...] = jnp.zeros_like(acc)
    tot[...] = jnp.zeros_like(tot)

    def block(k, carry):
        other = jnp.bitwise_xor(mine, k)

        @pl.when(blocks_meet(mine, other, lengths))
        def _():
            same = same_doc(mine * ROWS, ROWS, other * ROWS, ROWS, lengths)
            for h in range(HEADS):
                lane = h * ROWS
                expand(packs[k, 0:PLANES, lane : lane + ROWS].astype(F32), phis[h])
                score = dot(feat_q[h], phis[h][...])
                w = jnp.where(same, score * (1.0 / HASHES), 0.0)
                tot[h] += w[:, :128] + w[:, 128:]
                acc[h] += dot_nt(w.astype(BF16), packs[k, PLANES : PLANES + HS, lane : lane + ROWS])

        return carry

    lax.fori_loop(0, n, block, 0)
    near = same_doc(mine * ROWS, ROWS, mine * ROWS - 128, 512, lengths)
    ext = window(packs, mine, PLANES, PLANES + HS, n)
    outs, sums, parts = [], [], []
    for h in range(HEADS):
        total = 1.0 + jnp.sum(tot[h], axis=1, keepdims=True)
        taps_band = jnp.where(near, band(taps[h : h + 1, :]), 0.0)
        conv = split_dot(taps_band, ext(h), dot_nt)
        sums.append(jnp.broadcast_to(total, (ROWS, HS)))
        parts.append(acc[h])
        outs.append(acc[h] / total + conv)
    context[...] = jnp.concatenate(outs, axis=1).astype(BF16)
    half = ROWS // 2
    first = slot[0] >> 1
    near_half[...] = context[pl.ds(pl.multiple_of(first * half, 16), half), :]
    far_half[...] = context[pl.ds(pl.multiple_of((1 - first) * half, 16), half), :]
    weighted[...] = jnp.concatenate(parts, axis=1)
    total_out[...] = jnp.concatenate(sums, axis=1)


def forward(lengths, place, slot, feat_q, taps, packs):
    n = len(packs)
    wide = HEADS * HS
    return call(
        functools.partial(forward_body, n),
        "attend",
        (
            bf16(ROWS, wide),
            bf16(ROWS // 2, wide),
            bf16(ROWS // 2, wide),
            f32(ROWS, wide),
            f32(ROWS, wide),
        ),
        (lengths, place, slot, feat_q, taps, *packs),
        smem=3,
        scratch=(
            pltpu.VMEM((n, PLANES + HS, HEADS * ROWS), BF16),
            pltpu.VMEM((FEATS, ROWS), BF16),
            pltpu.VMEM((FEATS, ROWS), BF16),
            pltpu.VMEM((FEATS, ROWS), BF16),
            pltpu.VMEM((HEADS, ROWS, HS), F32),
            pltpu.VMEM((HEADS, ROWS, 128), F32),
        ),
        us=9,
    )


def unit_back(code_grad, tan, raw, planes_t):
    scale = lax.rsqrt(jnp.sum(raw * raw, axis=0, keepdims=True) + UNIT_EPS)
    unit_grad = dot_exact(planes_t, code_grad * (SHARP * (1.0 - tan * tan)))
    inner = jnp.sum(raw * unit_grad, axis=0, keepdims=True)
    return unit_grad * scale - raw * (scale * scale * scale) * inner


def codes_to_raw(dphi, picks, tan, raw, choose_back, planes_t):
    parts = []
    for h in range(HEADS):
        for u in range(2):
            lane = h * ROWS + u * 128
            parts.append(
                expand_back(picks[0:PLANES, lane : lane + 128].astype(F32), dphi.at[h], u * 128, 128)
            )
    pick_grad = jnp.concatenate(parts, axis=1) * (1.0 / HASHES)
    code_grad = dot_exact(choose_back[...], pick_grad)
    return unit_back(code_grad, tan[...], raw[...], planes_t[...])


def query_back_body(
    n, lengths, place, grads, row_totals, pick_q, tan, raw, choose_back, planes_t, weight, *refs
):
    pack_in, (grad_out, input_out, taps_out) = refs[:n], refs[n : n + 3]
    packs, phi0, phi1, phi2, dphi = refs[n + 3 :]
    phis = (phi0, phi1, phi2)
    mine = place[0]
    for k in range(n):
        packs[k] = pack_in[k][...]
    dphi[...] = jnp.zeros_like(dphi)

    def block(k, carry):
        other = jnp.bitwise_xor(mine, k)

        @pl.when(blocks_meet(mine, other, lengths))
        def _():
            same = same_doc(other * ROWS, ROWS, mine * ROWS, ROWS, lengths)
            for h in range(HEADS):
                lane = h * ROWS
                expand(packs[k, 0:PLANES, lane : lane + ROWS].astype(F32), phis[h])
                values = packs[k, PLANES : PLANES + HS, lane : lane + ROWS].T
                dw = dot_nt(values, grads[:, h * HS : (h + 1) * HS]) + row_totals[h : h + 1, :]
                dw = jnp.where(same, dw, 0.0).astype(BF16)
                dphi[h] += dot(phis[h][...], dw)

        return carry

    lax.fori_loop(0, n, block, 0)
    raw_grad = codes_to_raw(dphi, pick_q, tan, raw, choose_back, planes_t)
    turned = stacked(raw_grad).astype(BF16)
    grad_out[...] = turned
    input_out[...] = dot(turned.astype(F32).T.astype(BF16), weight[...])
    near_rev = same_doc(mine * ROWS, ROWS, mine * ROWS - 128, 512, lengths, reverse=True)
    turn = lax.broadcasted_iota(jnp.int32, (512, 512), 0) + lax.broadcasted_iota(
        jnp.int32, (512, 512), 1
    )
    flip = (turn == 511).astype(F32)
    flip_low = flip.astype(BF16)
    ext = window(packs, mine, PLANES, PLANES + HS, n)
    side = grads[:, 3 * HS : 4 * HS].astype(F32)
    tap_rows = []
    for h in range(HEADS):
        total = side[:, HEADS + h : HEADS + h + 1]
        context_grad = (grads[:, h * HS : (h + 1) * HS].astype(F32) * total).astype(BF16)
        flipped = dot(ext(h), flip_low).astype(BF16)
        cross = jnp.where(near_rev, dot(context_grad, flipped), 0.0)
        cross = pltpu.roll(cross, 0, 1, stride=1, stride_axis=0)
        tap_rows.append(jnp.sum(cross, axis=0, keepdims=True))
    tap_rows.append(jnp.zeros((8 - HEADS, 512), F32))
    taps_out[...] = dot_exact(jnp.concatenate(tap_rows, axis=0), flip)


def query_back(*ins):
    packs = ins[-1]
    n = len(packs)
    return call(
        functools.partial(query_back_body, n),
        "query_back",
        (bf16(HEADS * HS, ROWS), f32(ROWS, D), f32(8, 512)),
        (*ins[:-1], *packs),
        smem=2,
        scratch=(
            pltpu.VMEM((n, PLANES + HS, HEADS * ROWS), BF16),
            pltpu.VMEM((FEATS, ROWS), BF16),
            pltpu.VMEM((FEATS, ROWS), BF16),
            pltpu.VMEM((FEATS, ROWS), BF16),
            pltpu.VMEM((HEADS, FEATS, ROWS), F32),
        ),
        us=9,
    )


def key_back_body(
    n,
    parts,
    lengths,
    place,
    slot,
    feat_k,
    pack,
    tan,
    raw,
    taps_back,
    choose_back,
    planes_t,
    wk,
    wv,
    query_input,
    *refs,
):
    pick_in, grad_in = refs[:n], refs[n : 2 * n]
    turned_out = refs[2 * n]
    input_out = refs[2 * n + 1 : 2 * n + 1 + parts]
    picks, grads, phi0, phi1, phi2, dphi, acc, inputs = refs[2 * n + 1 + parts :]
    phis = (phi0, phi1, phi2)
    mine = place[0]
    for k in range(n):
        picks[k] = pick_in[k][...]
        grads[k] = grad_in[k][...]
    dphi[...] = jnp.zeros_like(dphi)
    acc[...] = jnp.zeros_like(acc)

    def block(k, carry):
        other = jnp.bitwise_xor(mine, k)

        @pl.when(blocks_meet(mine, other, lengths))
        def _():
            same = same_doc(mine * ROWS, ROWS, other * ROWS, ROWS, lengths)
            same_t = same_doc(other * ROWS, ROWS, mine * ROWS, ROWS, lengths)
            for h in range(HEADS):
                lane = h * ROWS
                expand(picks[k, :, lane : lane + ROWS].astype(F32), phis[h])
                score = dot(feat_k[h], phis[h][...])
                w = jnp.where(same, score * (1.0 / HASHES), 0.0).astype(BF16)
                grad = grads[k, :, h * HS : (h + 1) * HS]
                acc[h] += dot(w, grad)
                values_t = pack[PLANES : PLANES + HS, lane : lane + ROWS]
                side = grads[k, :, 3 * HS : 4 * HS].astype(F32)
                row_total = side[:, h : h + 1] + side[:, 2 * HEADS + h : 2 * HEADS + h + 1]
                dw = dot(grad, values_t) + row_total
                dw = jnp.where(same_t, dw, 0.0).astype(BF16)
                dphi[h] += dot(phis[h][...], dw)

        return carry

    lax.fori_loop(0, n, block, 0)
    raw_grad = codes_to_raw(dphi, pack, tan, raw, choose_back, planes_t)
    key_turned = stacked(raw_grad).astype(BF16)
    key_rows = key_turned.astype(F32).T

    before = jnp.bitwise_xor(mine, jnp.maximum(mine - 1, 0))
    after = jnp.bitwise_xor(mine, jnp.minimum(mine + 1, n - 1))
    near = same_doc(mine * ROWS, ROWS, mine * ROWS - 128, 512, lengths)
    ext = jnp.concatenate([grads[before, 128:, :], grads[0], grads[after, :128, :]], axis=0)
    side = ext[:, 3 * HS : 4 * HS].astype(F32)
    outs = []
    for h in range(HEADS):
        total = side[:, HEADS + h : HEADS + h + 1]
        context_grad = (ext[:, h * HS : (h + 1) * HS].astype(F32) * total).astype(BF16)
        taps_band = jnp.where(near, band(taps_back[h : h + 1, :]), 0.0)
        outs.append(acc[h] + split_dot(taps_band, context_grad, dot))
    value_rows = jnp.concatenate(outs, axis=1).astype(BF16)
    wide = HEADS * HS
    turned_out[0:wide, :] = key_turned
    turned_out[wide : 2 * wide, :] = value_rows.astype(F32).T.astype(BF16)
    inputs[...] = (
        query_input[...] + dot(key_rows.astype(BF16), wk[...]) + dot(value_rows, wv[...])
    ).astype(BF16)
    put_chunks(slot[0], inputs, input_out)


def key_back(ins, picks, grads, parts):
    n = len(picks)
    return call(
        functools.partial(key_back_body, n, parts),
        "key_back",
        (bf16(2 * HEADS * HS, ROWS), *[bf16(ROWS // parts, D)] * parts),
        (*ins, *picks, *grads),
        smem=3,
        scratch=(
            pltpu.VMEM((n, PLANES, HEADS * ROWS), BF16),
            pltpu.VMEM((n, ROWS, 4 * HS), BF16),
            pltpu.VMEM((FEATS, ROWS), BF16),
            pltpu.VMEM((FEATS, ROWS), BF16),
            pltpu.VMEM((FEATS, ROWS), BF16),
            pltpu.VMEM((HEADS, FEATS, ROWS), F32),
            pltpu.VMEM((HEADS, ROWS, HS), F32),
            pltpu.VMEM((ROWS, D), BF16),
        ),
        us=15,
    )


def padded(rows, n):
    return -(-rows // (16 * n)) * (16 * n)


def put_halves(place, whole, mine, other):
    half = whole.shape[0] // 2
    core = place & 1
    mine[...] = whole[pl.ds(pl.multiple_of(core * half, 16), half), :]
    other[...] = whole[pl.ds(pl.multiple_of((1 - core) * half, 16), half), :]


def put_chunks(index, whole, outs):
    rows = outs[0].shape[0]
    for k, out in enumerate(outs):
        start = pl.multiple_of(jnp.bitwise_xor(index, k) * rows, 16)
        out[...] = whole[pl.ds(start, rows), :]


def swap(value, axis, k):
    n = lax.axis_size(axis)
    return lax.ppermute(value, axis, [(i, i ^ k) for i in range(n)])


def over_seq(value):
    n = lax.axis_size("seq")
    got = [value] + [None] * (n - 1)
    for k in range(2, n, 2):
        got[k] = swap(value, "seq", k)
    for k in range(0, n, 2):
        got[k + 1] = swap(got[k], "seq", 1)
    return got


HID_ORDER = (0, 2, 1, 3)


def hid_swap(value, j):
    return swap(value, "hid", HID_ORDER[j])


def over_hid(value):
    return [value] + [hid_swap(value, j) for j in range(1, len(HID_ORDER))]


def exchange(chunks):
    return [chunks[0]] + [hid_swap(chunks[j], j) for j in range(1, len(chunks))]


def flat(ref):
    return ref[...].reshape(1, -1)


def norm_stats(rows):
    center = rows - jnp.mean(rows, axis=-1, keepdims=True)
    inverse = lax.rsqrt(jnp.mean(center * center, axis=-1, keepdims=True) + NORM_EPS)
    return center * inverse, inverse


def norm_grad(grad, normed, inverse, gain):
    scaled = grad * gain
    return inverse * (
        scaled
        - jnp.mean(scaled, axis=-1, keepdims=True)
        - normed * jnp.mean(scaled * normed, axis=-1, keepdims=True)
    )


def column_sums(*rows):
    sums = [jnp.sum(r, axis=0, keepdims=True) for r in rows]
    return jnp.concatenate(sums + [jnp.zeros((8 - len(sums), D), F32)], axis=0)


def two_parts(sums):
    high = sums.astype(BF16).astype(F32)
    return jnp.concatenate([high, sums - high], axis=0).astype(BF16)


def partner_weights(core, got, other, both):
    both[core] = got[...]
    both[1 - core] = other[...]


def gelu_parts(x):
    cdf = 0.5 * (1.0 + lax.erf(x * math.sqrt(0.5)))
    slope = cdf + x * (jnp.exp(-0.5 * x * x) * (1.0 / math.sqrt(2.0 * math.pi)))
    return (x * cdf).astype(BF16), slope


def keep_and_send(partial, quarter, keep, send):
    rows = keep.shape[0]
    keep[...] = partial[pl.ds(pl.multiple_of(quarter * rows, 8), rows), :]
    other = pl.multiple_of((1 - quarter) * rows, 8)
    send[...] = partial[pl.ds(other, rows), :].astype(BF16)


def feed_body(parts, place, slot, *refs):
    tokens, mixer_shift, gain, shift, up, up_shift, down, got, other, far_shift = refs[:10]
    contexts, mixers = refs[10 : 10 + parts], refs[10 + parts : 10 + 2 * parts]
    first_mine, normed_mine, inverse_mine, low_out, slope_out, keep, send = refs[
        10 + 2 * parts : 17 + 2 * parts
    ]
    first, normed, inverse, partial, both = refs[17 + 2 * parts :]
    half = ROWS // 2
    partner_weights(place[0] & 1, got, other, both)
    mine = tokens[pl.ds(pl.multiple_of((slot[0] >> 1) * half, 16), half), :]
    mixed = flat(mixer_shift) + mine.astype(F32)
    for c, m in zip(contexts, mixers):
        mixed = mixed + dot(c[...], m[...])
    n1, r1 = norm_stats(mixed)
    rows1 = n1 * flat(gain) + flat(shift)
    first[...] = rows1
    normed[...] = n1
    inverse[...] = jnp.broadcast_to(r1, inverse.shape)
    low = rows1.astype(BF16)
    low_out[...] = low
    hidden, slope = gelu_parts(dot(low, up[...]) + flat(up_shift))
    slope_out[:, 0:D] = slope
    far_hidden, far_slope = gelu_parts(dot(low, both[0]) + flat(far_shift))
    slope_out[:, D:] = far_slope
    partial[...] = dot(hidden, down[...]) + dot(far_hidden, both[1])
    quarter = slot[0] & 1
    keep_and_send(partial, quarter, keep, send)
    rows = first_mine.shape[0]
    start = pl.multiple_of(quarter * rows, 8)
    first_mine[...] = first[pl.ds(start, rows), :]
    normed_mine[...] = normed[pl.ds(start, rows), :]
    inverse_mine[...] = inverse[pl.ds(start, rows), :]


def second_body(slot, first, out_grad, down_shift, gain, shift, keep, got, layer, grad_out, low_out):
    rows = first.shape[0]
    total = first[...] + flat(down_shift) + keep[...] + got[...].astype(F32)
    n2, r2 = norm_stats(total)
    grad = out_grad[pl.ds(pl.multiple_of(slot[0] * rows, 8), rows), :]
    dh2 = norm_grad(grad, n2, r2, flat(gain))
    grad_out[...] = dh2
    low = dh2.astype(BF16)
    low_out[...] = low
    layer[0:rows, :] = (n2 * flat(gain) + flat(shift)).astype(BF16)
    layer[rows:, :] = two_parts(column_sums(grad * n2, grad, low.astype(F32)))


def feed_back_body(place, slot, slope, up, down, got, other, low_mine, low_got, low_half, keep, send, partial, both):
    partner_weights(place[0] & 1, got, other, both)
    quarter = slot[0] & 1
    take_chunks(quarter, (low_mine, low_got), low_half)
    low = low_half[...]
    near = (dot_nt(low, down[...]) * slope[:, 0:D]).astype(BF16)
    far = (dot_nt(low, both[1]) * slope[:, D:]).astype(BF16)
    partial[...] = dot_nt(near, up[...]) + dot_nt(far, both[0])
    keep_and_send(partial, quarter, keep, send)


def take_chunks(index, pieces, whole):
    rows = whole.shape[0] // len(pieces)
    for k, piece in enumerate(pieces):
        start = pl.multiple_of(jnp.bitwise_xor(index, k) * rows, 16)
        whole[pl.ds(start, rows), :] = piece[0:rows, :]


def first_back_body(parts, grad, normed, inverse, gain, keep, got, *refs):
    mixers = refs[:parts]
    dh1_out, payload = refs[parts : parts + 2]
    outs = refs[parts + 2 :]
    total = grad[...] + keep[...] + got[...].astype(F32)
    n1 = normed[...]
    dh1 = norm_grad(total, n1, inverse[:, 0:1], flat(gain))
    dh1_out[...] = dh1
    low = dh1.astype(BF16)
    rows = dh1.shape[0]
    payload[0:rows, :] = low
    payload[rows:, :] = two_parts(column_sums(total * n1, total, low.astype(F32)))
    for m, out in zip(mixers, outs):
        out[...] = dot_nt(low, m[...]).astype(BF16)


def split_body(parts, chunk, weighted, total, *refs):
    pieces, (grad_pack, row_totals), (whole,) = refs[:parts], refs[parts : parts + 2], refs[parts + 2 :]
    take_chunks(chunk[0], pieces, whole)
    dctx = whole[...].astype(F32)
    wide = HEADS * HS
    each = total[...]
    grad_pack[:, 0:wide] = (dctx / each).astype(BF16)
    product = dctx * weighted[...]
    cols = []
    for h in range(HEADS):
        norm = each[:, h * HS : h * HS + 1]
        inner = jnp.sum(product[:, h * HS : (h + 1) * HS], axis=1, keepdims=True)
        cols.append((-inner / (norm * norm), norm))
    lane = lax.broadcasted_iota(jnp.int32, (ROWS, 128), 1)
    side = jnp.zeros((ROWS, 128), F32)
    for h, (grad, norm) in enumerate(cols):
        high = grad.astype(BF16).astype(F32)
        side = jnp.where(lane == h, high, side)
        side = jnp.where(lane == HEADS + h, norm, side)
        side = jnp.where(lane == 2 * HEADS + h, grad - high, side)
        side = jnp.where(lane == 64 + h, grad, side)
    grad_pack[:, wide : wide + 64] = side[:, 0:64].astype(BF16)
    row_totals[...] = side.T[64:72, :]


def feed_grads_body(place, slot, low_mine, low_got, down_mine, down_got, up, up_shift, down, half_mine, half_other, sums, low_all, down_all, whole):
    take_chunks(slot[0] >> 1, (low_mine, low_got), low_all)
    take_chunks(slot[0] >> 1, (down_mine, down_got), down_all)
    low, grad = low_all[...], down_all[...]
    hidden, slope = gelu_parts(dot(low, up[...]) + flat(up_shift))
    up_low = (dot_nt(grad, down[...]) * slope).astype(BF16)
    ff = hidden.shape[1]
    whole[0:ff, :] = dot(hidden.T, grad).astype(BF16)
    whole[ff:, :] = dot(low.T, up_low).astype(BF16)
    put_halves(place[0], whole, half_mine, half_other)
    sums[...] = jnp.broadcast_to(jnp.sum(up_low.astype(F32), axis=0, keepdims=True), sums.shape)


def mixer_grads_body(parts, place, slot, context, up_sums, taps, *refs):
    layers, payloads = refs[:parts], refs[parts : 2 * parts]
    half_mine, half_other, layer_out, whole, mixed = refs[2 * parts :]
    wide = HEADS * HS
    take_chunks(slot[0], layers, layer_out)
    take_chunks(slot[0], payloads, mixed)
    rows = ROWS // parts

    def summed(refs):
        total = jnp.zeros((8, D), F32)
        for r in refs:
            total = total + r[rows : rows + 8, :].astype(F32) + r[rows + 8 : rows + 16, :].astype(F32)
        return total

    context_t = context[...].astype(F32).T.astype(BF16)
    whole[0:wide, :] = dot(context_t, mixed[...]).astype(BF16)
    tap_block = jnp.concatenate([taps[0:HEADS, :], jnp.zeros((HEADS, D - 512), F32)], axis=1)
    small = jnp.concatenate(
        [summed(layers)[0:3], summed(payloads)[0:3], up_sums[0:1, :], tap_block, jnp.zeros((6, D), F32)],
        axis=0,
    )
    whole[wide : wide + 16, :] = small.astype(BF16)
    rest = whole.shape[0] - wide - 16
    whole[wide + 16 :, :] = jnp.zeros((rest, D), BF16)
    put_halves(place[0], whole, half_mine, half_other)


def halve_body(place, mine, other, *refs):
    outs, (whole,) = refs[:-1], refs[-1:]
    whole[...] = (mine[...].astype(F32) + other[...].astype(F32)).astype(BF16)
    put_chunks(place[0] >> 1, whole, outs)


def settle_body(*refs):
    total = refs[0][...].astype(F32)
    for r in refs[1:-1]:
        total = total + r[...].astype(F32)
    refs[-1][...] = total.astype(BF16)


def join_body(place, *refs):
    take_chunks(place[0] >> 1, refs[:-1], refs[-1])


def chip_swaps(value, n):
    return [swap(value, "seq", 2 * k) for k in range(1, n // 2)]


def sum_over_seq(mine, other, place, n):
    chips = n // 2
    half, width = mine.shape
    piece = bf16(half // chips, width)
    got = swap(other, "seq", 1)
    pieces = call(
        halve_body,
        "halve",
        [piece] * chips,
        (place, mine, got),
        smem=1,
        scratch=(pltpu.VMEM((half, width), BF16),),
    )
    terms = [pieces[0]] + [swap(pieces[k], "seq", 2 * k) for k in range(1, chips)]
    settled = call(settle_body, "settle", piece, terms)
    full = call(
        join_body, "join", bf16(half, width), (place, settled, *chip_swaps(settled, n)), smem=1
    )
    return full, swap(full, "seq", 1)


def both_halves(place, mine, other, whole):
    half = mine.shape[0]
    core = place & 1
    whole[pl.ds(pl.multiple_of(core * half, 16), half), :] = mine[...]
    whole[pl.ds(pl.multiple_of((1 - core) * half, 16), half), :] = other[...]


def finish_feed_body(place, mine, other, down, up, whole):
    both_halves(place[0], mine, other, whole)
    ff = down.shape[0]
    down[...] = whole[0:ff, :].astype(F32)
    up[...] = whole[ff:, :].astype(F32)


def finish_small_body(place, mine, other, mixer, g2, s2, od, g1, s1, om, ou, taps, whole):
    both_halves(place[0], mine, other, whole)
    wide = HEADS * HS
    mixer[...] = whole[0:wide, :].astype(F32)
    rows = whole[wide : wide + 16, :].astype(F32)
    for i, out in enumerate((g2, s2, od, g1, s1, om, ou)):
        out[...] = rows[i : i + 1, :].reshape(D)
    taps[...] = rows[7 : 7 + HEADS, TAP_LANE : TAP_LANE + CONV]


def weight_grads_body(n, *refs):
    queries, others, tokens = refs[:n], refs[n : 2 * n], refs[2 * n : 3 * n]
    q, k, v, oq, ok, ov = refs[3 * n : 3 * n + 6]
    turned, rows = refs[3 * n + 6 :]
    wide = HEADS * HS
    for i in range(n):
        turned[0:wide, i * ROWS : (i + 1) * ROWS] = queries[i][...]
        turned[wide:, i * ROWS : (i + 1) * ROWS] = others[i][...]
        rows[i * ROWS : (i + 1) * ROWS, :] = tokens[i][...]
    ones = jnp.ones((16, n * ROWS), BF16)
    for i, (grad, sums) in enumerate(((q, oq), (k, ok), (v, ov))):
        part = turned[i * wide : (i + 1) * wide, :]
        grad[...] = dot(part, rows[...])
        sums[...] = dot_nt(ones, part)[0:1, :].reshape(wide)


def tokens_sum_body(grad, *refs):
    total = grad[...]
    for r in refs[:-1]:
        total = total + r[...].astype(F32)
    refs[-1][...] = total.astype(BF16)


def tokens_out_body(chunk, *refs):
    pieces, out = refs[:-1], refs[-1]
    rows = out.shape[0] // len(pieces)
    for k, piece in enumerate(pieces):
        start = pl.multiple_of(jnp.bitwise_xor(chunk[0], k) * rows, 16)
        out[pl.ds(start, rows), :] = piece[...].astype(F32)


def on_device(
    tokens,
    query_weight,
    query_shift,
    key_weight,
    key_shift,
    value_weight,
    value_shift,
    mixer_weight,
    mixer_shift,
    conv_taps,
    first_gain,
    first_shift,
    up_weight,
    up_shift,
    down_weight,
    down_shift,
    second_gain,
    second_shift,
    hyperplanes,
    plane_choice,
    doc_lengths,
    out_grad,
):
    n = lax.axis_size("seq")
    parts = lax.axis_size("hid")
    place = lax.axis_index("seq").reshape(1).astype(jnp.int32)
    hid = lax.axis_index("hid")
    slot = sum(jnp.where(hid == h, HID_ORDER[h], 0) for h in range(parts))
    slot = slot.reshape(1).astype(jnp.int32)
    rows, half = ROWS // parts, ROWS // 2
    units, wide = up_weight.shape[1], HEADS * HS
    hot = plane_choice.reshape(-1, 1) == jnp.arange(PLANES, dtype=jnp.int32)
    choose = hot.astype(BF16)
    choose_back = hot.astype(F32).T
    planes_t = hyperplanes.T
    wq, wk, wv = query_weight.T, key_weight.T, value_weight.T
    side = (TAP_LANE, 512 - TAP_LANE - CONV)
    taps = jnp.pad(conv_taps, ((0, 5), side))
    taps_back = jnp.pad(conv_taps[:, ::-1], ((0, 5), side))

    weights = jnp.where(place[0] % 2 == 0, up_weight, down_weight)
    got = hid_swap(weights, 2)
    other = swap(got, "seq", 1)
    far_shift = hid_swap(up_shift, 2)
    mixers = over_hid(mixer_weight)

    raw_q, raw_k, tan_q, tan_k, pick_q, pack = project(
        tokens, wq, query_shift, wk, key_shift, wv, value_shift, hyperplanes, choose
    )
    packs = over_seq(pack)
    feat_q, feat_k = local_feats(pick_q, pack)
    context, near_half, far_half, weighted, total = forward(
        doc_lengths, place, slot, feat_q, taps, packs
    )
    contexts = [
        near_half,
        hid_swap(near_half, 1),
        hid_swap(far_half, 2),
        hid_swap(far_half, 3),
    ]
    pick_later, tokens_later, context = lax.optimization_barrier((pick_q, tokens, context))
    picks = over_seq(pick_later)
    token_blocks = over_seq(tokens_later)
    first_mine, normed_mine, inverse_mine, low, slope, keep, send = call(
        functools.partial(feed_body, parts),
        "feed",
        (
            f32(rows, D),
            f32(rows, D),
            f32(rows, 128),
            bf16(half, D),
            f32(half, 2 * units),
            f32(rows, D),
            bf16(rows, D),
        ),
        (
            place,
            slot,
            tokens,
            mixer_shift,
            first_gain,
            first_shift,
            up_weight,
            up_shift,
            down_weight,
            got,
            other,
            far_shift,
            *contexts,
            *mixers,
        ),
        smem=2,
        scratch=(
            pltpu.VMEM((half, D), F32),
            pltpu.VMEM((half, D), F32),
            pltpu.VMEM((half, 128), F32),
            pltpu.VMEM((half, D), F32),
            pltpu.VMEM((2, D, units), BF16),
        ),
        us=5,
    )
    layer, dh2, down_low = call(
        second_body,
        "second_norm",
        (bf16(rows + 16, D), f32(rows, D), bf16(rows, D)),
        (
            slot,
            first_mine,
            out_grad,
            down_shift,
            second_gain,
            second_shift,
            keep,
            hid_swap(send, 1),
        ),
        smem=1,
    )
    down_half, keep, send = call(
        feed_back_body,
        "feed_back",
        (bf16(half, D), f32(rows, D), bf16(rows, D)),
        (
            place,
            slot,
            slope,
            up_weight,
            down_weight,
            got,
            other,
            down_low,
            hid_swap(down_low, 1),
        ),
        smem=2,
        scratch=(pltpu.VMEM((half, D), F32), pltpu.VMEM((2, D, units), BF16)),
        us=4,
    )
    first_back = call(
        functools.partial(first_back_body, parts),
        "first_norm_back",
        (f32(rows, D), bf16(rows + 16, D), *[bf16(rows, wide)] * parts),
        (dh2, normed_mine, inverse_mine, first_gain, keep, hid_swap(send, 1), *mixers),
        us=3,
    )
    dh1, payload = first_back[:2]
    grad_pack, row_totals = call(
        functools.partial(split_body, parts),
        "split",
        (bf16(ROWS, 4 * HS), f32(8, ROWS)),
        (slot, weighted, total, *exchange(first_back[2:])),
        smem=1,
        scratch=(pltpu.VMEM((ROWS, wide), BF16),),
    )
    grad_packs = over_seq(grad_pack)

    feed_half = padded(units + D, n) // 2
    feed_mine, feed_other, up_sums = call(
        feed_grads_body,
        "feed_grads",
        (bf16(feed_half, D), bf16(feed_half, D), f32(8, units)),
        (
            place,
            slot,
            low,
            hid_swap(low, 2),
            down_half,
            hid_swap(down_half, 2),
            up_weight,
            up_shift,
            down_weight,
        ),
        smem=2,
        scratch=(
            pltpu.VMEM((ROWS, D), BF16),
            pltpu.VMEM((ROWS, D), BF16),
            pltpu.VMEM((2 * feed_half, D), BF16),
        ),
        us=6,
    )
    feed_sums = sum_over_seq(feed_mine, feed_other, place, n)

    query_turned, query_input, tap_rows = query_back(
        doc_lengths,
        place,
        grad_pack,
        row_totals,
        pick_q,
        tan_q,
        raw_q,
        choose_back,
        planes_t,
        wq,
        packs,
    )
    query_blocks = over_seq(query_turned)
    layer_later, payload_later, grad_pack = lax.optimization_barrier((layer, payload, grad_pack))
    layers = over_hid(layer_later)
    payloads = over_hid(payload_later)
    small_half = padded(wide + 16, n) // 2
    small_mine, small_other, layer_out = call(
        functools.partial(mixer_grads_body, parts),
        "mixer_grads",
        (bf16(small_half, D), bf16(small_half, D), bf16(ROWS, D)),
        (place, slot, context, up_sums, tap_rows, *layers, *payloads),
        smem=2,
        scratch=(pltpu.VMEM((2 * small_half, D), BF16), pltpu.VMEM((ROWS, D), BF16)),
    )
    small_sums = sum_over_seq(small_mine, small_other, place, n)
    last = key_back(
        (
            doc_lengths,
            place,
            slot,
            feat_k,
            pack,
            tan_k,
            raw_k,
            taps_back,
            choose_back,
            planes_t,
            wk,
            wv,
            query_input,
        ),
        picks,
        grad_packs,
        parts,
    )
    other_blocks = over_seq(last[0])
    piece = call(tokens_sum_body, "tokens_sum", bf16(rows, D), (dh1, *exchange(last[1:])))
    tokens_grad = call(
        tokens_out_body, "tokens_out", f32(ROWS, D), (slot, *over_hid(piece)), smem=1
    )
    down_grad, up_grad = call(
        finish_feed_body,
        "finish_feed",
        (f32(units, D), f32(D, units)),
        (place, *feed_sums),
        smem=1,
        scratch=(pltpu.VMEM((2 * feed_half, D), BF16),),
        us=4,
    )
    mixer_grad, g2, s2, od, g1, s1, om, ou, taps_grad = call(
        finish_small_body,
        "finish_small",
        (f32(wide, D), *[f32(D)] * 6, f32(units), f32(HEADS, CONV)),
        (place, *small_sums),
        smem=1,
        scratch=(pltpu.VMEM((2 * small_half, D), BF16),),
    )
    q, k, v, oq, ok, ov = call(
        functools.partial(weight_grads_body, n),
        "weight_grads",
        (*[f32(wide, D)] * 3, *[f32(wide)] * 3),
        (*query_blocks, *other_blocks, *token_blocks),
        scratch=(pltpu.VMEM((3 * wide, n * ROWS), BF16), pltpu.VMEM((n * ROWS, D), BF16)),
        us=4,
    )
    return (
        layer_out,
        tokens_grad,
        q.T,
        oq,
        k.T,
        ok,
        v.T,
        ov,
        mixer_grad,
        om,
        taps_grad,
        g1,
        s1,
        up_grad,
        ou,
        down_grad,
        od,
        g2,
        s2,
    )


def solution(mesh):
    placed = (
        P("seq", None),
        P(None, "hid"),
        P("hid"),
        P(None, "hid"),
        P("hid"),
        P(None, "hid"),
        P("hid"),
        P("hid", None),
        P(),
        P("hid", None),
        P(),
        P(),
        P(None, "hid"),
        P("hid"),
        P("hid", None),
        P(),
        P(),
        P(),
        P(),
        P(),
        P(),
        P("seq", None),
    )
    return jax.shard_map(
        on_device,
        mesh=mesh,
        in_specs=placed,
        out_specs=(
            P("seq", None),
            P("seq", None),
            P(None, "hid"),
            P("hid"),
            P(None, "hid"),
            P("hid"),
            P(None, "hid"),
            P("hid"),
            P("hid", None),
            P(),
            P("hid", None),
            P(),
            P(),
            P(None, "hid"),
            P("hid"),
            P("hid", None),
            P(),
            P(),
            P(),
        ),
        check_vma=False,
    )
```

time: 388 us -> 290 us (0.75)
  waiting for transfers between devices: 220 us -> 85.8 us
  starting transfers between devices: 27.2 us -> 91.8 us
  Pallas kernels: 32.5 us -> 93.8 us
  blocking collectives: 32.5 us -> 0 us
  other arithmetic: 28 us -> 2.08 us
  matrix products: 18.6 us -> 0 us
  between operations: 14.4 us -> 1.48 us
    psum x5 -> x0, waiting for transfers between devices: 207 us -> none  [the longest x1 76.8 us: on_device(): lax.psum(weight_grad(query_low).astype(jnp.bfloat16), 'seq')]
    ppermute x21 -> x87, waiting for transfers between devices: 13 us -> 85.8 us  [swap(): return lax.ppermute(value, axis, [(i, i ^ k) for i in range(n)])]
    ppermute x21 -> x87, starting transfers between devices: 26.8 us -> 91.8 us  [swap(): return lax.ppermute(value, axis, [(i, i ^ k) for i in range(n)])]
    pallas_call x5 -> x23, Pallas kernels: 32.5 us -> 93.8 us  [call(): pl.pallas_call(body, out_shape=outs, in_specs=[SMEM] * smem + [VMEM] * (l...]
    psum x1 -> x0, blocking collectives: 32.5 us -> none  [on_device(): lax.psum(jnp.sum(query_low.astype(jnp.float32), axis=0).astype(jnp.bfloat...]
    dot_general x15 -> x0, matrix products: 18.6 us -> none  [the longest x1 3.17 us: on_device(): jnp.dot(first_low, up_weight, preferred_element_type=jnp.float32) + up_shift]
    convert_element_type x18 -> x0, other arithmetic: 16.6 us -> none  [the longest x1 1.91 us: on_device(): lax.psum(weight_grad(key_low).astype(jnp.bfloat16), 'seq')]
    reduce_sum x12 -> x0, other arithmetic: 7.94 us -> none  [the longest x2 3.33 us: norm_backward(): return (rows_grad, jnp.sum(grad * normed, axis=0), jnp.sum(grad, axis=0))]
  transfers between devices with their start and end apart: 26 -> 87, of which waited for: 10 -> 17; matrix products, arithmetic and copies ran while one was open for 8% -> 1% of each run, Pallas kernels for 3% -> 27%
where the time goes in v2:
time: 290 us; the launch traced here: 288 us
  Pallas kernels  93.8 us (32%)
  starting transfers between devices  91.8 us (32%)
  waiting for transfers between devices  85.8 us (30%)
  local copies, waits for them, and re-layouts  12.7 us (4%)
    pallas_call x23, Pallas kernels, call(): pl.pallas_call(body, out_shape=outs, in_specs=[SMEM] * smem + [VMEM] * (l...  93.8 us
    ppermute x87, starting transfers between devices, swap(): return lax.ppermute(value, axis, [(i, i ^ k) for i in range(n)])  91.8 us
    ppermute x87, waiting for transfers between devices, swap(): return lax.ppermute(value, axis, [(i, i ^ k) for i in range(n)])  85.8 us
    unnamed x199, local copies, waits for them, and re-layouts  11.2 us
  transfers between devices with their start and end apart: 87, of which 17 were waited for; matrix products, arithmetic and copies ran while one was open for 1% of the time, Pallas kernels for 27%

profile of v2, /device:TPU:0, one launch (start us, length us, event | category | flops | bytes accessed | tf_op | source)
XLA Modules:
  0.0 287.6 jit_solution(2951762567415683208)
XLA Ops:
  2.1 3.1 %collective-permute-start.7 = (bf16[768,768]{1,0:T(8,128)(2,1)S(1)}, bf16[768,768]{1,0:T(8,128)(2,1)S(1)}, u32[]{:S(2)}, u32[]{:S(2)}) collective-permute-start(bf16[768,768]{1,0:T(8,128)(2,1)S(1)} %broadcast_select_fusion), channel_id=1, source_target_pairs={{0,1},{1,0},{2,3},{3,2},{4,5},{5,4},{6,7},{7,6},{8,9},{9,8},{10,11... | collective-permute-start | bytes 3538952 | tf_op jit(solution)/shard_map/ppermute | solution.py:538
  6.0 3.2 %project.1 = (f32[64,768]{1,0:T(8,128)}, f32[64,768]{1,0:T(8,128)}, f32[32,768]{1,0:T(8,128)}, f32[32,768]{1,0:T(8,128)}, bf16[32,768]{1,0:T(8,128)(2,1)}, /*index=5*/bf16[96,768]{1,0:T(8,128)(2,1)}) custom-call(bf16[256,768]{1,0:T(8,128)(2,1)} %refs_16_, bf16[192,768]{1,0:T(8,128)(2,1)} %bitcast.11, f32[192]{0:T(256)} %bq.1, bf16[192,768]{1,0:T(8,128)(2,1)} %bitcast.13, ...), custom_call_target="tpu_custom_call" | custom-call | flops 3000000000 | bytes 100000 | tf_op jit(solution)/shard_map/project/pallas_call | solution.py:164
  12.6 18.5 %collective-permute-done.7.refs_7_.got = bf16[768,768]{1,0:T(8,128)(2,1)S(1)} collective-permute-done((bf16[768,768]{1,0:T(8,128)(2,1)S(1)}, bf16[768,768]{1,0:T(8,128)(2,1)S(1)}, u32[]{:S(2)}, u32[]{:S(2)}) %collective-permute-start.7) | collective-permute-done | bytes 1179680 | tf_op jit(solution)/shard_map/ppermute | solution.py:538
  33.0 3.1 %local_feats.1 = (bf16[3,256,1024]{2,1,0:T(8,128)(2,1)}, bf16[3,256,1024]{2,1,0:T(8,128)(2,1)}) custom-call(bf16[32,768]{1,0:T(8,128)(2,1)} %get-tuple-element.138.pick_q.refs_0_, bf16[96,768]{1,0:T(8,128)(2,1)} %get-tuple-element.98.pack.refs_0_), custom_call_target="tpu_custom_call" | custom-call | flops 3000000000 | bytes 100000 | tf_op jit(solution)/shard_map/local_feats/pallas_call | solution.py:164
  36.1 2.8 collective-permute-start.13
  41.7 8.5 %attend.1 = (bf16[256,192]{1,0:T(8,128)(2,1)}, bf16[128,192]{1,0:T(8,128)(2,1)}, bf16[128,192]{1,0:T(8,128)(2,1)}, f32[256,192]{1,0:T(8,128)}, f32[256,192]{1,0:T(8,128)}) custom-call(s32[2]{0:T(128)} %lengths.5, s32[1]{0:T(128)} %bitcast.place, s32[1]{0:T(128)} %bitcast.1.slot.chunk, bf16[3,256,1024]{2,1,0:T(8,128)(2,1)} %get-tuple-element.99.feat_q, ...), custom_call_target="tpu_custom_call" | custom-call | flops 8999999488 | bytes 100000 | tf_op jit(solution)/shard_map/attend/pallas_call | solution.py:164
  50.2 8.4 %collective-permute-done.9.refs_9_ = f32[768]{0:T(1024)S(1)} collective-permute-done((f32[768]{0:T(1024)S(1)}, f32[768]{0:T(1024)S(1)}, u32[]{:S(2)}, u32[]{:S(2)}) %collective-permute-start.9) | collective-permute-done | bytes 3104 | tf_op jit(solution)/shard_map/ppermute | solution.py:538
  63.6 6.6 %collective-permute-done.10.refs_11_ = bf16[128,192]{1,0:T(8,128)(2,1)S(1)} collective-permute-done((bf16[128,192]{1,0:T(8,128)(2,1)}, bf16[128,192]{1,0:T(8,128)(2,1)S(1)}, u32[]{:S(2)}, u32[]{:S(2)}) %collective-permute-start.10) | collective-permute-done | bytes 49184 | tf_op jit(solution)/shard_map/ppermute | solution.py:538
  71.9 5.7 %feed.1 = (f32[64,768]{1,0:T(8,128)}, f32[64,768]{1,0:T(8,128)}, f32[64,128]{1,0:T(8,128)}, bf16[128,768]{1,0:T(8,128)(2,1)}, f32[128,1536]{1,0:T(8,128)}, /*index=5*/f32[64,768]{1,0:T(8,128)}, bf16[64,768]{1,0:T(8,128)(2,1)}) custom-call(s32[1]{0:T(128)} %bitcast.place, s32[1]{0:T(128)} %bitcast.1.slot.chunk, bf16[256,768]{1,0:T(8,128)(2,1)} %refs_16_, ...), custom_call_target="tpu_custom_call" | custom-call | flops 5000000000 | bytes 100000 | tf_op jit(solution)/shard_map/feed/pallas_call | solution.py:164
  77.6 3.5 %collective-permute-start.17 = (bf16[64,768]{1,0:T(8,128)(2,1)}, bf16[64,768]{1,0:T(8,128)(2,1)S(1)}, u32[]{:S(2)}, u32[]{:S(2)}) collective-permute-start(bf16[64,768]{1,0:T(8,128)(2,1)} %get-tuple-element.108), channel_id=1, source_target_pairs={{0,2},{1,3},{2,0},{3,1},{4,6},{5,7},{6,4},{7,5},{8,10},{9,11},{10,... | collective-permute-start | bytes 294920 | tf_op jit(solution)/shard_map/ppermute | solution.py:538
  81.1 5.3 %collective-permute-done.17.got = bf16[64,768]{1,0:T(8,128)(2,1)S(1)} collective-permute-done((bf16[64,768]{1,0:T(8,128)(2,1)}, bf16[64,768]{1,0:T(8,128)(2,1)S(1)}, u32[]{:S(2)}, u32[]{:S(2)}) %collective-permute-start.17) | collective-permute-done | bytes 98336 | tf_op jit(solution)/shard_map/ppermute | solution.py:538
  90.1 6.0 %collective-permute-done.18.low_got = bf16[64,768]{1,0:T(8,128)(2,1)S(1)} collective-permute-done((bf16[64,768]{1,0:T(8,128)(2,1)}, bf16[64,768]{1,0:T(8,128)(2,1)S(1)}, u32[]{:S(2)}, u32[]{:S(2)}) %collective-permute-start.18) | collective-permute-done | bytes 98336 | tf_op jit(solution)/shard_map/ppermute | solution.py:538
  96.7 5.3 %feed_back.1 = (bf16[128,768]{1,0:T(8,128)(2,1)}, f32[64,768]{1,0:T(8,128)}, bf16[64,768]{1,0:T(8,128)(2,1)}) custom-call(s32[1]{0:T(128)} %bitcast.place, s32[1]{0:T(128)} %bitcast.1.slot.chunk, f32[128,1536]{1,0:T(8,128)} %get-tuple-element.105.slope, bf16[768,768]{1,0:T(8,128)(2,1)} %up.3, bf16[768,768]{1,0:T(8,128)(2,1)} %down.3, ...), custom_call_target="tpu_custom_call" | custom-call | flops 4000000000 | bytes 100000 | tf_op jit(solution)/shard_map/feed_back/pallas_call | solution.py:164
  105.6 2.7 collective-permute-done.20.got
  109.0 2.8 first_norm_back.1
  120.5 2.5 split.1
  126.8 3.0 %collective-permute-start.25 = (bf16[80,768]{1,0:T(8,128)(2,1)S(1)}, bf16[80,768]{1,0:T(8,128)(2,1)S(1)}, u32[]{:S(2)}, u32[]{:S(2)}) collective-permute-start(bf16[80,768]{1,0:T(8,128)(2,1)S(1)} %copy-done.48), channel_id=1, source_target_pairs={{0,1},{1,0},{2,3},{3,2},{4,5},{5,4},{6,7},{7,6},{8,9},{9,8},{10,11... | collective-permute-start | bytes 368648 | tf_op jit(solution)/shard_map/ppermute | solution.py:538
  129.8 5.2 %feed_grads.1 = (bf16[768,768]{1,0:T(8,128)(2,1)}, bf16[768,768]{1,0:T(8,128)(2,1)}, f32[8,768]{1,0:T(8,128)}) custom-call(s32[1]{0:T(128)} %bitcast.place, s32[1]{0:T(128)} %bitcast.1.slot.chunk, bf16[128,768]{1,0:T(8,128)(2,1)} %get-tuple-element.104.low_mine, bf16[128,768]{1,0:T(8,128)(2,1)} %copy-done.30, bf16[128,768]{1,0:T(8,128)(2,1)} %get-tuple-element.110.down_mine, ...), custom_call_target="tpu_custom_call" | custom-call | flops 6000000000 | bytes 100000 | tf_op jit(solution)/shard_map/feed_grads/pallas_call | solution.py:164
  135.2 8.6 %collective-permute-done.67.refs_20_ = bf16[256,768]{1,0:T(8,128)(2,1)S(1)} collective-permute-done((bf16[256,768]{1,0:T(8,128)(2,1)S(1)}, bf16[256,768]{1,0:T(8,128)(2,1)S(1)}, u32[]{:S(2)}, u32[]{:S(2)}) %collective-permute-start.67) | collective-permute-done | bytes 393248 | tf_op jit(solution)/shard_map/ppermute | solution.py:538
  152.0 5.5 %collective-permute-done.27.refs_5_ = bf16[80,768]{1,0:T(8,128)(2,1)S(1)} collective-permute-done((bf16[80,768]{1,0:T(8,128)(2,1)}, bf16[80,768]{1,0:T(8,128)(2,1)S(1)}, u32[]{:S(2)}, u32[]{:S(2)}) %collective-permute-start.27) | collective-permute-done | bytes 122912 | tf_op jit(solution)/shard_map/ppermute | solution.py:538
  158.6 9.6 %query_back.1 = (bf16[192,256]{1,0:T(8,128)(2,1)}, f32[256,768]{1,0:T(8,128)}, f32[8,512]{1,0:T(8,128)}) custom-call(s32[2]{0:T(128)} %lengths.5, s32[1]{0:T(128)} %bitcast.place, bf16[256,256]{1,0:T(8,128)(2,1)} %get-tuple-element.123.grads.refs_8_, f32[8,256]{1,0:T(8,128)} %get-tuple-element.124.row_totals, ...), custom_call_target="tpu_custom_call" | custom-call | flops 8999999488 | bytes 100000 | tf_op jit(solution)/shard_map/query_back/pallas_call | solution.py:164
  168.3 2.6 mixer_grads.1
  171.0 3.9 %collective-permute-start.50 = (bf16[192,256]{1,0:T(8,128)(2,1)S(1)}, bf16[192,256]{1,0:T(8,128)(2,1)S(1)}, u32[]{:S(2)}, u32[]{:S(2)}) collective-permute-start(bf16[192,256]{1,0:T(8,128)(2,1)S(1)} %copy-done.53), channel_id=1, source_target_pairs={{0,4},{4,0},{8,12},{12,8},{16,20},{20,16},{24,28},{28,24},{1,5},{5... | collective-permute-start | bytes 294920 | tf_op jit(solution)/shard_map/ppermute | solution.py:538
  176.0 3.3 %halve.3 = (bf16[192,768]{1,0:T(8,128)(2,1)}, bf16[192,768]{1,0:T(8,128)(2,1)}, bf16[192,768]{1,0:T(8,128)(2,1)}, bf16[192,768]{1,0:T(8,128)(2,1)}) custom-call(s32[1]{0:T(128)} %bitcast.place, bf16[768,768]{1,0:T(8,128)(2,1)} %get-tuple-element.163.mine, bf16[768,768]{1,0:T(8,128)(2,1)} %copy-done.6), custom_call_target="tpu_custom_call" | custom-call | flops 2000000000 | bytes 100000 | tf_op jit(solution)/shard_map/halve/pallas_call | solution.py:164
  180.4 3.1 %collective-permute-start.82 = (bf16[192,768]{1,0:T(8,128)(2,1)}, bf16[192,768]{1,0:T(8,128)(2,1)S(1)}, u32[]{:S(2)}, u32[]{:S(2)}) collective-permute-start(bf16[192,768]{1,0:T(8,128)(2,1)} %get-tuple-element.168), channel_id=1, source_target_pairs={{0,24},{4,28},{8,16},{12,20},{16,8},{20,12},{24,0},{28,4},{1,25},{... | collective-permute-start | bytes 884744 | tf_op jit(solution)/shard_map/ppermute | solution.py:538
  187.9 12.7 %collective-permute-done.40.refs_12_ = bf16[256,256]{1,0:T(8,128)(2,1)S(1)} collective-permute-done((bf16[256,256]{1,0:T(8,128)(2,1)}, bf16[256,256]{1,0:T(8,128)(2,1)S(1)}, u32[]{:S(2)}, u32[]{:S(2)}) %collective-permute-start.40) | collective-permute-done | bytes 131104 | tf_op jit(solution)/shard_map/ppermute | solution.py:538
  211.3 14.4 %key_back.1 = (bf16[384,256]{1,0:T(8,128)(2,1)}, bf16[64,768]{1,0:T(8,128)(2,1)}, bf16[64,768]{1,0:T(8,128)(2,1)}, bf16[64,768]{1,0:T(8,128)(2,1)}, bf16[64,768]{1,0:T(8,128)(2,1)}) custom-call(s32[2]{0:T(128)} %lengths.5, s32[1]{0:T(128)} %bitcast.place, s32[1]{0:T(128)} %bitcast.1.slot.chunk, bf16[3,256,1024]{2,1,0:T(8,128)(2,1)} %get-tuple-element.134.feat_k, ...), custom_call_target="tpu_custom_call" | custom-call | flops 15000000512 | bytes 100000 | tf_op jit(solution)/shard_map/key_back/pallas_call | solution.py:164
  233.6 3.9 %collective-permute-start.52 = (bf16[192,256]{1,0:T(8,128)(2,1)S(1)}, bf16[192,256]{1,0:T(8,128)(2,1)S(1)}, u32[]{:S(2)}, u32[]{:S(2)}) collective-permute-start(bf16[192,256]{1,0:T(8,128)(2,1)S(1)} %collective-permute-done.51.refs_2_), channel_id=1, source_target_pairs={{0,4},{4,0},{8,12},{12,8},{16,20},{20,16},{24,28},{28,24},{1,5},{5... | collective-permute-start | bytes 294920 | tf_op jit(solution)/shard_map/ppermute | solution.py:538
  263.1 3.0 %collective-permute-done.58.refs_10_ = bf16[384,256]{1,0:T(8,128)(2,1)S(1)} collective-permute-done((bf16[384,256]{1,0:T(8,128)(2,1)S(1)}, bf16[384,256]{1,0:T(8,128)(2,1)S(1)}, u32[]{:S(2)}, u32[]{:S(2)}) %collective-permute-start.58) | collective-permute-done | bytes 196640 | tf_op jit(solution)/shard_map/ppermute | solution.py:538
  266.1 4.3 %collective-permute-done.60.refs_12_ = bf16[384,256]{1,0:T(8,128)(2,1)S(1)} collective-permute-done((bf16[384,256]{1,0:T(8,128)(2,1)S(1)}, bf16[384,256]{1,0:T(8,128)(2,1)S(1)}, u32[]{:S(2)}, u32[]{:S(2)}) %collective-permute-start.60) | collective-permute-done | bytes 196640 | tf_op jit(solution)/shard_map/ppermute | solution.py:538
  276.4 6.0 %weight_grads.1 = (f32[192,768]{1,0:T(8,128)}, f32[192,768]{1,0:T(8,128)}, f32[192,768]{1,0:T(8,128)}, f32[192]{0:T(256)}, f32[192]{0:T(256)}, /*index=5*/f32[192]{0:T(256)}) custom-call(bf16[192,256]{1,0:T(8,128)(2,1)} %get-tuple-element.143.refs_0_, bf16[192,256]{1,0:T(8,128)(2,1)} %copy-done.55, bf16[192,256]{1,0:T(8,128)(2,1)} %copy-done.56, ...), custom_call_target="tpu_custom_call" | custom-call | flops 4000000000 | bytes 100000 | tf_op jit(solution)/shard_map/weight_grads/pallas_call | solution.py:164
  283.5 4.1 %finish_feed.1 = (f32[768,768]{1,0:T(8,128)}, f32[768,768]{1,0:T(8,128)}) custom-call(s32[1]{0:T(128)} %bitcast.place, bf16[768,768]{1,0:T(8,128)(2,1)} %join.3.mine, bf16[768,768]{1,0:T(8,128)(2,1)} %copy-done.5), custom_call_target="tpu_custom_call" | custom-call | flops 4000000000 | bytes 100000 | tf_op jit(solution)/shard_map/finish_feed/pallas_call | solution.py:164
  (370 shorter events, 104.9 us)
Async XLA Ops:
  2.1 29.1 %collective-permute-start.7 = (bf16[768,768]{1,0:T(8,128)(2,1)S(1)}, bf16[768,768]{1,0:T(8,128)(2,1)S(1)}, u32[]{:S(2)}, u32[]{:S(2)}) collective-permute-start(bf16[768,768]{1,0:T(8,128)(2,1)S(1)} %broadcast_select_fusion), channel_id=1, source_target_pairs={{0,1},{1,0},{2,3},{3,2},{4,5},{5,4},{6,7},{7,6},{8,9},{9,8},{10,11... | collective-permute-start | bytes 3538952 | tf_op jit(solution)/shard_map/ppermute | solution.py:538
  9.2 23.2 %collective-permute-start.1 = (bf16[96,768]{1,0:T(8,128)(2,1)}, bf16[96,768]{1,0:T(8,128)(2,1)S(1)}, u32[]{:S(2)}, u32[]{:S(2)}) collective-permute-start(bf16[96,768]{1,0:T(8,128)(2,1)} %get-tuple-element.98.pack.refs_0_), channel_id=1, source_target_pairs={{0,8},{4,12},{8,0},{12,4},{16,24},{20,28},{24,16},{28,20},{1,9},{5... | collective-permute-start | bytes 442376 | tf_op jit(solution)/shard_map/ppermute | solution.py:538
  10.6 21.7 %collective-permute-start.3 = (bf16[96,768]{1,0:T(8,128)(2,1)}, bf16[96,768]{1,0:T(8,128)(2,1)S(1)}, u32[]{:S(2)}, u32[]{:S(2)}) collective-permute-start(bf16[96,768]{1,0:T(8,128)(2,1)} %get-tuple-element.98.pack.refs_0_), channel_id=1, source_target_pairs={{0,16},{4,20},{8,24},{12,28},{16,0},{20,4},{24,8},{28,12},{1,17},{... | collective-permute-start | bytes 442376 | tf_op jit(solution)/shard_map/ppermute | solution.py:538
  12.2 20.7 %collective-permute-start.5 = (bf16[96,768]{1,0:T(8,128)(2,1)}, bf16[96,768]{1,0:T(8,128)(2,1)}, u32[]{:S(2)}, u32[]{:S(2)}) collective-permute-start(bf16[96,768]{1,0:T(8,128)(2,1)} %get-tuple-element.98.pack.refs_0_), channel_id=1, source_target_pairs={{0,24},{4,28},{8,16},{12,20},{16,8},{20,12},{24,0},{28,4},{1,25},{... | collective-permute-start | bytes 442376 | tf_op jit(solution)/shard_map/ppermute | solution.py:538
  31.2 39.1 %collective-permute-start.8 = (bf16[768,768]{1,0:T(8,128)(2,1)S(1)}, bf16[768,768]{1,0:T(8,128)(2,1)S(1)}, u32[]{:S(2)}, u32[]{:S(2)}) collective-permute-start(bf16[768,768]{1,0:T(8,128)(2,1)S(1)} %collective-permute-done.7.refs_7_.got), channel_id=1, source_target_pairs={{0,4},{4,0},{8,12},{12,8},{16,20},{20,16},{24,28},{28,24},{1,5},{5... | collective-permute-start | bytes 3538952 | tf_op jit(solution)/shard_map/ppermute | solution.py:538
  36.1 24.9 %collective-permute-start.13 = (bf16[192,768]{1,0:T(8,128)(2,1)S(1)}, bf16[192,768]{1,0:T(8,128)(2,1)S(1)}, u32[]{:S(2)}, u32[]{:S(2)}) collective-permute-start(bf16[192,768]{1,0:T(8,128)(2,1)S(1)} %copy-done.14), channel_id=1, source_target_pairs={{0,2},{1,3},{2,0},{3,1},{4,6},{5,7},{6,4},{7,5},{8,10},{9,11},{10,... | collective-permute-start | bytes 884744 | tf_op jit(solution)/shard_map/ppermute | solution.py:538
  39.0 22.2 %collective-permute-start.14 = (bf16[192,768]{1,0:T(8,128)(2,1)S(1)}, bf16[192,768]{1,0:T(8,128)(2,1)S(1)}, u32[]{:S(2)}, u32[]{:S(2)}) collective-permute-start(bf16[192,768]{1,0:T(8,128)(2,1)S(1)} %copy-done.14), channel_id=1, source_target_pairs={{0,1},{1,0},{2,3},{3,2},{4,5},{5,4},{6,7},{7,6},{8,9},{9,8},{10,11... | collective-permute-start | bytes 884744 | tf_op jit(solution)/shard_map/ppermute | solution.py:538
  40.6 23.0 %collective-permute-start.15 = (bf16[192,768]{1,0:T(8,128)(2,1)S(1)}, bf16[192,768]{1,0:T(8,128)(2,1)S(1)}, u32[]{:S(2)}, u32[]{:S(2)}) collective-permute-start(bf16[192,768]{1,0:T(8,128)(2,1)S(1)} %copy-done.14), channel_id=1, source_target_pairs={{0,3},{1,2},{2,1},{3,0},{4,7},{5,6},{6,5},{7,4},{8,11},{9,10},{10,... | collective-permute-start | bytes 884744 | tf_op jit(solution)/shard_map/ppermute | solution.py:538
  41.0 17.6 %collective-permute-start.9 = (f32[768]{0:T(1024)S(1)}, f32[768]{0:T(1024)S(1)}, u32[]{:S(2)}, u32[]{:S(2)}) collective-permute-start(f32[768]{0:T(1024)S(1)} %copy-done.97), channel_id=1, source_target_pairs={{0,1},{1,0},{2,3},{3,2},{4,5},{5,4},{6,7},{7,6},{8,9},{9,8},{10,11... | collective-permute-start | bytes 9224 | tf_op jit(solution)/shard_map/ppermute | solution.py:538
  103.6 12.5 %collective-permute-start.33 = (bf16[32,768]{1,0:T(8,128)(2,1)S(1)}, bf16[32,768]{1,0:T(8,128)(2,1)S(1)}, u32[]{:S(2)}, u32[]{:S(2)}) collective-permute-start(bf16[32,768]{1,0:T(8,128)(2,1)S(1)} %copy-done.77), channel_id=1, source_target_pairs={{0,16},{4,20},{8,24},{12,28},{16,0},{20,4},{24,8},{28,12},{1,17},{... | collective-permute-start | bytes 147464 | tf_op jit(solution)/shard_map/ppermute | solution.py:538
  124.7 19.1 %collective-permute-start.67 = (bf16[256,768]{1,0:T(8,128)(2,1)S(1)}, bf16[256,768]{1,0:T(8,128)(2,1)S(1)}, u32[]{:S(2)}, u32[]{:S(2)}) collective-permute-start(bf16[256,768]{1,0:T(8,128)(2,1)S(1)} %copy-done.7), channel_id=1, source_target_pairs={{0,16},{4,20},{8,24},{12,28},{16,0},{20,4},{24,8},{28,12},{1,17},{... | collective-permute-start | bytes 1179656 | tf_op jit(solution)/shard_map/ppermute | solution.py:538
  126.2 20.1 %collective-permute-start.69 = (bf16[256,768]{1,0:T(8,128)(2,1)S(1)}, bf16[256,768]{1,0:T(8,128)(2,1)S(1)}, u32[]{:S(2)}, u32[]{:S(2)}) collective-permute-start(bf16[256,768]{1,0:T(8,128)(2,1)S(1)} %copy-done.7), channel_id=1, source_target_pairs={{0,24},{4,28},{8,16},{12,20},{16,8},{20,12},{24,0},{28,4},{1,25},{... | collective-permute-start | bytes 1179656 | tf_op jit(solution)/shard_map/ppermute | solution.py:538
  126.7 19.6 %collective-permute-start.24 = (bf16[80,768]{1,0:T(8,128)(2,1)S(1)}, bf16[80,768]{1,0:T(8,128)(2,1)S(1)}, u32[]{:S(2)}, u32[]{:S(2)}) collective-permute-start(bf16[80,768]{1,0:T(8,128)(2,1)S(1)} %copy-done.48), channel_id=1, source_target_pairs={{0,2},{1,3},{2,0},{3,1},{4,6},{5,7},{6,4},{7,5},{8,10},{9,11},{10,... | collective-permute-start | bytes 368648 | tf_op jit(solution)/shard_map/ppermute | solution.py:538
  126.8 21.4 %collective-permute-start.25 = (bf16[80,768]{1,0:T(8,128)(2,1)S(1)}, bf16[80,768]{1,0:T(8,128)(2,1)S(1)}, u32[]{:S(2)}, u32[]{:S(2)}) collective-permute-start(bf16[80,768]{1,0:T(8,128)(2,1)S(1)} %copy-done.48), channel_id=1, source_target_pairs={{0,1},{1,0},{2,3},{3,2},{4,5},{5,4},{6,7},{7,6},{8,9},{9,8},{10,11... | collective-permute-start | bytes 368648 | tf_op jit(solution)/shard_map/ppermute | solution.py:538
  135.2 39.7 %collective-permute-start.79 = (bf16[768,768]{1,0:T(8,128)(2,1)}, bf16[768,768]{1,0:T(8,128)(2,1)S(1)}, u32[]{:S(2)}, u32[]{:S(2)}) collective-permute-start(bf16[768,768]{1,0:T(8,128)(2,1)} %get-tuple-element.164), channel_id=1, source_target_pairs={{0,4},{4,0},{8,12},{12,8},{16,20},{20,16},{24,28},{28,24},{1,5},{5... | collective-permute-start | bytes 3538952 | tf_op jit(solution)/shard_map/ppermute | solution.py:538
  152.0 18.8 %collective-permute-start.64 = (bf16[256,768]{1,0:T(8,128)(2,1)S(1)}, bf16[256,768]{1,0:T(8,128)(2,1)S(1)}, u32[]{:S(2)}, u32[]{:S(2)}) collective-permute-start(bf16[256,768]{1,0:T(8,128)(2,1)S(1)} %copy-done.7), channel_id=1, source_target_pairs={{0,4},{4,0},{8,12},{12,8},{16,20},{20,16},{24,28},{28,24},{1,5},{5... | collective-permute-start | bytes 1179656 | tf_op jit(solution)/shard_map/ppermute | solution.py:538
  157.5 13.5 %collective-permute-start.66 = (bf16[256,768]{1,0:T(8,128)(2,1)S(1)}, bf16[256,768]{1,0:T(8,128)(2,1)S(1)}, u32[]{:S(2)}, u32[]{:S(2)}) collective-permute-start(bf16[256,768]{1,0:T(8,128)(2,1)S(1)} %collective-permute-done.65.refs_18_), channel_id=1, source_target_pairs={{0,4},{4,0},{8,12},{12,8},{16,20},{20,16},{24,28},{28,24},{1,5},{5... | collective-permute-start | bytes 1179656 | tf_op jit(solution)/shard_map/ppermute | solution.py:538
  158.1 21.2 %collective-permute-start.68 = (bf16[256,768]{1,0:T(8,128)(2,1)S(1)}, bf16[256,768]{1,0:T(8,128)(2,1)S(1)}, u32[]{:S(2)}, u32[]{:S(2)}) collective-permute-start(bf16[256,768]{1,0:T(8,128)(2,1)S(1)} %collective-permute-done.67.refs_20_), channel_id=1, source_target_pairs={{0,4},{4,0},{8,12},{12,8},{16,20},{20,16},{24,28},{28,24},{1,5},{5... | collective-permute-start | bytes 1179656 | tf_op jit(solution)/shard_map/ppermute | solution.py:538
  158.1 21.5 %collective-permute-start.70 = (bf16[256,768]{1,0:T(8,128)(2,1)S(1)}, bf16[256,768]{1,0:T(8,128)(2,1)}, u32[]{:S(2)}, u32[]{:S(2)}) collective-permute-start(bf16[256,768]{1,0:T(8,128)(2,1)S(1)} %collective-permute-done.69.refs_22_), channel_id=1, source_target_pairs={{0,4},{4,0},{8,12},{12,8},{16,20},{20,16},{24,28},{28,24},{1,5},{5... | collective-permute-start | bytes 1179656 | tf_op jit(solution)/shard_map/ppermute | solution.py:538
  170.9 13.4 %collective-permute-start.38 = (bf16[256,256]{1,0:T(8,128)(2,1)}, bf16[256,256]{1,0:T(8,128)(2,1)}, u32[]{:S(2)}, u32[]{:S(2)}) collective-permute-start(bf16[256,256]{1,0:T(8,128)(2,1)} %get-tuple-element.123.grads.refs_8_), channel_id=1, source_target_pairs={{0,8},{4,12},{8,0},{12,4},{16,24},{20,28},{24,16},{28,20},{1,9},{5... | collective-permute-start | bytes 393224 | tf_op jit(solution)/shard_map/ppermute | solution.py:538
  179.3 21.8 %collective-permute-start.80 = (bf16[192,768]{1,0:T(8,128)(2,1)}, bf16[192,768]{1,0:T(8,128)(2,1)S(1)}, u32[]{:S(2)}, u32[]{:S(2)}) collective-permute-start(bf16[192,768]{1,0:T(8,128)(2,1)} %get-tuple-element.166), channel_id=1, source_target_pairs={{0,8},{4,12},{8,0},{12,4},{16,24},{20,28},{24,16},{28,20},{1,9},{5... | collective-permute-start | bytes 884744 | tf_op jit(solution)/shard_map/ppermute | solution.py:538
  179.7 21.5 %collective-permute-start.81 = (bf16[192,768]{1,0:T(8,128)(2,1)}, bf16[192,768]{1,0:T(8,128)(2,1)S(1)}, u32[]{:S(2)}, u32[]{:S(2)}) collective-permute-start(bf16[192,768]{1,0:T(8,128)(2,1)} %get-tuple-element.167), channel_id=1, source_target_pairs={{0,16},{4,20},{8,24},{12,28},{16,0},{20,4},{24,8},{28,12},{1,17},{... | collective-permute-start | bytes 884744 | tf_op jit(solution)/shard_map/ppermute | solution.py:538
  180.4 21.2 %collective-permute-start.82 = (bf16[192,768]{1,0:T(8,128)(2,1)}, bf16[192,768]{1,0:T(8,128)(2,1)S(1)}, u32[]{:S(2)}, u32[]{:S(2)}) collective-permute-start(bf16[192,768]{1,0:T(8,128)(2,1)} %get-tuple-element.168), channel_id=1, source_target_pairs={{0,24},{4,28},{8,16},{12,20},{16,8},{20,12},{24,0},{28,4},{1,25},{... | collective-permute-start | bytes 884744 | tf_op jit(solution)/shard_map/ppermute | solution.py:538
  184.3 16.3 %collective-permute-start.40 = (bf16[256,256]{1,0:T(8,128)(2,1)}, bf16[256,256]{1,0:T(8,128)(2,1)S(1)}, u32[]{:S(2)}, u32[]{:S(2)}) collective-permute-start(bf16[256,256]{1,0:T(8,128)(2,1)} %get-tuple-element.123.grads.refs_8_), channel_id=1, source_target_pairs={{0,16},{4,20},{8,24},{12,28},{16,0},{20,4},{24,8},{28,12},{1,17},{... | collective-permute-start | bytes 393224 | tf_op jit(solution)/shard_map/ppermute | solution.py:538
  184.3 16.3 %collective-permute-start.42 = (bf16[256,256]{1,0:T(8,128)(2,1)}, bf16[256,256]{1,0:T(8,128)(2,1)S(1)}, u32[]{:S(2)}, u32[]{:S(2)}) collective-permute-start(bf16[256,256]{1,0:T(8,128)(2,1)} %get-tuple-element.123.grads.refs_8_), channel_id=1, source_target_pairs={{0,24},{4,28},{8,16},{12,20},{16,8},{20,12},{24,0},{28,4},{1,25},{... | collective-permute-start | bytes 393224 | tf_op jit(solution)/shard_map/ppermute | solution.py:538
  205.5 20.2 %collective-permute-start.73 = (bf16[32,768]{1,0:T(8,128)(2,1)S(1)}, bf16[32,768]{1,0:T(8,128)(2,1)S(1)}, u32[]{:S(2)}, u32[]{:S(2)}) collective-permute-start(bf16[32,768]{1,0:T(8,128)(2,1)S(1)} %copy-done.86), channel_id=1, source_target_pairs={{0,16},{4,20},{8,24},{12,28},{16,0},{20,4},{24,8},{28,12},{1,17},{... | collective-permute-start | bytes 147464 | tf_op jit(solution)/shard_map/ppermute | solution.py:538
  205.9 21.3 %collective-permute-start.74 = (bf16[32,768]{1,0:T(8,128)(2,1)S(1)}, bf16[32,768]{1,0:T(8,128)(2,1)S(1)}, u32[]{:S(2)}, u32[]{:S(2)}) collective-permute-start(bf16[32,768]{1,0:T(8,128)(2,1)S(1)} %copy-done.85), channel_id=1, source_target_pairs={{0,24},{4,28},{8,16},{12,20},{16,8},{20,12},{24,0},{28,4},{1,25},{... | collective-permute-start | bytes 147464 | tf_op jit(solution)/shard_map/ppermute | solution.py:538
  207.8 29.7 %collective-permute-start.83 = (bf16[192,768]{1,0:T(8,128)(2,1)}, bf16[192,768]{1,0:T(8,128)(2,1)S(1)}, u32[]{:S(2)}, u32[]{:S(2)}) collective-permute-start(bf16[192,768]{1,0:T(8,128)(2,1)} %settle.3.refs_0_), channel_id=1, source_target_pairs={{0,8},{4,12},{8,0},{12,4},{16,24},{20,28},{24,16},{28,20},{1,9},{5... | collective-permute-start | bytes 884744 | tf_op jit(solution)/shard_map/ppermute | solution.py:538
  209.1 30.3 %collective-permute-start.84 = (bf16[192,768]{1,0:T(8,128)(2,1)}, bf16[192,768]{1,0:T(8,128)(2,1)S(1)}, u32[]{:S(2)}, u32[]{:S(2)}) collective-permute-start(bf16[192,768]{1,0:T(8,128)(2,1)} %settle.3.refs_0_), channel_id=1, source_target_pairs={{0,16},{4,20},{8,24},{12,28},{16,0},{20,4},{24,8},{28,12},{1,17},{... | collective-permute-start | bytes 884744 | tf_op jit(solution)/shard_map/ppermute | solution.py:538
  209.4 30.7 %collective-permute-start.85 = (bf16[192,768]{1,0:T(8,128)(2,1)}, bf16[192,768]{1,0:T(8,128)(2,1)S(1)}, u32[]{:S(2)}, u32[]{:S(2)}) collective-permute-start(bf16[192,768]{1,0:T(8,128)(2,1)} %settle.3.refs_0_), channel_id=1, source_target_pairs={{0,24},{4,28},{8,16},{12,20},{16,8},{20,12},{24,0},{28,4},{1,25},{... | collective-permute-start | bytes 884744 | tf_op jit(solution)/shard_map/ppermute | solution.py:538
  231.1 13.4 %collective-permute-start.55 = (bf16[192,256]{1,0:T(8,128)(2,1)S(1)}, bf16[192,256]{1,0:T(8,128)(2,1)S(1)}, u32[]{:S(2)}, u32[]{:S(2)}) collective-permute-start(bf16[192,256]{1,0:T(8,128)(2,1)S(1)} %copy-done.54), channel_id=1, source_target_pairs={{0,24},{4,28},{8,16},{12,20},{16,8},{20,12},{24,0},{28,4},{1,25},{... | collective-permute-start | bytes 294920 | tf_op jit(solution)/shard_map/ppermute | solution.py:538
  248.8 33.7 %collective-permute-start.86 = (bf16[768,768]{1,0:T(8,128)(2,1)}, bf16[768,768]{1,0:T(8,128)(2,1)S(1)}, u32[]{:S(2)}, u32[]{:S(2)}) collective-permute-start(bf16[768,768]{1,0:T(8,128)(2,1)} %join.3.mine), channel_id=1, source_target_pairs={{0,4},{4,0},{8,12},{12,8},{16,20},{20,16},{24,28},{28,24},{1,5},{5... | collective-permute-start | bytes 3538952 | tf_op jit(solution)/shard_map/ppermute | solution.py:538
  (154 other events, 1033.9 us)

commit v3 on v2

--- a/solution.py
+++ b/solution.py
@@ -25,6 +25,7 @@
 BF16 = jnp.bfloat16
 ROWS = 256
 HEADS = 3
+KEPT = PLANES + HS
 TAP_LANE = 111
 VMEM = pl.BlockSpec(memory_space=pltpu.VMEM)
 SMEM = pl.BlockSpec(memory_space=pltpu.SMEM)
@@ -140,7 +141,7 @@
 
 
 def project_body(
-    tokens, wq, bq, wk, bk, wv, bv, planes, choose, raw_q, raw_k, tan_q, tan_k, pick_q, pack
+    tokens, wq, bq, wk, bk, wv, bv, planes, choose, raw_q, raw_k, tan_q, tan_k, pack
 ):
     x = tokens[...]
 
@@ -155,7 +156,7 @@
     pack[0:PLANES, :] = codes(wk, bk, raw_k, tan_k)
     values = beside(dot_nt(wv[...], x) + column(bv[...].reshape(1, -1)))
     pack[PLANES : PLANES + HS, :] = values.astype(BF16)
-    pick_q[...] = codes(wq, bq, raw_q, tan_q)
+    pack[KEPT:, :] = codes(wq, bq, raw_q, tan_q)
 
 
 def call(body, name, out_shape, ins, smem=0, scratch=(), us=2):
@@ -194,31 +195,27 @@
             f32(HS, wide),
             f32(PLANES, wide),
             f32(PLANES, wide),
-            bf16(PLANES, wide),
-            bf16(PLANES + HS, wide),
+            bf16(KEPT + PLANES, wide),
         ),
         ins,
-        us=3,
-    )
-
-
-def local_feats_body(pick_q, pack, feat_q, feat_k, phi):
-    for src, dst in ((pick_q, feat_q), (pack, feat_k)):
-        for h in range(HEADS):
-            picks = src[0:PLANES, h * ROWS : (h + 1) * ROWS].astype(F32)
-            expand(picks, phi)
-            dst[h] = phi[...].T
-
-
-def local_feats(pick_q, pack):
-    shape = bf16(HEADS, ROWS, FEATS)
+        us=0.1,
+    )
+
+
+def local_feats_body(row, pack, feat, phi):
+    for h in range(HEADS):
+        picks = pack[row : row + PLANES, h * ROWS : (h + 1) * ROWS].astype(F32)
+        expand(picks, phi)
+        feat[h] = phi[...].T
+
+
+def local_feats(row, pack):
     return call(
-        local_feats_body,
+        functools.partial(local_feats_body, row),
         "local_feats",
-        (shape, shape),
-        (pick_q, pack),
+        bf16(HEADS, ROWS, FEATS),
+        (pack,),
         scratch=(pltpu.VMEM((FEATS, ROWS), BF16),),
-        us=3,
     )
 
 
@@ -255,7 +252,7 @@
     phis = (phi0, phi1, phi2)
     mine = place[0]
     for k in range(n):
-        packs[k] = pack_in[k][...]
+        packs[k] = pack_in[k][0:KEPT, :]
     acc[...] = jnp.zeros_like(acc)
     tot[...] = jnp.zeros_like(tot)
 
@@ -329,13 +326,15 @@
     return unit_grad * scale - raw * (scale * scale * scale) * inner
 
 
-def codes_to_raw(dphi, picks, tan, raw, choose_back, planes_t):
+def codes_to_raw(dphi, pack, row, tan, raw, choose_back, planes_t):
     parts = []
     for h in range(HEADS):
         for u in range(2):
             lane = h * ROWS + u * 128
             parts.append(
-                expand_back(picks[0:PLANES, lane : lane + 128].astype(F32), dphi.at[h], u * 128, 128)
+                expand_back(
+                    pack[row : row + PLANES, lane : lane + 128].astype(F32), dphi.at[h], u * 128, 128
+                )
             )
     pick_grad = jnp.concatenate(parts, axis=1) * (1.0 / HASHES)
     code_grad = dot_exact(choose_back[...], pick_grad)
@@ -343,14 +342,14 @@
 
 
 def query_back_body(
-    n, lengths, place, grads, row_totals, pick_q, tan, raw, choose_back, planes_t, weight, *refs
+    n, lengths, place, grads, row_totals, tan, raw, choose_back, planes_t, weight, *refs
 ):
     pack_in, (grad_out, input_out, taps_out) = refs[:n], refs[n : n + 3]
     packs, phi0, phi1, phi2, dphi = refs[n + 3 :]
     phis = (phi0, phi1, phi2)
     mine = place[0]
     for k in range(n):
-        packs[k] = pack_in[k][...]
+        packs[k] = pack_in[k][0:KEPT, :]
     dphi[...] = jnp.zeros_like(dphi)
 
     def block(k, carry):
@@ -370,7 +369,7 @@
         return carry
 
     lax.fori_loop(0, n, block, 0)
-    raw_grad = codes_to_raw(dphi, pick_q, tan, raw, choose_back, planes_t)
+    raw_grad = codes_to_raw(dphi, pack_in[0], KEPT, tan, raw, choose_back, planes_t)
     turned = stacked(raw_grad).astype(BF16)
     grad_out[...] = turned
     input_out[...] = dot(turned.astype(F32).T.astype(BF16), weight[...])
@@ -416,12 +415,10 @@
 
 def key_back_body(
     n,
-    parts,
     lengths,
     place,
     slot,
     feat_k,
-    pack,
     tan,
     raw,
     taps_back,
@@ -430,16 +427,18 @@
     wk,
     wv,
     query_input,
+    query_turned,
+    dh1,
     *refs,
 ):
-    pick_in, grad_in = refs[:n], refs[n : 2 * n]
-    turned_out = refs[2 * n]
-    input_out = refs[2 * n + 1 : 2 * n + 1 + parts]
-    picks, grads, phi0, phi1, phi2, dphi, acc, inputs = refs[2 * n + 1 + parts :]
+    pack_in, grad_in = refs[:n], refs[n : 2 * n]
+    pack = pack_in[0]
+    turned_out, input_out = refs[2 * n : 2 * n + 2]
+    picks, grads, phi0, phi1, phi2, dphi, acc, inputs = refs[2 * n + 2 :]
     phis = (phi0, phi1, phi2)
     mine = place[0]
     for k in range(n):
-        picks[k] = pick_in[k][...]
+        picks[k] = pack_in[k][KEPT:, :]
         grads[k] = grad_in[k][...]
     dphi[...] = jnp.zeros_like(dphi)
     acc[...] = jnp.zeros_like(acc)
@@ -468,7 +467,7 @@
         return carry
 
     lax.fori_loop(0, n, block, 0)
-    raw_grad = codes_to_raw(dphi, pack, tan, raw, choose_back, planes_t)
+    raw_grad = codes_to_raw(dphi, pack_in[0], 0, tan, raw, choose_back, planes_t)
     key_turned = stacked(raw_grad).astype(BF16)
     key_rows = key_turned.astype(F32).T
 
@@ -485,20 +484,22 @@
         outs.append(acc[h] + split_dot(taps_band, context_grad, dot))
     value_rows = jnp.concatenate(outs, axis=1).astype(BF16)
     wide = HEADS * HS
-    turned_out[0:wide, :] = key_turned
-    turned_out[wide : 2 * wide, :] = value_rows.astype(F32).T.astype(BF16)
-    inputs[...] = (
-        query_input[...] + dot(key_rows.astype(BF16), wk[...]) + dot(value_rows, wv[...])
-    ).astype(BF16)
-    put_chunks(slot[0], inputs, input_out)
-
-
-def key_back(ins, picks, grads, parts):
+    turned_out[0:wide, :] = query_turned[...]
+    turned_out[wide : 2 * wide, :] = key_turned
+    turned_out[2 * wide :, :] = value_rows.astype(F32).T.astype(BF16)
+    inputs[...] = query_input[...] + dot(key_rows.astype(BF16), wk[...]) + dot(value_rows, wv[...])
+    rows = dh1.shape[0]
+    own = pl.ds(pl.multiple_of(slot[0] * rows, 16), rows)
+    inputs[own, :] = inputs[own, :] + dh1[...]
+    input_out[...] = inputs[...].astype(BF16)
+
+
+def key_back(ins, picks, grads):
     n = len(picks)
     return call(
-        functools.partial(key_back_body, n, parts),
+        functools.partial(key_back_body, n),
         "key_back",
-        (bf16(2 * HEADS * HS, ROWS), *[bf16(ROWS // parts, D)] * parts),
+        (bf16(3 * HEADS * HS, ROWS), bf16(ROWS, D)),
         (*ins, *picks, *grads),
         smem=3,
         scratch=(
@@ -509,7 +510,7 @@
             pltpu.VMEM((FEATS, ROWS), BF16),
             pltpu.VMEM((HEADS, FEATS, ROWS), F32),
             pltpu.VMEM((HEADS, ROWS, HS), F32),
-            pltpu.VMEM((ROWS, D), BF16),
+            pltpu.VMEM((ROWS, D), F32),
         ),
         us=15,
     )
@@ -538,14 +539,23 @@
     return lax.ppermute(value, axis, [(i, i ^ k) for i in range(n)])
 
 
+def cross_chips(value):
+    return [value] + [swap(value, "seq", k) for k in range(2, lax.axis_size("seq"), 2)]
+
+
+def from_partner(blocks):
+    got = []
+    for block in blocks:
+        got += [block, swap(block, "seq", 1)]
+    return got
+
+
 def over_seq(value):
-    n = lax.axis_size("seq")
-    got = [value] + [None] * (n - 1)
-    for k in range(2, n, 2):
-        got[k] = swap(value, "seq", k)
-    for k in range(0, n, 2):
-        got[k + 1] = swap(got[k], "seq", 1)
-    return got
+    return from_partner(cross_chips(value))
+
+
+def after(value, then):
+    return lax.optimization_barrier((value, then))
 
 
 HID_ORDER = (0, 2, 1, 3)
@@ -553,6 +563,15 @@
 
 def hid_swap(value, j):
     return swap(value, "hid", HID_ORDER[j])
+
+
+def far_swap(value):
+    chips, parts = lax.axis_size("seq"), lax.axis_size("hid")
+    pairs = []
+    for s in range(chips):
+        flip = HID_ORDER[3] if s % 2 else HID_ORDER[1]
+        pairs += [(s * parts + h, s * parts + (h ^ flip)) for h in range(parts)]
+    return lax.ppermute(value, ("seq", "hid"), pairs)
 
 
 def over_hid(value):
@@ -592,9 +611,57 @@
     return jnp.concatenate([high, sums - high], axis=0).astype(BF16)
 
 
+def bundle_body(place, up, down, mixer, shift, bundle):
+    core = place[0] & 1
+    size, rows = up.shape[0], mixer.shape[0] // 2
+
+    @pl.when(core == 0)
+    def _():
+        bundle[0:size, :] = up[...]
+
+    @pl.when(core == 1)
+    def _():
+        bundle[0:size, :] = down[...]
+
+    mine = mixer[pl.ds(pl.multiple_of(core * rows, 16), rows), :]
+    bundle[size : size + rows, :] = mine
+    left = flat(shift)
+    parts = []
+    for _ in range(3):
+        part = left.astype(BF16).astype(F32)
+        parts.append(part)
+        left = left - part
+    parts.append(jnp.zeros((13, D), F32))
+    bundle[size + rows :, :] = jnp.concatenate(parts, axis=0).astype(BF16)
+
+
+def make_bundle(place, up, down, mixer, shift):
+    rows = mixer.shape[0] // 2
+    return call(
+        bundle_body,
+        "bundle",
+        bf16(up.shape[0] + rows + 16, D),
+        (place, up, down, mixer, shift),
+        smem=1,
+        us=20,
+    )
+
+
 def partner_weights(core, got, other, both):
-    both[core] = got[...]
-    both[1 - core] = other[...]
+    size = both.shape[1]
+    both[core] = got[0:size, :]
+    both[1 - core] = other[0:size, :]
+
+
+def put_mixers(core, size, own, got, other, mine, theirs, mixers):
+    rows = own.shape[0] // 2
+    mixers[0] = own[...]
+    start = pl.multiple_of(core * rows, 16)
+    far = pl.multiple_of((1 - core) * rows, 16)
+    mixers[2, pl.ds(start, rows), :] = got[size : size + rows, :]
+    mixers[2, pl.ds(far, rows), :] = other[size : size + rows, :]
+    mixers[1 + 2 * core] = mine[...]
+    mixers[3 - 2 * core] = theirs[...]
 
 
 def gelu_parts(x):
@@ -611,18 +678,24 @@
 
 
 def feed_body(parts, place, slot, *refs):
-    tokens, mixer_shift, gain, shift, up, up_shift, down, got, other, far_shift = refs[:10]
-    contexts, mixers = refs[10 : 10 + parts], refs[10 + parts : 10 + 2 * parts]
-    first_mine, normed_mine, inverse_mine, low_out, slope_out, keep, send = refs[
-        10 + 2 * parts : 17 + 2 * parts
+    tokens, mixer_shift, gain, shift, up, up_shift, down, got, other, mixer = refs[:10]
+    far_mixer, other_mixer = refs[10:12]
+    contexts = refs[12 : 12 + parts]
+    first_mine, normed_mine, inverse_mine, low_out, slope_out, keep, send, mixers = refs[
+        12 + parts : 20 + parts
     ]
-    first, normed, inverse, partial, both = refs[17 + 2 * parts :]
+    first, normed, inverse, partial, both = refs[20 + parts :]
     half = ROWS // 2
-    partner_weights(place[0] & 1, got, other, both)
+    core = place[0] & 1
+    partner_weights(core, got, other, both)
+    put_mixers(core, both.shape[1], mixer, got, other, far_mixer, other_mixer, mixers)
     mine = tokens[pl.ds(pl.multiple_of((slot[0] >> 1) * half, 16), half), :]
     mixed = flat(mixer_shift) + mine.astype(F32)
-    for c, m in zip(contexts, mixers):
-        mixed = mixed + dot(c[...], m[...])
+    for j, c in enumerate(contexts):
+        mixed = mixed + dot(c[...], mixers[j])
+    base = both.shape[1] + mixer.shape[0] // 2
+    shift_rows = got[base : base + 16, :].astype(F32)
+    far_shift = (shift_rows[0:1] + shift_rows[1:2]) + shift_rows[2:3]
     n1, r1 = norm_stats(mixed)
     rows1 = n1 * flat(gain) + flat(shift)
     first[...] = rows1
@@ -632,7 +705,7 @@
     low_out[...] = low
     hidden, slope = gelu_parts(dot(low, up[...]) + flat(up_shift))
     slope_out[:, 0:D] = slope
-    far_hidden, far_slope = gelu_parts(dot(low, both[0]) + flat(far_shift))
+    far_hidden, far_slope = gelu_parts(dot(low, both[0]) + far_shift)
     slope_out[:, D:] = far_slope
     partial[...] = dot(hidden, down[...]) + dot(far_hidden, both[1])
     quarter = slot[0] & 1
@@ -668,17 +741,16 @@
     keep_and_send(partial, quarter, keep, send)
 
 
-def take_chunks(index, pieces, whole):
+def take_chunks(index, pieces, whole, first=0):
     rows = whole.shape[0] // len(pieces)
     for k, piece in enumerate(pieces):
         start = pl.multiple_of(jnp.bitwise_xor(index, k) * rows, 16)
-        whole[pl.ds(start, rows), :] = piece[0:rows, :]
-
-
-def first_back_body(parts, grad, normed, inverse, gain, keep, got, *refs):
-    mixers = refs[:parts]
-    dh1_out, payload = refs[parts : parts + 2]
-    outs = refs[parts + 2 :]
+        whole[pl.ds(start, rows), :] = piece[first : first + rows, :]
+
+
+def first_back_body(parts, grad, normed, inverse, gain, keep, got, layer, mixers, *refs):
+    dh1_out, payload = refs[:2]
+    outs = refs[2:]
     total = grad[...] + keep[...] + got[...].astype(F32)
     n1 = normed[...]
     dh1 = norm_grad(total, n1, inverse[:, 0:1], flat(gain))
@@ -686,9 +758,10 @@
     low = dh1.astype(BF16)
     rows = dh1.shape[0]
     payload[0:rows, :] = low
-    payload[rows:, :] = two_parts(column_sums(total * n1, total, low.astype(F32)))
-    for m, out in zip(mixers, outs):
-        out[...] = dot_nt(low, m[...]).astype(BF16)
+    payload[rows : 2 * rows + 16, :] = layer[...]
+    payload[2 * rows + 16 :, :] = two_parts(column_sums(total * n1, total, low.astype(F32)))
+    for j, out in enumerate(outs):
+        out[...] = dot_nt(low, mixers[j]).astype(BF16)
 
 
 def split_body(parts, chunk, weighted, total, *refs):
@@ -716,50 +789,59 @@
     row_totals[...] = side.T[64:72, :]
 
 
-def feed_grads_body(place, slot, low_mine, low_got, down_mine, down_got, up, up_shift, down, half_mine, half_other, sums, low_all, down_all, whole):
+def feed_grads_body(place, slot, low_mine, low_got, down_mine, down_got, up, up_shift, down, half_mine, half_other, sums, low_all, down_all):
     take_chunks(slot[0] >> 1, (low_mine, low_got), low_all)
     take_chunks(slot[0] >> 1, (down_mine, down_got), down_all)
     low, grad = low_all[...], down_all[...]
     hidden, slope = gelu_parts(dot(low, up[...]) + flat(up_shift))
     up_low = (dot_nt(grad, down[...]) * slope).astype(BF16)
-    ff = hidden.shape[1]
-    whole[0:ff, :] = dot(hidden.T, grad).astype(BF16)
-    whole[ff:, :] = dot(low.T, up_low).astype(BF16)
-    put_halves(place[0], whole, half_mine, half_other)
+    down_part = dot(hidden.T, grad).astype(BF16)
+    up_part = dot(low.T, up_low).astype(BF16)
+    core = place[0] & 1
+
+    def put(first, second):
+        first[0 : down_part.shape[0], :] = down_part
+        second[0 : up_part.shape[0], :] = up_part
+
+    pl.when(core == 0)(lambda: put(half_mine, half_other))
+    pl.when(core == 1)(lambda: put(half_other, half_mine))
     sums[...] = jnp.broadcast_to(jnp.sum(up_low.astype(F32), axis=0, keepdims=True), sums.shape)
 
 
 def mixer_grads_body(parts, place, slot, context, up_sums, taps, *refs):
-    layers, payloads = refs[:parts], refs[parts : 2 * parts]
-    half_mine, half_other, layer_out, whole, mixed = refs[2 * parts :]
+    payloads = refs[:parts]
+    half_mine, half_other, layer_out, whole, mixed = refs[parts:]
     wide = HEADS * HS
-    take_chunks(slot[0], layers, layer_out)
+    rows = ROWS // parts
+    take_chunks(slot[0], payloads, layer_out, rows)
     take_chunks(slot[0], payloads, mixed)
-    rows = ROWS // parts
-
-    def summed(refs):
+
+    def summed(row):
         total = jnp.zeros((8, D), F32)
-        for r in refs:
-            total = total + r[rows : rows + 8, :].astype(F32) + r[rows + 8 : rows + 16, :].astype(F32)
-        return total
+        for r in payloads:
+            total = total + r[row : row + 8, :].astype(F32) + r[row + 8 : row + 16, :].astype(F32)
+        return total[0:3]
 
     context_t = context[...].astype(F32).T.astype(BF16)
     whole[0:wide, :] = dot(context_t, mixed[...]).astype(BF16)
     tap_block = jnp.concatenate([taps[0:HEADS, :], jnp.zeros((HEADS, D - 512), F32)], axis=1)
     small = jnp.concatenate(
-        [summed(layers)[0:3], summed(payloads)[0:3], up_sums[0:1, :], tap_block, jnp.zeros((6, D), F32)],
+        [summed(2 * rows), summed(2 * rows + 16), up_sums[0:1, :], tap_block, jnp.zeros((6, D), F32)],
         axis=0,
     )
     whole[wide : wide + 16, :] = small.astype(BF16)
     rest = whole.shape[0] - wide - 16
-    whole[wide + 16 :, :] = jnp.zeros((rest, D), BF16)
+    if rest:
+        whole[wide + 16 :, :] = jnp.zeros((rest, D), BF16)
     put_halves(place[0], whole, half_mine, half_other)
 
 
-def halve_body(place, mine, other, *refs):
-    outs, (whole,) = refs[:-1], refs[-1:]
-    whole[...] = (mine[...].astype(F32) + other[...].astype(F32)).astype(BF16)
-    put_chunks(place[0] >> 1, whole, outs)
+def halve_body(place, mine, other, *outs):
+    rows = outs[0].shape[0]
+    for k, out in enumerate(outs):
+        start = pl.multiple_of(jnp.bitwise_xor(place[0] >> 1, k) * rows, 16)
+        at = pl.ds(start, rows)
+        out[...] = (mine[at, :].astype(F32) + other[at, :].astype(F32)).astype(BF16)
 
 
 def settle_body(*refs):
@@ -777,25 +859,42 @@
     return [swap(value, "seq", 2 * k) for k in range(1, n // 2)]
 
 
-def sum_over_seq(mine, other, place, n):
+def scatter_chips(mine, got, place, n):
     chips = n // 2
     half, width = mine.shape
-    piece = bf16(half // chips, width)
-    got = swap(other, "seq", 1)
-    pieces = call(
+    return call(
         halve_body,
         "halve",
-        [piece] * chips,
+        [bf16(half // chips, width)] * chips,
         (place, mine, got),
         smem=1,
-        scratch=(pltpu.VMEM((half, width), BF16),),
-    )
-    terms = [pieces[0]] + [swap(pieces[k], "seq", 2 * k) for k in range(1, chips)]
-    settled = call(settle_body, "settle", piece, terms)
-    full = call(
-        join_body, "join", bf16(half, width), (place, settled, *chip_swaps(settled, n)), smem=1
-    )
-    return full, swap(full, "seq", 1)
+    )
+
+
+def halve_all_body(mine, other, out):
+    out[...] = (mine[...].astype(F32) + other[...].astype(F32)).astype(BF16)
+
+
+def total_body(place, *refs):
+    pieces, out, stack = refs[:-2], refs[-2], refs[-1]
+    for k, piece in enumerate(pieces):
+        stack[jnp.bitwise_xor(place[0] >> 1, k)] = piece[...]
+    total = stack[0].astype(F32)
+    for k in range(1, len(pieces)):
+        total = total + stack[k].astype(F32)
+    out[...] = total.astype(BF16)
+
+
+def total_chips(chip, got, place):
+    terms = [chip] + list(got)
+    return call(
+        total_body,
+        "total_small",
+        bf16(*chip.shape),
+        (place, *terms),
+        smem=1,
+        scratch=(pltpu.VMEM((len(terms), *chip.shape), BF16),),
+    )
 
 
 def both_halves(place, mine, other, whole):
@@ -805,11 +904,16 @@
     whole[pl.ds(pl.multiple_of((1 - core) * half, 16), half), :] = other[...]
 
 
-def finish_feed_body(place, mine, other, down, up, whole):
-    both_halves(place[0], mine, other, whole)
+def finish_feed_body(place, mine, other, down, up):
     ff = down.shape[0]
-    down[...] = whole[0:ff, :].astype(F32)
-    up[...] = whole[ff:, :].astype(F32)
+    core = place[0] & 1
+
+    def put(first, second):
+        down[...] = first[0:ff, :].astype(F32)
+        up[...] = second[0:D, :].astype(F32)
+
+    pl.when(core == 0)(lambda: put(mine, other))
+    pl.when(core == 1)(lambda: put(other, mine))
 
 
 def finish_small_body(place, mine, other, mixer, g2, s2, od, g1, s1, om, ou, taps, whole):
@@ -823,13 +927,12 @@
 
 
 def weight_grads_body(n, *refs):
-    queries, others, tokens = refs[:n], refs[n : 2 * n], refs[2 * n : 3 * n]
-    q, k, v, oq, ok, ov = refs[3 * n : 3 * n + 6]
-    turned, rows = refs[3 * n + 6 :]
+    blocks, tokens = refs[:n], refs[n : 2 * n]
+    q, k, v, oq, ok, ov = refs[2 * n : 2 * n + 6]
+    turned, rows = refs[2 * n + 6 :]
     wide = HEADS * HS
     for i in range(n):
-        turned[0:wide, i * ROWS : (i + 1) * ROWS] = queries[i][...]
-        turned[wide:, i * ROWS : (i + 1) * ROWS] = others[i][...]
+        turned[:, i * ROWS : (i + 1) * ROWS] = blocks[i][...]
         rows[i * ROWS : (i + 1) * ROWS, :] = tokens[i][...]
     ones = jnp.ones((16, n * ROWS), BF16)
     for i, (grad, sums) in enumerate(((q, oq), (k, ok), (v, ov))):
@@ -838,19 +941,12 @@
         sums[...] = dot_nt(ones, part)[0:1, :].reshape(wide)
 
 
-def tokens_sum_body(grad, *refs):
-    total = grad[...]
-    for r in refs[:-1]:
-        total = total + r[...].astype(F32)
-    refs[-1][...] = total.astype(BF16)
-
-
-def tokens_out_body(chunk, *refs):
-    pieces, out = refs[:-1], refs[-1]
-    rows = out.shape[0] // len(pieces)
-    for k, piece in enumerate(pieces):
-        start = pl.multiple_of(jnp.bitwise_xor(chunk[0], k) * rows, 16)
-        out[pl.ds(start, rows), :] = piece[...].astype(F32)
+def tokens_sum_body(mine, other, out):
+    out[...] = (mine[...].astype(F32) + other[...].astype(F32)).astype(BF16)
+
+
+def tokens_out_body(mine, other, out):
+    out[...] = mine[...].astype(F32) + other[...].astype(F32)
 
 
 def on_device(
@@ -894,17 +990,17 @@
     taps = jnp.pad(conv_taps, ((0, 5), side))
     taps_back = jnp.pad(conv_taps[:, ::-1], ((0, 5), side))
 
-    weights = jnp.where(place[0] % 2 == 0, up_weight, down_weight)
-    got = hid_swap(weights, 2)
-    other = swap(got, "seq", 1)
-    far_shift = hid_swap(up_shift, 2)
-    mixers = over_hid(mixer_weight)
-
-    raw_q, raw_k, tan_q, tan_k, pick_q, pack = project(
+    far_mixer = far_swap(mixer_weight)
+    bundle = make_bundle(place, up_weight, down_weight, mixer_weight, up_shift)
+    got = hid_swap(bundle, 2)
+
+    raw_q, raw_k, tan_q, tan_k, pack = project(
         tokens, wq, query_shift, wk, key_shift, wv, value_shift, hyperplanes, choose
     )
+    far_mixer, pack = after(far_mixer, pack)
+    other_mixer = swap(far_mixer, "seq", 1)
     packs = over_seq(pack)
-    feat_q, feat_k = local_feats(pick_q, pack)
+    feat_q = local_feats(KEPT, pack)
     context, near_half, far_half, weighted, total = forward(
         doc_lengths, place, slot, feat_q, taps, packs
     )
@@ -914,10 +1010,9 @@
         hid_swap(far_half, 2),
         hid_swap(far_half, 3),
     ]
-    pick_later, tokens_later, context = lax.optimization_barrier((pick_q, tokens, context))
-    picks = over_seq(pick_later)
-    token_blocks = over_seq(tokens_later)
-    first_mine, normed_mine, inverse_mine, low, slope, keep, send = call(
+    got, context = after(got, context)
+    other = swap(got, "seq", 1)
+    first_mine, normed_mine, inverse_mine, low, slope, keep, send, mixers = call(
         functools.partial(feed_body, parts),
         "feed",
         (
@@ -928,6 +1023,7 @@
             f32(half, 2 * units),
             f32(rows, D),
             bf16(rows, D),
+            bf16(parts, wide, D),
         ),
         (
             place,
@@ -941,9 +1037,10 @@
             down_weight,
             got,
             other,
-            far_shift,
+            mixer_weight,
+            far_mixer,
+            other_mixer,
             *contexts,
-            *mixers,
         ),
         smem=2,
         scratch=(
@@ -955,6 +1052,9 @@
         ),
         us=5,
     )
+    partial = hid_swap(send, 1)
+    tokens_later, keep = after(tokens, keep)
+    token_blocks = cross_chips(tokens_later)
     layer, dh2, down_low = call(
         second_body,
         "second_norm",
@@ -967,10 +1067,12 @@
             second_gain,
             second_shift,
             keep,
-            hid_swap(send, 1),
+            partial,
         ),
         smem=1,
     )
+    pack_later, dh2 = after(pack, dh2)
+    feat_k, slope = after(local_feats(0, pack_later), slope)
     down_half, keep, send = call(
         feed_back_body,
         "feed_back",
@@ -990,25 +1092,17 @@
         scratch=(pltpu.VMEM((half, D), F32), pltpu.VMEM((2, D, units), BF16)),
         us=4,
     )
+    token_blocks, mixers = after(token_blocks, mixers)
     first_back = call(
         functools.partial(first_back_body, parts),
         "first_norm_back",
-        (f32(rows, D), bf16(rows + 16, D), *[bf16(rows, wide)] * parts),
-        (dh2, normed_mine, inverse_mine, first_gain, keep, hid_swap(send, 1), *mixers),
+        (f32(rows, D), bf16(2 * rows + 32, D), *[bf16(rows, wide)] * parts),
+        (dh2, normed_mine, inverse_mine, first_gain, keep, hid_swap(send, 1), layer, mixers),
         us=3,
     )
     dh1, payload = first_back[:2]
-    grad_pack, row_totals = call(
-        functools.partial(split_body, parts),
-        "split",
-        (bf16(ROWS, 4 * HS), f32(8, ROWS)),
-        (slot, weighted, total, *exchange(first_back[2:])),
-        smem=1,
-        scratch=(pltpu.VMEM((ROWS, wide), BF16),),
-    )
-    grad_packs = over_seq(grad_pack)
-
-    feed_half = padded(units + D, n) // 2
+    pieces = exchange(first_back[2:])
+    feed_half = padded(2 * max(units, D), n) // 2
     feed_mine, feed_other, up_sums = call(
         feed_grads_body,
         "feed_grads",
@@ -1028,18 +1122,28 @@
         scratch=(
             pltpu.VMEM((ROWS, D), BF16),
             pltpu.VMEM((ROWS, D), BF16),
-            pltpu.VMEM((2 * feed_half, D), BF16),
         ),
         us=6,
     )
-    feed_sums = sum_over_seq(feed_mine, feed_other, place, n)
-
+    pieces, feed_other = after(pieces, feed_other)
+    grad_pack, row_totals = call(
+        functools.partial(split_body, parts),
+        "split",
+        (bf16(ROWS, 4 * HS), f32(8, ROWS)),
+        (slot, weighted, total, *pieces),
+        smem=1,
+        scratch=(pltpu.VMEM((ROWS, wide), BF16),),
+    )
+    payload, grad_pack = after(payload, grad_pack)
+    grad_blocks = cross_chips(grad_pack)
+    feed_pieces = scatter_chips(feed_mine, swap(feed_other, "seq", 1), place, n)
+    feed_got = [swap(feed_pieces[k], "seq", 2 * k) for k in range(1, n // 2)]
+    feed_own, row_totals = after(feed_pieces[0], row_totals)
     query_turned, query_input, tap_rows = query_back(
         doc_lengths,
         place,
         grad_pack,
         row_totals,
-        pick_q,
         tan_q,
         raw_q,
         choose_back,
@@ -1047,27 +1151,28 @@
         wq,
         packs,
     )
-    query_blocks = over_seq(query_turned)
-    layer_later, payload_later, grad_pack = lax.optimization_barrier((layer, payload, grad_pack))
-    layers = over_hid(layer_later)
-    payloads = over_hid(payload_later)
-    small_half = padded(wide + 16, n) // 2
+    grad_blocks, query_turned = after(grad_blocks, query_turned)
+    grad_packs = from_partner(grad_blocks)
+    payloads = over_hid(payload)
+    settled = call(settle_body, "settle", bf16(*feed_own.shape), (feed_own, *feed_got))
+    small_half = -(-(wide + 16) // 32) * 16
     small_mine, small_other, layer_out = call(
         functools.partial(mixer_grads_body, parts),
         "mixer_grads",
         (bf16(small_half, D), bf16(small_half, D), bf16(ROWS, D)),
-        (place, slot, context, up_sums, tap_rows, *layers, *payloads),
+        (place, slot, context, up_sums, tap_rows, *payloads),
         smem=2,
         scratch=(pltpu.VMEM((2 * small_half, D), BF16), pltpu.VMEM((ROWS, D), BF16)),
     )
-    small_sums = sum_over_seq(small_mine, small_other, place, n)
+    (settled, small_other), grad_packs = after((settled, small_other), grad_packs)
+    small_got = swap(small_other, "seq", 1)
+    feed_chips = chip_swaps(settled, n)
     last = key_back(
         (
             doc_lengths,
             place,
             slot,
             feat_k,
-            pack,
             tan_k,
             raw_k,
             taps_back,
@@ -1076,23 +1181,32 @@
             wk,
             wv,
             query_input,
-        ),
-        picks,
+            query_turned,
+            dh1,
+        ),
+        packs,
         grad_packs,
-        parts,
-    )
-    other_blocks = over_seq(last[0])
-    piece = call(tokens_sum_body, "tokens_sum", bf16(rows, D), (dh1, *exchange(last[1:])))
-    tokens_grad = call(
-        tokens_out_body, "tokens_out", f32(ROWS, D), (slot, *over_hid(piece)), smem=1
-    )
+    )
+    last, (small_got, feed_chips) = after(last, (small_got, feed_chips))
+    near_tokens = hid_swap(last[1], 2)
+    blocks = over_seq(last[0])
+    both = call(tokens_sum_body, "tokens_sum", bf16(ROWS, D), (last[1], near_tokens))
+    small_chip = call(halve_all_body, "halve_small", bf16(*small_mine.shape), (small_mine, small_got))
+    both, small_chip = after(both, small_chip)
+    feed_full = call(
+        join_body, "join", bf16(feed_half, D), (place, settled, *feed_chips), smem=1
+    )
+    tokens_grad = call(tokens_out_body, "tokens_out", f32(ROWS, D), (both, hid_swap(both, 1)))
+    feed_sums = (feed_full, swap(feed_full, "seq", 1))
+    small_full = total_chips(small_chip, chip_swaps(small_chip, n), place)
+    small_sums = (small_full, swap(small_full, "seq", 1))
+    token_blocks = from_partner(token_blocks)
     down_grad, up_grad = call(
         finish_feed_body,
         "finish_feed",
         (f32(units, D), f32(D, units)),
         (place, *feed_sums),
         smem=1,
-        scratch=(pltpu.VMEM((2 * feed_half, D), BF16),),
         us=4,
     )
     mixer_grad, g2, s2, od, g1, s1, om, ou, taps_grad = call(
@@ -1107,7 +1221,7 @@
         functools.partial(weight_grads_body, n),
         "weight_grads",
         (*[f32(wide, D)] * 3, *[f32(wide)] * 3),
-        (*query_blocks, *other_blocks, *token_blocks),
+        (*blocks, *token_blocks),
         scratch=(pltpu.VMEM((3 * wide, n * ROWS), BF16), pltpu.VMEM((n * ROWS, D), BF16)),
         us=4,
     )

time: 290 us -> 233 us (0.80)
  waiting for transfers between devices: 85.8 us -> 47.1 us
  starting transfers between devices: 91.8 us -> 75.4 us
    ppermute x87 -> x60, waiting for transfers between devices: 85.8 us -> 41.7 us  [swap(): return lax.ppermute(value, axis, [(i, i ^ k) for i in range(n)])]
    ppermute x87 -> x60, starting transfers between devices: 91.8 us -> 71.2 us  [swap(): return lax.ppermute(value, axis, [(i, i ^ k) for i in range(n)])]
    ppermute x0 -> x1, waiting for transfers between devices: none -> 5.38 us  [far_swap(): return lax.ppermute(value, ('seq', 'hid'), pairs)]
    ppermute x0 -> x1, starting transfers between devices: none -> 4.13 us  [far_swap(): return lax.ppermute(value, ('seq', 'hid'), pairs)]
    unnamed x199 -> x139, local copies, waits for them, and re-layouts: 11.2 us -> 13.7 us
    pallas_call x23 -> x24, Pallas kernels: 93.8 us -> 93.1 us  [call(): pl.pallas_call(body, out_shape=outs, in_specs=[SMEM] * smem + [VMEM] * (l...]
  transfers between devices with their start and end apart: 87 -> 61, of which waited for: 17 -> 16; matrix products, arithmetic and copies ran while one was open for 1% -> 1% of each run, Pallas kernels for 27% -> 36%
where the time goes in v3:
time: 233 us
  Pallas kernels  93.1 us (40%)
  starting transfers between devices  75.4 us (32%)
  waiting for transfers between devices  47.1 us (20%)
  local copies, waits for them, and re-layouts  15.2 us (7%)
    pallas_call x24, Pallas kernels, call(): pl.pallas_call(body, out_shape=outs, in_specs=[SMEM] * smem + [VMEM] * (l...  93.1 us
    ppermute x60, starting transfers between devices, swap(): return lax.ppermute(value, axis, [(i, i ^ k) for i in range(n)])  71.2 us
    ppermute x60, waiting for transfers between devices, swap(): return lax.ppermute(value, axis, [(i, i ^ k) for i in range(n)])  41.7 us
    unnamed x139, local copies, waits for them, and re-layouts  13.7 us
    ppermute x1, waiting for transfers between devices, far_swap(): return lax.ppermute(value, ('seq', 'hid'), pairs)  5.38 us
  transfers between devices with their start and end apart: 61, of which 16 were waited for; matrix products, arithmetic and copies ran while one was open for 1% of the time, Pallas kernels for 36%

profile of v3, /device:TPU:0, one launch (start us, length us, event | category | flops | bytes accessed | tf_op | source)
XLA Modules:
  0.0 232.6 jit_solution(17222731082389184627)
XLA Ops:
  0.7 4.1 %collective-permute-start.1 = (bf16[192,768]{1,0:T(8,128)(2,1)}, bf16[192,768]{1,0:T(8,128)(2,1)S(1)}, u32[]{:S(2)}, u32[]{:S(2)}) collective-permute-start(bf16[192,768]{1,0:T(8,128)(2,1)} %refs_9_.1), channel_id=1, source_target_pairs={{0,2},{1,3},{2,0},{3,1},{4,7},{5,6},{6,5},{7,4},{8,10},{9,11},{10,... | collective-permute-start | bytes 884744 | tf_op jit(solution)/shard_map/ppermute | solution.py:574
  4.8 2.9 %bundle.1 = bf16[880,768]{1,0:T(8,128)(2,1)} custom-call(s32[1]{0:T(128)} %bitcast.place, bf16[768,768]{1,0:T(8,128)(2,1)} %up.5, bf16[768,768]{1,0:T(8,128)(2,1)} %down.5, bf16[192,768]{1,0:T(8,128)(2,1)} %refs_9_.1, f32[768]{0:T(1024)} %up_shift.1), custom_call_target="tpu_custom_call" | custom-call | flops 20000000000 | bytes 100000 | tf_op jit(solution)/shard_map/bundle/pallas_call | solution.py:165
  10.0 3.2 %project.1 = (f32[64,768]{1,0:T(8,128)}, f32[64,768]{1,0:T(8,128)}, f32[32,768]{1,0:T(8,128)}, f32[32,768]{1,0:T(8,128)}, bf16[128,768]{1,0:T(8,128)(2,1)}) custom-call(bf16[256,768]{1,0:T(8,128)(2,1)} %refs_8_, bf16[192,768]{1,0:T(8,128)(2,1)} %bitcast.9, f32[192]{0:T(256)} %bq.1, bf16[192,768]{1,0:T(8,128)(2,1)} %bitcast.11, f32[192]{0:T(256)} %bk.1, ...), custom_call_target="tpu_custom_call" | custom-call | flops 100000000 | bytes 100000 | tf_op jit(solution)/shard_map/project/pallas_call | solution.py:165
  13.2 5.4 %collective-permute-done.1.refs_10_ = bf16[192,768]{1,0:T(8,128)(2,1)S(1)} collective-permute-done((bf16[192,768]{1,0:T(8,128)(2,1)}, bf16[192,768]{1,0:T(8,128)(2,1)S(1)}, u32[]{:S(2)}, u32[]{:S(2)}) %collective-permute-start.1) | collective-permute-done | bytes 294944 | tf_op jit(solution)/shard_map/ppermute | solution.py:574
  24.5 2.8 %collective-permute-done.5.refs_4_ = bf16[128,768]{1,0:T(8,128)(2,1)S(1)} collective-permute-done((bf16[128,768]{1,0:T(8,128)(2,1)}, bf16[128,768]{1,0:T(8,128)(2,1)S(1)}, u32[]{:S(2)}, u32[]{:S(2)}) %collective-permute-start.5) | collective-permute-done | bytes 196640 | tf_op jit(solution)/shard_map/ppermute | solution.py:539
  29.1 2.5 %local_feats.2.feat_q = bf16[3,256,1024]{2,1,0:T(8,128)(2,1)} custom-call(bf16[128,768]{1,0:T(8,128)(2,1)} %get-tuple-element.144.pack.refs_0_), custom_call_target="tpu_custom_call" | custom-call | flops 2000000000 | bytes 100000 | tf_op jit(solution)/shard_map/local_feats/pallas_call | solution.py:165
  32.5 7.3 %attend.1 = (bf16[256,192]{1,0:T(8,128)(2,1)}, bf16[128,192]{1,0:T(8,128)(2,1)}, bf16[128,192]{1,0:T(8,128)(2,1)}, f32[256,192]{1,0:T(8,128)}, f32[256,192]{1,0:T(8,128)}) custom-call(s32[2]{0:T(128)} %lengths.5, s32[1]{0:T(128)} %bitcast.place, s32[1]{0:T(128)} %bitcast.1.slot.chunk, bf16[3,256,1024]{2,1,0:T(8,128)(2,1)} %local_feats.2.feat_q, ...), custom_call_target="tpu_custom_call" | custom-call | flops 8999999488 | bytes 100000 | tf_op jit(solution)/shard_map/attend/pallas_call | solution.py:165
  39.8 3.7 %collective-permute-done.refs_7_.got = bf16[880,768]{1,0:T(8,128)(2,1)S(1)} collective-permute-done((bf16[880,768]{1,0:T(8,128)(2,1)}, bf16[880,768]{1,0:T(8,128)(2,1)S(1)}, u32[]{:S(2)}, u32[]{:S(2)}) %collective-permute-start) | collective-permute-done | bytes 1351712 | tf_op jit(solution)/shard_map/ppermute | solution.py:539
  55.1 5.7 %feed.1 = (f32[64,768]{1,0:T(8,128)}, f32[64,768]{1,0:T(8,128)}, f32[64,128]{1,0:T(8,128)}, bf16[128,768]{1,0:T(8,128)(2,1)}, f32[128,1536]{1,0:T(8,128)}, /*ind...) custom-call(s32[1]{0:T(128)} %bitcast.place, s32[1]{0:T(128)} %bitcast.1.slot.chunk, ...), custom_call_target="tpu_custom_call" | custom-call | flops 5000000000 | bytes 100000 | tf_op jit(solution)/shard_map/feed/pallas_call | solution.py:165
  61.8 3.8 %collective-permute-start.19 = (bf16[256,768]{1,0:T(8,128)(2,1)S(1)}, bf16[256,768]{1,0:T(8,128)(2,1)S(1)}, u32[]{:S(2)}, u32[]{:S(2)}) collective-permute-start(bf16[256,768]{1,0:T(8,128)(2,1)S(1)} %copy-done), channel_id=1, source_target_pairs={{0,8},{4,12},{8,0},{12,4},{16,24},{20,28},{24,16},{28,20},{1,9},{5... | collective-permute-start | bytes 1179656 | tf_op jit(solution)/shard_map/ppermute | solution.py:539
  72.0 2.5 %local_feats.3.feat_k = bf16[3,256,1024]{2,1,0:T(8,128)(2,1)} custom-call(bf16[128,768]{1,0:T(8,128)(2,1)} %get-tuple-element.144.pack.refs_0_), custom_call_target="tpu_custom_call" | custom-call | flops 2000000000 | bytes 100000 | tf_op jit(solution)/shard_map/local_feats/pallas_call | solution.py:165
  77.7 5.4 %feed_back.1 = (bf16[128,768]{1,0:T(8,128)(2,1)}, f32[64,768]{1,0:T(8,128)}, bf16[64,768]{1,0:T(8,128)(2,1)}) custom-call(s32[1]{0:T(128)} %bitcast.place, s32[1]{0:T(128)} %bitcast.1.slot.chunk, f32[128,1536]{1,0:T(8,128)} %get-tuple-element.146.slope, bf16[768,768]{1,0:T(8,128)(2,1)} %up.5, bf16[768,768]{1,0:T(8,128)(2,1)} %down.5, ...), custom_call_target="tpu_custom_call" | custom-call | flops 4000000000 | bytes 100000 | tf_op jit(solution)/shard_map/feed_back/pallas_call | solution.py:165
  86.0 3.6 %collective-permute-done.18.got = bf16[64,768]{1,0:T(8,128)(2,1)S(1)} collective-permute-done((bf16[64,768]{1,0:T(8,128)(2,1)}, bf16[64,768]{1,0:T(8,128)(2,1)S(1)}, u32[]{:S(2)}, u32[]{:S(2)}) %collective-permute-start.18) | collective-permute-done | bytes 98336 | tf_op jit(solution)/shard_map/ppermute | solution.py:539
  90.3 2.8 %first_norm_back.1 = (f32[64,768]{1,0:T(8,128)}, bf16[160,768]{1,0:T(8,128)(2,1)}, bf16[64,192]{1,0:T(8,128)(2,1)}, bf16[64,192]{1,0:T(8,128)(2,1)}, bf16[64,192]{1,0:T(8,128)(2,1)}, /*index=5*/bf16[64,192]{1,0:T(8,128)(2,1)}) custom-call(f32[64,768]{1,0:T(8,128)} %get-tuple-element.150.grad, f32[64,768]{1,0:T(8,128)} %get-tuple-element.151.normed, ...), custom_call_target="tpu_custom_call" | custom-call | flops 3000000000 | bytes 100000 | tf_op jit(solution)/shard_map/first_norm_back/pallas_call | solution.py:165
  98.8 5.2 %feed_grads.1 = (bf16[768,768]{1,0:T(8,128)(2,1)}, bf16[768,768]{1,0:T(8,128)(2,1)}, f32[8,768]{1,0:T(8,128)}) custom-call(s32[1]{0:T(128)} %bitcast.place, s32[1]{0:T(128)} %bitcast.1.slot.chunk, bf16[128,768]{1,0:T(8,128)(2,1)} %get-tuple-element.138.low_mine, bf16[128,768]{1,0:T(8,128)(2,1)} %copy-done.44, bf16[128,768]{1,0:T(8,128)(2,1)} %get-tuple-element.148.down_mine, ...), custom_call_target="tpu_custom_call" | custom-call | flops 6000000000 | bytes 100000 | tf_op jit(solution)/shard_map/feed_grads/pallas_call | solution.py:165
  104.7 2.5 %split.1 = (bf16[256,256]{1,0:T(8,128)(2,1)}, f32[8,256]{1,0:T(8,128)}) custom-call(s32[1]{0:T(128)} %bitcast.1.slot.chunk, f32[256,192]{1,0:T(8,128)} %get-tuple-element.160.weighted, f32[256,192]{1,0:T(8,128)} %get-tuple-element.161.total, bf16[64,192]{1,0:T(8,128)(2,1)} %get-tuple-element.167.refs_0_, bf16[64,192]{1,0:T(8,128)(2,1)} %copy-done.66, ...), custom_call_target="tpu_custom_call" | custom-call | flops 2000000000 | bytes 100000 | tf_op jit(solution)/shard_map/split/pallas_call | solution.py:165
  108.8 2.8 %collective-permute-start.27 = (bf16[160,768]{1,0:T(8,128)(2,1)S(1)}, bf16[160,768]{1,0:T(8,128)(2,1)S(1)}, u32[]{:S(2)}, u32[]{:S(2)}) collective-permute-start(bf16[160,768]{1,0:T(8,128)(2,1)S(1)} %copy-done.32), channel_id=1, source_target_pairs={{0,1},{1,0},{2,3},{3,2},{4,5},{5,4},{6,7},{7,6},{8,9},{9,8},{10,11... | collective-permute-start | bytes 737288 | tf_op jit(solution)/shard_map/ppermute | solution.py:539
  111.6 2.6 %collective-permute-start.29 = (bf16[256,256]{1,0:T(8,128)(2,1)}, bf16[256,256]{1,0:T(8,128)(2,1)S(1)}, u32[]{:S(2)}, u32[]{:S(2)}) collective-permute-start(bf16[256,256]{1,0:T(8,128)(2,1)} %get-tuple-element.199.grads.refs_8_), channel_id=1, source_target_pairs={{0,8},{4,12},{8,0},{12,4},{16,24},{20,28},{24,16},{28,20},{1,9},{5... | collective-permute-start | bytes 393224 | tf_op jit(solution)/shard_map/ppermute | solution.py:539
  115.7 2.7 %halve.1 = (bf16[192,768]{1,0:T(8,128)(2,1)}, bf16[192,768]{1,0:T(8,128)(2,1)}, bf16[192,768]{1,0:T(8,128)(2,1)}, bf16[192,768]{1,0:T(8,128)(2,1)}) custom-call(s32[1]{0:T(128)} %bitcast.place, bf16[768,768]{1,0:T(8,128)(2,1)} %get-tuple-element.173.mine, bf16[768,768]{1,0:T(8,128)(2,1)} %copy-done.7), custom_call_target="tpu_custom_call" | custom-call | flops 2000000000 | bytes 100000 | tf_op jit(solution)/shard_map/halve/pallas_call | solution.py:165
  123.7 2.8 %collective-permute-start.34 = (bf16[192,768]{1,0:T(8,128)(2,1)}, bf16[192,768]{1,0:T(8,128)(2,1)S(1)}, u32[]{:S(2)}, u32[]{:S(2)}) collective-permute-start(bf16[192,768]{1,0:T(8,128)(2,1)} %get-tuple-element.193), channel_id=1, source_target_pairs={{0,24},{4,28},{8,16},{12,20},{16,8},{20,12},{24,0},{28,4},{1,25},{... | collective-permute-start | bytes 884744 | tf_op jit(solution)/shard_map/ppermute | solution.py:539
  126.6 8.5 %query_back.1 = (bf16[192,256]{1,0:T(8,128)(2,1)}, f32[256,768]{1,0:T(8,128)}, f32[8,512]{1,0:T(8,128)}) custom-call(s32[2]{0:T(128)} %lengths.5, s32[1]{0:T(128)} %bitcast.place, bf16[256,256]{1,0:T(8,128)(2,1)} %get-tuple-element.199.grads.refs_8_, f32[8,256]{1,0:T(8,128)} %get-tuple-element.177.row_totals, f32[32,768]{1,0:T(8,128)} %get-tuple-element.178.tan, ...), custom_call_target="tpu_custom_call" | custom-call | flops 8999999488 | bytes 100000 | tf_op jit(solution)/shard_map/query_back/pallas_call | solution.py:165
  135.9 2.6 %mixer_grads.1 = (bf16[112,768]{1,0:T(8,128)(2,1)}, bf16[112,768]{1,0:T(8,128)(2,1)}, bf16[256,768]{1,0:T(8,128)(2,1)}) custom-call(s32[1]{0:T(128)} %bitcast.place, s32[1]{0:T(128)} %bitcast.1.slot.chunk, bf16[256,192]{1,0:T(8,128)(2,1)} %get-tuple-element.133.context, f32[8,768]{1,0:T(8,128)} %get-tuple-element.149.up_sums, ...), custom_call_target="tpu_custom_call" | custom-call | flops 2000000000 | bytes 100000 | tf_op jit(solution)/shard_map/mixer_grads/pallas_call | solution.py:165
  142.0 5.7 %collective-permute-start.40 = (bf16[192,768]{1,0:T(8,128)(2,1)}, bf16[192,768]{1,0:T(8,128)(2,1)S(1)}, u32[]{:S(2)}, u32[]{:S(2)}) collective-permute-start(bf16[192,768]{1,0:T(8,128)(2,1)} %settle.1.refs_0_), channel_id=1, source_target_pairs={{0,8},{4,12},{8,0},{12,4},{16,24},{20,28},{24,16},{28,20},{1,9},{5... | collective-permute-start | bytes 884744 | tf_op jit(solution)/shard_map/ppermute | solution.py:539
  149.3 12.6 %key_back.1 = (bf16[576,256]{1,0:T(8,128)(2,1)}, bf16[256,768]{1,0:T(8,128)(2,1)}) custom-call(s32[2]{0:T(128)} %lengths.5, s32[1]{0:T(128)} %bitcast.place, s32[1]{0:T(128)} %bitcast.1.slot.chunk, bf16[3,256,1024]{2,1,0:T(8,128)(2,1)} %local_feats.3.feat_k, f32[32,768]{1,0:T(8,128)} %get-tuple-element.184.tan, f32[64,768]{1,0:T(8,128)} %get-tuple-element.185.raw, ...), custom_call_target="tpu_custom_call" | custom-call | flops 15000000512 | bytes 100000 | tf_op jit(solution)/shard_map/key_back/pallas_call | solution.py:165
  164.8 11.1 %collective-permute-start.46 = (bf16[576,256]{1,0:T(8,128)(2,1)}, bf16[576,256]{1,0:T(8,128)(2,1)}, u32[]{:S(2)}, u32[]{:S(2)}) collective-permute-start(bf16[576,256]{1,0:T(8,128)(2,1)} %get-tuple-element.215.refs_0_), channel_id=1, source_target_pairs={{0,8},{4,12},{8,0},{12,4},{16,24},{20,28},{24,16},{28,20},{1,9},{5... | collective-permute-start | bytes 884744 | tf_op jit(solution)/shard_map/ppermute | solution.py:539
  177.6 3.6 %collective-permute-start.48 = (bf16[576,256]{1,0:T(8,128)(2,1)S(1)}, bf16[576,256]{1,0:T(8,128)(2,1)}, u32[]{:S(2)}, u32[]{:S(2)}) collective-permute-start(bf16[576,256]{1,0:T(8,128)(2,1)S(1)} %copy-done.18), channel_id=1, source_target_pairs={{0,16},{4,20},{8,24},{12,28},{16,0},{20,4},{24,8},{28,12},{1,17},{... | collective-permute-start | bytes 884744 | tf_op jit(solution)/shard_map/ppermute | solution.py:539
  183.3 3.3 %collective-permute-start.50 = (bf16[576,256]{1,0:T(8,128)(2,1)S(1)}, bf16[576,256]{1,0:T(8,128)(2,1)S(1)}, u32[]{:S(2)}, u32[]{:S(2)}) collective-permute-start(bf16[576,256]{1,0:T(8,128)(2,1)S(1)} %copy-done.18), channel_id=1, source_target_pairs={{0,24},{4,28},{8,16},{12,20},{16,8},{20,12},{24,0},{28,4},{1,25},{... | collective-permute-start | bytes 884744 | tf_op jit(solution)/shard_map/ppermute | solution.py:539
  187.4 2.7 %collective-permute-start.58 = (bf16[112,768]{1,0:T(8,128)(2,1)}, bf16[112,768]{1,0:T(8,128)(2,1)}, u32[]{:S(2)}, u32[]{:S(2)}) collective-permute-start(bf16[112,768]{1,0:T(8,128)(2,1)} %halve_small.1.refs_0_), channel_id=1, source_target_pairs={{0,24},{4,28},{8,16},{12,20},{16,8},{20,12},{24,0},{28,4},{1,25},{... | collective-permute-start | bytes 516104 | tf_op jit(solution)/shard_map/ppermute | solution.py:539
  192.4 6.1 %collective-permute-done.48.refs_4_ = bf16[576,256]{1,0:T(8,128)(2,1)} collective-permute-done((bf16[576,256]{1,0:T(8,128)(2,1)S(1)}, bf16[576,256]{1,0:T(8,128)(2,1)}, u32[]{:S(2)}, u32[]{:S(2)}) %collective-permute-start.48) | collective-permute-done | bytes 294944 | tf_op jit(solution)/shard_map/ppermute | solution.py:539
  207.4 5.9 %weight_grads.1 = (f32[192,768]{1,0:T(8,128)}, f32[192,768]{1,0:T(8,128)}, f32[192,768]{1,0:T(8,128)}, f32[192]{0:T(256)}, f32[192]{0:T(256)}, /*index=5*/f32[192]{0:T(256)}) custom-call(bf16[576,256]{1,0:T(8,128)(2,1)} %get-tuple-element.215.refs_0_, bf16[576,256]{1,0:T(8,128)(2,1)} %copy-done.26, bf16[576,256]{1,0:T(8,128)(2,1)} %collective-permute-done.46.refs_2_, ...), custom_call_target="tpu_custom_call" | custom-call | flops 4000000000 | bytes 100000 | tf_op jit(solution)/shard_map/weight_grads/pallas_call | solution.py:165
  215.9 8.8 %collective-permute-done.44.other = bf16[256,768]{1,0:T(8,128)(2,1)S(1)} collective-permute-done((bf16[256,768]{1,0:T(8,128)(2,1)S(1)}, bf16[256,768]{1,0:T(8,128)(2,1)S(1)}, u32[]{:S(2)}, u32[]{:S(2)}) %collective-permute-start.44) | collective-permute-done | bytes 393248 | tf_op jit(solution)/shard_map/ppermute | solution.py:539
  228.5 4.1 %finish_feed.1 = (f32[768,768]{1,0:T(8,128)}, f32[768,768]{1,0:T(8,128)}) custom-call(s32[1]{0:T(128)} %bitcast.place, bf16[768,768]{1,0:T(8,128)(2,1)} %join.1.mine, bf16[768,768]{1,0:T(8,128)(2,1)} %copy-done.6), custom_call_target="tpu_custom_call" | custom-call | flops 4000000000 | bytes 100000 | tf_op jit(solution)/shard_map/finish_feed/pallas_call | solution.py:165
  (258 shorter events, 82.0 us)
Async XLA Ops:
  0.7 17.9 %collective-permute-start.1 = (bf16[192,768]{1,0:T(8,128)(2,1)}, bf16[192,768]{1,0:T(8,128)(2,1)S(1)}, u32[]{:S(2)}, u32[]{:S(2)}) collective-permute-start(bf16[192,768]{1,0:T(8,128)(2,1)} %refs_9_.1), channel_id=1, source_target_pairs={{0,2},{1,3},{2,0},{3,1},{4,7},{5,6},{6,5},{7,4},{8,10},{9,11},{10,... | collective-permute-start | bytes 884744 | tf_op jit(solution)/shard_map/ppermute | solution.py:574
  7.6 35.8 %collective-permute-start = (bf16[880,768]{1,0:T(8,128)(2,1)}, bf16[880,768]{1,0:T(8,128)(2,1)S(1)}, u32[]{:S(2)}, u32[]{:S(2)}) collective-permute-start(bf16[880,768]{1,0:T(8,128)(2,1)} %bundle.1), channel_id=1, source_target_pairs={{0,1},{1,0},{2,3},{3,2},{4,5},{5,4},{6,7},{7,6},{8,9},{9,8},{10,11... | collective-permute-start | bytes 4055048 | tf_op jit(solution)/shard_map/ppermute | solution.py:539
  61.8 24.1 %collective-permute-start.19 = (bf16[256,768]{1,0:T(8,128)(2,1)S(1)}, bf16[256,768]{1,0:T(8,128)(2,1)S(1)}, u32[]{:S(2)}, u32[]{:S(2)}) collective-permute-start(bf16[256,768]{1,0:T(8,128)(2,1)S(1)} %copy-done), channel_id=1, source_target_pairs={{0,8},{4,12},{8,0},{12,4},{16,24},{20,28},{24,16},{28,20},{1,9},{5... | collective-permute-start | bytes 1179656 | tf_op jit(solution)/shard_map/ppermute | solution.py:539
  65.6 20.4 %collective-permute-start.20 = (bf16[256,768]{1,0:T(8,128)(2,1)S(1)}, bf16[256,768]{1,0:T(8,128)(2,1)S(1)}, u32[]{:S(2)}, u32[]{:S(2)}) collective-permute-start(bf16[256,768]{1,0:T(8,128)(2,1)S(1)} %copy-done), channel_id=1, source_target_pairs={{0,16},{4,20},{8,24},{12,28},{16,0},{20,4},{24,8},{28,12},{1,17},{... | collective-permute-start | bytes 1179656 | tf_op jit(solution)/shard_map/ppermute | solution.py:539
  65.6 20.4 %collective-permute-start.21 = (bf16[256,768]{1,0:T(8,128)(2,1)S(1)}, bf16[256,768]{1,0:T(8,128)(2,1)S(1)}, u32[]{:S(2)}, u32[]{:S(2)}) collective-permute-start(bf16[256,768]{1,0:T(8,128)(2,1)S(1)} %copy-done), channel_id=1, source_target_pairs={{0,24},{4,28},{8,16},{12,20},{16,8},{20,12},{24,0},{28,4},{1,25},{... | collective-permute-start | bytes 1179656 | tf_op jit(solution)/shard_map/ppermute | solution.py:539
  83.8 13.6 %collective-permute-start.14 = (bf16[128,768]{1,0:T(8,128)(2,1)S(1)}, bf16[128,768]{1,0:T(8,128)(2,1)S(1)}, u32[]{:S(2)}, u32[]{:S(2)}) collective-permute-start(bf16[128,768]{1,0:T(8,128)(2,1)S(1)} %copy-done.43), channel_id=1, source_target_pairs={{0,1},{1,0},{2,3},{3,2},{4,5},{5,4},{6,7},{7,6},{8,9},{9,8},{10,11... | collective-permute-start | bytes 589832 | tf_op jit(solution)/shard_map/ppermute | solution.py:539
  85.9 11.6 %collective-permute-start.17 = (bf16[128,768]{1,0:T(8,128)(2,1)}, bf16[128,768]{1,0:T(8,128)(2,1)S(1)}, u32[]{:S(2)}, u32[]{:S(2)}) collective-permute-start(bf16[128,768]{1,0:T(8,128)(2,1)} %get-tuple-element.148.down_mine), channel_id=1, source_target_pairs={{0,1},{1,0},{2,3},{3,2},{4,5},{5,4},{6,7},{7,6},{8,9},{9,8},{10,11... | collective-permute-start | bytes 589832 | tf_op jit(solution)/shard_map/ppermute | solution.py:539
  93.1 11.0 %collective-permute-start.22 = (bf16[64,192]{1,0:T(8,128)(2,1)}, bf16[64,192]{1,0:T(8,128)(2,1)S(1)}, u32[]{:S(2)}, u32[]{:S(2)}) collective-permute-start(bf16[64,192]{1,0:T(8,128)(2,1)} %get-tuple-element.163), channel_id=1, source_target_pairs={{0,2},{1,3},{2,0},{3,1},{4,6},{5,7},{6,4},{7,5},{8,10},{9,11},{10,... | collective-permute-start | bytes 73736 | tf_op jit(solution)/shard_map/ppermute | solution.py:539
  104.1 10.1 %collective-permute-start.25 = (bf16[768,768]{1,0:T(8,128)(2,1)}, bf16[768,768]{1,0:T(8,128)(2,1)S(1)}, u32[]{:S(2)}, u32[]{:S(2)}) collective-permute-start(bf16[768,768]{1,0:T(8,128)(2,1)} %get-tuple-element.174), channel_id=1, source_target_pairs={{0,4},{4,0},{8,12},{12,8},{16,20},{20,16},{24,28},{28,24},{1,5},{5... | collective-permute-start | bytes 3538952 | tf_op jit(solution)/shard_map/ppermute | solution.py:539
  107.3 16.5 %collective-permute-start.26 = (bf16[160,768]{1,0:T(8,128)(2,1)S(1)}, bf16[160,768]{1,0:T(8,128)(2,1)S(1)}, u32[]{:S(2)}, u32[]{:S(2)}) collective-permute-start(bf16[160,768]{1,0:T(8,128)(2,1)S(1)} %copy-done.32), channel_id=1, source_target_pairs={{0,2},{1,3},{2,0},{3,1},{4,6},{5,7},{6,4},{7,5},{8,10},{9,11},{10,... | collective-permute-start | bytes 737288 | tf_op jit(solution)/shard_map/ppermute | solution.py:539
  108.8 26.2 %collective-permute-start.27 = (bf16[160,768]{1,0:T(8,128)(2,1)S(1)}, bf16[160,768]{1,0:T(8,128)(2,1)S(1)}, u32[]{:S(2)}, u32[]{:S(2)}) collective-permute-start(bf16[160,768]{1,0:T(8,128)(2,1)S(1)} %copy-done.32), channel_id=1, source_target_pairs={{0,1},{1,0},{2,3},{3,2},{4,5},{5,4},{6,7},{7,6},{8,9},{9,8},{10,11... | collective-permute-start | bytes 737288 | tf_op jit(solution)/shard_map/ppermute | solution.py:539
  118.4 16.8 %collective-permute-start.28 = (bf16[160,768]{1,0:T(8,128)(2,1)S(1)}, bf16[160,768]{1,0:T(8,128)(2,1)S(1)}, u32[]{:S(2)}, u32[]{:S(2)}) collective-permute-start(bf16[160,768]{1,0:T(8,128)(2,1)S(1)} %copy-done.32), channel_id=1, source_target_pairs={{0,3},{1,2},{2,1},{3,0},{4,7},{5,6},{6,5},{7,4},{8,11},{9,10},{10,... | collective-permute-start | bytes 737288 | tf_op jit(solution)/shard_map/ppermute | solution.py:539
  122.4 16.1 %collective-permute-start.32 = (bf16[192,768]{1,0:T(8,128)(2,1)}, bf16[192,768]{1,0:T(8,128)(2,1)S(1)}, u32[]{:S(2)}, u32[]{:S(2)}) collective-permute-start(bf16[192,768]{1,0:T(8,128)(2,1)} %get-tuple-element.191), channel_id=1, source_target_pairs={{0,8},{4,12},{8,0},{12,4},{16,24},{20,28},{24,16},{28,20},{1,9},{5... | collective-permute-start | bytes 884744 | tf_op jit(solution)/shard_map/ppermute | solution.py:539
  123.7 15.4 %collective-permute-start.33 = (bf16[192,768]{1,0:T(8,128)(2,1)}, bf16[192,768]{1,0:T(8,128)(2,1)S(1)}, u32[]{:S(2)}, u32[]{:S(2)}) collective-permute-start(bf16[192,768]{1,0:T(8,128)(2,1)} %get-tuple-element.192), channel_id=1, source_target_pairs={{0,16},{4,20},{8,24},{12,28},{16,0},{20,4},{24,8},{28,12},{1,17},{... | collective-permute-start | bytes 884744 | tf_op jit(solution)/shard_map/ppermute | solution.py:539
  123.7 15.4 %collective-permute-start.34 = (bf16[192,768]{1,0:T(8,128)(2,1)}, bf16[192,768]{1,0:T(8,128)(2,1)S(1)}, u32[]{:S(2)}, u32[]{:S(2)}) collective-permute-start(bf16[192,768]{1,0:T(8,128)(2,1)} %get-tuple-element.193), channel_id=1, source_target_pairs={{0,24},{4,28},{8,16},{12,20},{16,8},{20,12},{24,0},{28,4},{1,25},{... | collective-permute-start | bytes 884744 | tf_op jit(solution)/shard_map/ppermute | solution.py:539
  135.1 29.7 %collective-permute-start.52 = (bf16[256,768]{1,0:T(8,128)(2,1)S(1)}, bf16[256,768]{1,0:T(8,128)(2,1)S(1)}, u32[]{:S(2)}, u32[]{:S(2)}) collective-permute-start(bf16[256,768]{1,0:T(8,128)(2,1)S(1)} %copy-done), channel_id=1, source_target_pairs={{0,4},{4,0},{8,12},{12,8},{16,20},{20,16},{24,28},{28,24},{1,5},{5... | collective-permute-start | bytes 1179656 | tf_op jit(solution)/shard_map/ppermute | solution.py:539
  142.0 19.9 %collective-permute-start.40 = (bf16[192,768]{1,0:T(8,128)(2,1)}, bf16[192,768]{1,0:T(8,128)(2,1)S(1)}, u32[]{:S(2)}, u32[]{:S(2)}) collective-permute-start(bf16[192,768]{1,0:T(8,128)(2,1)} %settle.1.refs_0_), channel_id=1, source_target_pairs={{0,8},{4,12},{8,0},{12,4},{16,24},{20,28},{24,16},{28,20},{1,9},{5... | collective-permute-start | bytes 884744 | tf_op jit(solution)/shard_map/ppermute | solution.py:539
  147.7 15.6 %collective-permute-start.41 = (bf16[192,768]{1,0:T(8,128)(2,1)}, bf16[192,768]{1,0:T(8,128)(2,1)S(1)}, u32[]{:S(2)}, u32[]{:S(2)}) collective-permute-start(bf16[192,768]{1,0:T(8,128)(2,1)} %settle.1.refs_0_), channel_id=1, source_target_pairs={{0,16},{4,20},{8,24},{12,28},{16,0},{20,4},{24,8},{28,12},{1,17},{... | collective-permute-start | bytes 884744 | tf_op jit(solution)/shard_map/ppermute | solution.py:539
  147.7 15.6 %collective-permute-start.42 = (bf16[192,768]{1,0:T(8,128)(2,1)}, bf16[192,768]{1,0:T(8,128)(2,1)S(1)}, u32[]{:S(2)}, u32[]{:S(2)}) collective-permute-start(bf16[192,768]{1,0:T(8,128)(2,1)} %settle.1.refs_0_), channel_id=1, source_target_pairs={{0,24},{4,28},{8,16},{12,20},{16,8},{20,12},{24,0},{28,4},{1,25},{... | collective-permute-start | bytes 884744 | tf_op jit(solution)/shard_map/ppermute | solution.py:539
  149.3 12.7 %collective-permute-start.39 = (bf16[112,768]{1,0:T(8,128)(2,1)S(1)}, bf16[112,768]{1,0:T(8,128)(2,1)S(1)}, u32[]{:S(2)}, u32[]{:S(2)}) collective-permute-start(bf16[112,768]{1,0:T(8,128)(2,1)S(1)} %copy-done.46), channel_id=1, source_target_pairs={{0,4},{4,0},{8,12},{12,8},{16,20},{20,16},{24,28},{28,24},{1,5},{5... | collective-permute-start | bytes 516104 | tf_op jit(solution)/shard_map/ppermute | solution.py:539
  164.1 13.5 %collective-permute-start.43 = (bf16[256,768]{1,0:T(8,128)(2,1)}, bf16[256,768]{1,0:T(8,128)(2,1)S(1)}, u32[]{:S(2)}, u32[]{:S(2)}) collective-permute-start(bf16[256,768]{1,0:T(8,128)(2,1)} %get-tuple-element.211.mine), channel_id=1, source_target_pairs={{0,1},{1,0},{2,3},{3,2},{4,5},{5,4},{6,7},{7,6},{8,9},{9,8},{10,11... | collective-permute-start | bytes 1179656 | tf_op jit(solution)/shard_map/ppermute | solution.py:539
  164.2 19.1 %collective-permute-start.53 = (bf16[256,768]{1,0:T(8,128)(2,1)S(1)}, bf16[256,768]{1,0:T(8,128)(2,1)S(1)}, u32[]{:S(2)}, u32[]{:S(2)}) collective-permute-start(bf16[256,768]{1,0:T(8,128)(2,1)S(1)} %collective-permute-done.19.refs_10_), channel_id=1, source_target_pairs={{0,4},{4,0},{8,12},{12,8},{16,20},{20,16},{24,28},{28,24},{1,5},{5... | collective-permute-start | bytes 1179656 | tf_op jit(solution)/shard_map/ppermute | solution.py:539
  164.2 22.4 %collective-permute-start.54 = (bf16[256,768]{1,0:T(8,128)(2,1)S(1)}, bf16[256,768]{1,0:T(8,128)(2,1)S(1)}, u32[]{:S(2)}, u32[]{:S(2)}) collective-permute-start(bf16[256,768]{1,0:T(8,128)(2,1)S(1)} %collective-permute-done.20.refs_12_), channel_id=1, source_target_pairs={{0,4},{4,0},{8,12},{12,8},{16,20},{20,16},{24,28},{28,24},{1,5},{5... | collective-permute-start | bytes 1179656 | tf_op jit(solution)/shard_map/ppermute | solution.py:539
  164.7 21.9 %collective-permute-start.55 = (bf16[256,768]{1,0:T(8,128)(2,1)S(1)}, bf16[256,768]{1,0:T(8,128)(2,1)S(1)}, u32[]{:S(2)}, u32[]{:S(2)}) collective-permute-start(bf16[256,768]{1,0:T(8,128)(2,1)S(1)} %collective-permute-done.21.refs_14_), channel_id=1, source_target_pairs={{0,4},{4,0},{8,12},{12,8},{16,20},{20,16},{24,28},{28,24},{1,5},{5... | collective-permute-start | bytes 1179656 | tf_op jit(solution)/shard_map/ppermute | solution.py:539
  164.8 22.6 %collective-permute-start.46 = (bf16[576,256]{1,0:T(8,128)(2,1)}, bf16[576,256]{1,0:T(8,128)(2,1)}, u32[]{:S(2)}, u32[]{:S(2)}) collective-permute-start(bf16[576,256]{1,0:T(8,128)(2,1)} %get-tuple-element.215.refs_0_), channel_id=1, source_target_pairs={{0,8},{4,12},{8,0},{12,4},{16,24},{20,28},{24,16},{28,20},{1,9},{5... | collective-permute-start | bytes 884744 | tf_op jit(solution)/shard_map/ppermute | solution.py:539
  177.6 20.9 %collective-permute-start.48 = (bf16[576,256]{1,0:T(8,128)(2,1)S(1)}, bf16[576,256]{1,0:T(8,128)(2,1)}, u32[]{:S(2)}, u32[]{:S(2)}) collective-permute-start(bf16[576,256]{1,0:T(8,128)(2,1)S(1)} %copy-done.18), channel_id=1, source_target_pairs={{0,16},{4,20},{8,24},{12,28},{16,0},{20,4},{24,8},{28,12},{1,17},{... | collective-permute-start | bytes 884744 | tf_op jit(solution)/shard_map/ppermute | solution.py:539
  183.3 15.3 %collective-permute-start.50 = (bf16[576,256]{1,0:T(8,128)(2,1)S(1)}, bf16[576,256]{1,0:T(8,128)(2,1)S(1)}, u32[]{:S(2)}, u32[]{:S(2)}) collective-permute-start(bf16[576,256]{1,0:T(8,128)(2,1)S(1)} %copy-done.18), channel_id=1, source_target_pairs={{0,24},{4,28},{8,16},{12,20},{16,8},{20,12},{24,0},{28,4},{1,25},{... | collective-permute-start | bytes 884744 | tf_op jit(solution)/shard_map/ppermute | solution.py:539
  186.6 12.5 %collective-permute-start.56 = (bf16[112,768]{1,0:T(8,128)(2,1)}, bf16[112,768]{1,0:T(8,128)(2,1)S(1)}, u32[]{:S(2)}, u32[]{:S(2)}) collective-permute-start(bf16[112,768]{1,0:T(8,128)(2,1)} %halve_small.1.refs_0_), channel_id=1, source_target_pairs={{0,8},{4,12},{8,0},{12,4},{16,24},{20,28},{24,16},{28,20},{1,9},{5... | collective-permute-start | bytes 516104 | tf_op jit(solution)/shard_map/ppermute | solution.py:539
  186.6 15.0 %collective-permute-start.57 = (bf16[112,768]{1,0:T(8,128)(2,1)}, bf16[112,768]{1,0:T(8,128)(2,1)S(1)}, u32[]{:S(2)}, u32[]{:S(2)}) collective-permute-start(bf16[112,768]{1,0:T(8,128)(2,1)} %halve_small.1.refs_0_), channel_id=1, source_target_pairs={{0,16},{4,20},{8,24},{12,28},{16,0},{20,4},{24,8},{28,12},{1,17},{... | collective-permute-start | bytes 516104 | tf_op jit(solution)/shard_map/ppermute | solution.py:539
  187.4 14.2 %collective-permute-start.58 = (bf16[112,768]{1,0:T(8,128)(2,1)}, bf16[112,768]{1,0:T(8,128)(2,1)}, u32[]{:S(2)}, u32[]{:S(2)}) collective-permute-start(bf16[112,768]{1,0:T(8,128)(2,1)} %halve_small.1.refs_0_), channel_id=1, source_target_pairs={{0,24},{4,28},{8,16},{12,20},{16,8},{20,12},{24,0},{28,4},{1,25},{... | collective-permute-start | bytes 516104 | tf_op jit(solution)/shard_map/ppermute | solution.py:539
  198.6 28.9 %collective-permute-start.60 = (bf16[768,768]{1,0:T(8,128)(2,1)}, bf16[768,768]{1,0:T(8,128)(2,1)S(1)}, u32[]{:S(2)}, u32[]{:S(2)}) collective-permute-start(bf16[768,768]{1,0:T(8,128)(2,1)} %join.1.mine), channel_id=1, source_target_pairs={{0,4},{4,0},{8,12},{12,8},{16,20},{20,16},{24,28},{28,24},{1,5},{5... | collective-permute-start | bytes 3538952 | tf_op jit(solution)/shard_map/ppermute | solution.py:539
  204.3 20.3 %collective-permute-start.44 = (bf16[256,768]{1,0:T(8,128)(2,1)S(1)}, bf16[256,768]{1,0:T(8,128)(2,1)S(1)}, u32[]{:S(2)}, u32[]{:S(2)}) collective-permute-start(bf16[256,768]{1,0:T(8,128)(2,1)S(1)} %copy-done.12), channel_id=1, source_target_pairs={{0,2},{1,3},{2,0},{3,1},{4,6},{5,7},{6,4},{7,5},{8,10},{9,11},{10,... | collective-permute-start | bytes 1179656 | tf_op jit(solution)/shard_map/ppermute | solution.py:539
  (98 other events, 679.1 us)

commit v4 on v3

--- a/solution.py
+++ b/solution.py
@@ -40,6 +40,10 @@
     return lax.dot_general(a, b, (((1,), (1,)), ((), ())), preferred_element_type=F32)
 
 
+def dot_tn(a, b):
+    return lax.dot_general(a, b, (((0,), (0,)), ((), ())), preferred_element_type=F32)
+
+
 def dot_exact(a, b):
     return lax.dot_general(
         a, b, (((1,), (0,)), ((), ())), precision=EXACT, preferred_element_type=F32
@@ -55,12 +59,57 @@
     return found + (pos >= start).astype(jnp.int32)
 
 
-def blocks_meet(mine, other, lengths):
-    a0 = doc_count(mine * ROWS, lengths)
-    a1 = doc_count(mine * ROWS + (ROWS - 1), lengths)
-    b0 = doc_count(other * ROWS, lengths)
-    b1 = doc_count(other * ROWS + (ROWS - 1), lengths)
-    return jnp.logical_and(a0 <= b1, b0 <= a1)
+def doc_range(block, lengths):
+    return doc_count(block * ROWS, lengths), doc_count(block * ROWS + (ROWS - 1), lengths)
+
+
+def doc_mask(block, doc, lengths):
+    pos = block * ROWS + lax.broadcasted_iota(jnp.int32, (1, ROWS), 1)
+    return (doc_count(pos, lengths) == doc).astype(F32)
+
+
+def ones_rows():
+    return (lax.broadcasted_iota(jnp.int32, (HS, ROWS), 0) < 2).astype(F32)
+
+
+def add_states(n, mine, doc, lengths, codes, partners, phis, state):
+    state[...] = jnp.zeros_like(state)
+
+    def block(k, carry):
+        other = jnp.bitwise_xor(mine, k)
+        low, high = doc_range(other, lengths)
+
+        @pl.when(jnp.logical_and(low <= doc, doc <= high))
+        def _():
+            mask = doc_mask(other, doc, lengths)
+            for h in range(HEADS):
+                lane = h * ROWS
+                expand(codes[k, 0:PLANES, lane : lane + ROWS].astype(F32), phis[h])
+                state[h] += dot_nt(phis[h][...], (partners(k, h) * mask).astype(BF16))
+
+        return carry
+
+    lax.fori_loop(0, n, block, 0)
+
+
+def split_state(state, both):
+    for row in range(0, FEATS, ROWS):
+        part = state[row : row + ROWS, :]
+        high = part.astype(BF16)
+        both[row : row + ROWS, 0:128] = high
+        both[row : row + ROWS, 128:256] = (part - high.astype(F32)).astype(BF16)
+
+
+def own_feats(pack, row, feats):
+    for h in range(HEADS):
+        picks = pack[row : row + PLANES, h * ROWS : (h + 1) * ROWS].astype(F32)
+        expand(picks, feats.at[h])
+
+
+def with_ones(values, mask):
+    rows = jnp.concatenate([values, ones_rows()], axis=0) * mask
+    rows = rows.astype(BF16)
+    return jnp.concatenate([rows, rows], axis=0)
 
 
 def same_doc(row_start, rows, col_start, cols, lengths, reverse=False):
@@ -80,12 +129,12 @@
     return factors
 
 
-def hash_feats(picks, m, lanes):
+def hash_feats(picks, m, lanes, bits=BITS):
     factors = hash_base(picks, m, lanes)
     scale = 2.0 ** (-0.5 * BITS)
     feats = [(factors[0][1] * scale) * (factors[1][1] * factors[2][1])]
     rows = {}
-    for b in range(3, BITS):
+    for b in range(3, bits):
         rows[b] = jnp.broadcast_to(picks[m * BITS + b : m * BITS + b + 1, :], (8, lanes))
         feats = feats + [f * rows[b] for f in feats]
     return feats, rows, factors
@@ -94,10 +143,14 @@
 def expand(picks, phi_ref):
     lanes = picks.shape[1]
     for m in range(HASHES):
-        feats = hash_feats(picks, m, lanes)[0]
+        feats = hash_feats(picks, m, lanes, BITS - 1)[0]
+        last = m * BITS + BITS - 1
+        row = jnp.broadcast_to(picks[last : last + 1, :], (16, lanes)).astype(BF16)
         for i in range(0, len(feats), 2):
-            both = jnp.concatenate([feats[i], feats[i + 1]], axis=0)
-            phi_ref[m * 256 + i * 8 : m * 256 + i * 8 + 16, :] = both.astype(BF16)
+            both = jnp.concatenate([feats[i], feats[i + 1]], axis=0).astype(BF16)
+            at = m * 256 + i * 8
+            phi_ref[at : at + 16, :] = both
+            phi_ref[at + 128 : at + 144, :] = both * row
 
 
 def expand_back(picks, dphi_ref, lane0, lanes):
@@ -202,23 +255,6 @@
     )
 
 
-def local_feats_body(row, pack, feat, phi):
-    for h in range(HEADS):
-        picks = pack[row : row + PLANES, h * ROWS : (h + 1) * ROWS].astype(F32)
-        expand(picks, phi)
-        feat[h] = phi[...].T
-
-
-def local_feats(row, pack):
-    return call(
-        functools.partial(local_feats_body, row),
-        "local_feats",
-        bf16(HEADS, ROWS, FEATS),
-        (pack,),
-        scratch=(pltpu.VMEM((FEATS, ROWS), BF16),),
-    )
-
-
 def window(packs, mine, low, high, n):
     def at(h):
         before = jnp.bitwise_xor(mine, jnp.maximum(mine - 1, 0))
@@ -246,53 +282,51 @@
     return mul(high, b) + mul(low, b)
 
 
-def forward_body(n, lengths, place, slot, feat_q, taps, *refs):
-    pack_in, (context, near_half, far_half, weighted, total_out) = refs[:n], refs[n : n + 5]
-    packs, phi0, phi1, phi2, acc, tot = refs[n + 5 :]
+def forward_body(n, lengths, place, slot, taps, *refs):
+    pack_in, (context, near_half, far_half, weighted, total_out, states) = refs[:n], refs[n : n + 6]
+    packs, phi0, phi1, phi2, feats, state, acc = refs[n + 6 :]
     phis = (phi0, phi1, phi2)
     mine = place[0]
     for k in range(n):
         packs[k] = pack_in[k][0:KEPT, :]
     acc[...] = jnp.zeros_like(acc)
-    tot[...] = jnp.zeros_like(tot)
-
-    def block(k, carry):
-        other = jnp.bitwise_xor(mine, k)
-
-        @pl.when(blocks_meet(mine, other, lengths))
-        def _():
-            same = same_doc(mine * ROWS, ROWS, other * ROWS, ROWS, lengths)
-            for h in range(HEADS):
-                lane = h * ROWS
-                expand(packs[k, 0:PLANES, lane : lane + ROWS].astype(F32), phis[h])
-                score = dot(feat_q[h], phis[h][...])
-                w = jnp.where(same, score * (1.0 / HASHES), 0.0)
-                tot[h] += w[:, :128] + w[:, 128:]
-                acc[h] += dot_nt(w.astype(BF16), packs[k, PLANES : PLANES + HS, lane : lane + ROWS])
-
+    own_feats(pack_in[0], KEPT, feats)
+    first, last = doc_range(mine, lengths)
+
+    def values(k, h):
+        rows = packs[k, PLANES:KEPT, h * ROWS : (h + 1) * ROWS].astype(F32)
+        return jnp.concatenate([rows, ones_rows()], axis=0)
+
+    def document(doc, carry):
+        add_states(n, mine, doc, lengths, packs, values, phis, state)
+        mask = doc_mask(mine, doc, lengths)
+        for h in range(HEADS):
+            split_state(state.at[h], states.at[doc - 1, h])
+            got = dot_tn(states[doc - 1, h], feats[h])
+            acc[h] += (got[0:128] + got[128:256]) * mask
         return carry
 
-    lax.fori_loop(0, n, block, 0)
+    lax.fori_loop(first, last + 1, document, 0)
     near = same_doc(mine * ROWS, ROWS, mine * ROWS - 128, 512, lengths)
-    ext = window(packs, mine, PLANES, PLANES + HS, n)
-    outs, sums, parts = [], [], []
+    ext = window(packs, mine, PLANES, KEPT, n)
+    outs = []
+    total_out[...] = jnp.zeros_like(total_out)
     for h in range(HEADS):
-        total = 1.0 + jnp.sum(tot[h], axis=1, keepdims=True)
+        sums = acc[h] * (1.0 / HASHES)
+        total = 1.0 + sums[HS : HS + 1]
         taps_band = jnp.where(near, band(taps[h : h + 1, :]), 0.0)
-        conv = split_dot(taps_band, ext(h), dot_nt)
-        sums.append(jnp.broadcast_to(total, (ROWS, HS)))
-        parts.append(acc[h])
-        outs.append(acc[h] / total + conv)
-    context[...] = jnp.concatenate(outs, axis=1).astype(BF16)
+        conv = split_dot(taps_band, ext(h), lambda a, b: dot_nt(b, a))
+        total_out[h : h + 1, :] = total
+        weighted[h * HS : (h + 1) * HS, :] = sums[0:HS]
+        outs.append(sums[0:HS] / total + conv)
+    context[...] = jnp.concatenate(outs, axis=0).T.astype(BF16)
     half = ROWS // 2
     first = slot[0] >> 1
     near_half[...] = context[pl.ds(pl.multiple_of(first * half, 16), half), :]
     far_half[...] = context[pl.ds(pl.multiple_of((1 - first) * half, 16), half), :]
-    weighted[...] = jnp.concatenate(parts, axis=1)
-    total_out[...] = jnp.concatenate(sums, axis=1)
-
-
-def forward(lengths, place, slot, feat_q, taps, packs):
+
+
+def forward(lengths, place, slot, taps, packs):
     n = len(packs)
     wide = HEADS * HS
     return call(
@@ -302,21 +336,36 @@
             bf16(ROWS, wide),
             bf16(ROWS // 2, wide),
             bf16(ROWS // 2, wide),
-            f32(ROWS, wide),
-            f32(ROWS, wide),
-        ),
-        (lengths, place, slot, feat_q, taps, *packs),
+            f32(wide, ROWS),
+            f32(8, ROWS),
+            bf16(lengths.shape[0], HEADS, FEATS, 256),
+        ),
+        (lengths, place, slot, taps, *packs),
         smem=3,
         scratch=(
-            pltpu.VMEM((n, PLANES + HS, HEADS * ROWS), BF16),
+            pltpu.VMEM((n, KEPT, HEADS * ROWS), BF16),
             pltpu.VMEM((FEATS, ROWS), BF16),
             pltpu.VMEM((FEATS, ROWS), BF16),
             pltpu.VMEM((FEATS, ROWS), BF16),
-            pltpu.VMEM((HEADS, ROWS, HS), F32),
-            pltpu.VMEM((HEADS, ROWS, 128), F32),
+            pltpu.VMEM((HEADS, FEATS, ROWS), BF16),
+            pltpu.VMEM((HEADS, FEATS, 128), F32),
+            pltpu.VMEM((HEADS, 128, ROWS), F32),
         ),
         us=9,
     )
+
+
+GROUP = 16
+
+
+def grad_rows(grads, h):
+    base = HEADS * HS + h * GROUP
+    return grads[h * HS : (h + 1) * HS].astype(F32), grads[base : base + GROUP].astype(F32)
+
+
+def grad_partners(grads, h):
+    rows, side = grad_rows(grads, h)
+    return jnp.concatenate([rows, side, jnp.zeros((HS - GROUP, rows.shape[1]), F32)], axis=0)
 
 
 def unit_back(code_grad, tan, raw, planes_t):
@@ -342,33 +391,24 @@
 
 
 def query_back_body(
-    n, lengths, place, grads, row_totals, tan, raw, choose_back, planes_t, weight, *refs
+    n, lengths, place, grads, states, tan, raw, choose_back, planes_t, weight, *refs
 ):
     pack_in, (grad_out, input_out, taps_out) = refs[:n], refs[n : n + 3]
-    packs, phi0, phi1, phi2, dphi = refs[n + 3 :]
-    phis = (phi0, phi1, phi2)
+    packs, dphi = refs[n + 3 :]
     mine = place[0]
     for k in range(n):
-        packs[k] = pack_in[k][0:KEPT, :]
+        packs[k] = pack_in[k][PLANES:KEPT, :]
     dphi[...] = jnp.zeros_like(dphi)
-
-    def block(k, carry):
-        other = jnp.bitwise_xor(mine, k)
-
-        @pl.when(blocks_meet(mine, other, lengths))
-        def _():
-            same = same_doc(other * ROWS, ROWS, mine * ROWS, ROWS, lengths)
-            for h in range(HEADS):
-                lane = h * ROWS
-                expand(packs[k, 0:PLANES, lane : lane + ROWS].astype(F32), phis[h])
-                values = packs[k, PLANES : PLANES + HS, lane : lane + ROWS].T
-                dw = dot_nt(values, grads[:, h * HS : (h + 1) * HS]) + row_totals[h : h + 1, :]
-                dw = jnp.where(same, dw, 0.0).astype(BF16)
-                dphi[h] += dot(phis[h][...], dw)
-
+    first, last = doc_range(mine, lengths)
+
+    def document(doc, carry):
+        mask = doc_mask(mine, doc, lengths)
+        for h in range(HEADS):
+            rows = (grad_partners(grads[...], h) * mask).astype(BF16)
+            dphi[h] += dot(states[doc - 1, h], jnp.concatenate([rows, rows], axis=0))
         return carry
 
-    lax.fori_loop(0, n, block, 0)
+    lax.fori_loop(first, last + 1, document, 0)
     raw_grad = codes_to_raw(dphi, pack_in[0], KEPT, tan, raw, choose_back, planes_t)
     turned = stacked(raw_grad).astype(BF16)
     grad_out[...] = turned
@@ -379,14 +419,13 @@
     )
     flip = (turn == 511).astype(F32)
     flip_low = flip.astype(BF16)
-    ext = window(packs, mine, PLANES, PLANES + HS, n)
-    side = grads[:, 3 * HS : 4 * HS].astype(F32)
+    ext = window(packs, mine, 0, HS, n)
     tap_rows = []
     for h in range(HEADS):
-        total = side[:, HEADS + h : HEADS + h + 1]
-        context_grad = (grads[:, h * HS : (h + 1) * HS].astype(F32) * total).astype(BF16)
+        rows, side = grad_rows(grads[...], h)
+        context_grad = (rows * side[2:3]).astype(BF16)
         flipped = dot(ext(h), flip_low).astype(BF16)
-        cross = jnp.where(near_rev, dot(context_grad, flipped), 0.0)
+        cross = jnp.where(near_rev, dot_tn(context_grad, flipped), 0.0)
         cross = pltpu.roll(cross, 0, 1, stride=1, stride_axis=0)
         tap_rows.append(jnp.sum(cross, axis=0, keepdims=True))
     tap_rows.append(jnp.zeros((8 - HEADS, 512), F32))
@@ -403,13 +442,10 @@
         (*ins[:-1], *packs),
         smem=2,
         scratch=(
-            pltpu.VMEM((n, PLANES + HS, HEADS * ROWS), BF16),
-            pltpu.VMEM((FEATS, ROWS), BF16),
-            pltpu.VMEM((FEATS, ROWS), BF16),
-            pltpu.VMEM((FEATS, ROWS), BF16),
+            pltpu.VMEM((n, HS, HEADS * ROWS), BF16),
             pltpu.VMEM((HEADS, FEATS, ROWS), F32),
         ),
-        us=9,
+        us=6,
     )
 
 
@@ -418,7 +454,6 @@
     lengths,
     place,
     slot,
-    feat_k,
     tan,
     raw,
     taps_back,
@@ -433,8 +468,8 @@
 ):
     pack_in, grad_in = refs[:n], refs[n : 2 * n]
     pack = pack_in[0]
-    turned_out, input_out = refs[2 * n : 2 * n + 2]
-    picks, grads, phi0, phi1, phi2, dphi, acc, inputs = refs[2 * n + 2 :]
+    turned_out, input_mine, input_other = refs[2 * n : 2 * n + 3]
+    picks, grads, phi0, phi1, phi2, feats, state, both, dphi, acc, inputs = refs[2 * n + 3 :]
     phis = (phi0, phi1, phi2)
     mine = place[0]
     for k in range(n):
@@ -442,77 +477,75 @@
         grads[k] = grad_in[k][...]
     dphi[...] = jnp.zeros_like(dphi)
     acc[...] = jnp.zeros_like(acc)
-
-    def block(k, carry):
-        other = jnp.bitwise_xor(mine, k)
-
-        @pl.when(blocks_meet(mine, other, lengths))
-        def _():
-            same = same_doc(mine * ROWS, ROWS, other * ROWS, ROWS, lengths)
-            same_t = same_doc(other * ROWS, ROWS, mine * ROWS, ROWS, lengths)
-            for h in range(HEADS):
-                lane = h * ROWS
-                expand(picks[k, :, lane : lane + ROWS].astype(F32), phis[h])
-                score = dot(feat_k[h], phis[h][...])
-                w = jnp.where(same, score * (1.0 / HASHES), 0.0).astype(BF16)
-                grad = grads[k, :, h * HS : (h + 1) * HS]
-                acc[h] += dot(w, grad)
-                values_t = pack[PLANES : PLANES + HS, lane : lane + ROWS]
-                side = grads[k, :, 3 * HS : 4 * HS].astype(F32)
-                row_total = side[:, h : h + 1] + side[:, 2 * HEADS + h : 2 * HEADS + h + 1]
-                dw = dot(grad, values_t) + row_total
-                dw = jnp.where(same_t, dw, 0.0).astype(BF16)
-                dphi[h] += dot(phis[h][...], dw)
-
+    own_feats(pack, 0, feats)
+    first, last = doc_range(mine, lengths)
+
+    def document(doc, carry):
+        add_states(
+            n, mine, doc, lengths, picks, lambda k, h: grad_partners(grads[k], h), phis, state
+        )
+        mask = doc_mask(mine, doc, lengths)
+        for h in range(HEADS):
+            split_state(state.at[h], both)
+            values = pack[PLANES:KEPT, h * ROWS : (h + 1) * ROWS].astype(F32)
+            dphi[h] += dot(both[...], with_ones(values, mask))
+            got = dot_tn(both[...], feats[h])
+            acc[h] += (got[0:HS] + got[128 : 128 + HS]) * (mask * (1.0 / HASHES))
         return carry
 
-    lax.fori_loop(0, n, block, 0)
-    raw_grad = codes_to_raw(dphi, pack_in[0], 0, tan, raw, choose_back, planes_t)
+    lax.fori_loop(first, last + 1, document, 0)
+    raw_grad = codes_to_raw(dphi, pack, 0, tan, raw, choose_back, planes_t)
     key_turned = stacked(raw_grad).astype(BF16)
     key_rows = key_turned.astype(F32).T
 
     before = jnp.bitwise_xor(mine, jnp.maximum(mine - 1, 0))
     after = jnp.bitwise_xor(mine, jnp.minimum(mine + 1, n - 1))
     near = same_doc(mine * ROWS, ROWS, mine * ROWS - 128, 512, lengths)
-    ext = jnp.concatenate([grads[before, 128:, :], grads[0], grads[after, :128, :]], axis=0)
-    side = ext[:, 3 * HS : 4 * HS].astype(F32)
+    ext = jnp.concatenate([grads[before, :, 128:], grads[0], grads[after, :, :128]], axis=1)
     outs = []
     for h in range(HEADS):
-        total = side[:, HEADS + h : HEADS + h + 1]
-        context_grad = (ext[:, h * HS : (h + 1) * HS].astype(F32) * total).astype(BF16)
+        rows, side = grad_rows(ext, h)
+        context_grad = (rows * side[2:3]).astype(BF16)
         taps_band = jnp.where(near, band(taps_back[h : h + 1, :]), 0.0)
-        outs.append(acc[h] + split_dot(taps_band, context_grad, dot))
-    value_rows = jnp.concatenate(outs, axis=1).astype(BF16)
+        outs.append(acc[h] + split_dot(taps_band, context_grad, lambda a, b: dot_nt(b, a)))
+    value_turned = jnp.concatenate(outs, axis=0).astype(BF16)
+    value_rows = value_turned.astype(F32).T.astype(BF16)
     wide = HEADS * HS
     turned_out[0:wide, :] = query_turned[...]
     turned_out[wide : 2 * wide, :] = key_turned
-    turned_out[2 * wide :, :] = value_rows.astype(F32).T.astype(BF16)
+    turned_out[2 * wide :, :] = value_turned
     inputs[...] = query_input[...] + dot(key_rows.astype(BF16), wk[...]) + dot(value_rows, wv[...])
     rows = dh1.shape[0]
     own = pl.ds(pl.multiple_of(slot[0] * rows, 16), rows)
     inputs[own, :] = inputs[own, :] + dh1[...]
-    input_out[...] = inputs[...].astype(BF16)
-
-
-def key_back(ins, picks, grads):
-    n = len(picks)
+    half = input_mine.shape[0]
+    kept = slot[0] >> 1
+    input_mine[...] = inputs[pl.ds(pl.multiple_of(kept * half, 16), half), :].astype(BF16)
+    input_other[...] = inputs[pl.ds(pl.multiple_of((1 - kept) * half, 16), half), :].astype(BF16)
+
+
+def key_back(ins, packs, grads):
+    n = len(packs)
     return call(
         functools.partial(key_back_body, n),
         "key_back",
-        (bf16(3 * HEADS * HS, ROWS), bf16(ROWS, D)),
-        (*ins, *picks, *grads),
+        (bf16(3 * HEADS * HS, ROWS), *[bf16(ROWS // 2, D)] * 2),
+        (*ins, *packs, *grads),
         smem=3,
         scratch=(
             pltpu.VMEM((n, PLANES, HEADS * ROWS), BF16),
-            pltpu.VMEM((n, ROWS, 4 * HS), BF16),
+            pltpu.VMEM((n, HEADS * (HS + GROUP), ROWS), BF16),
             pltpu.VMEM((FEATS, ROWS), BF16),
             pltpu.VMEM((FEATS, ROWS), BF16),
             pltpu.VMEM((FEATS, ROWS), BF16),
+            pltpu.VMEM((HEADS, FEATS, ROWS), BF16),
+            pltpu.VMEM((HEADS, FEATS, 128), F32),
+            pltpu.VMEM((FEATS, ROWS), BF16),
             pltpu.VMEM((HEADS, FEATS, ROWS), F32),
-            pltpu.VMEM((HEADS, ROWS, HS), F32),
+            pltpu.VMEM((HEADS, HS, ROWS), F32),
             pltpu.VMEM((ROWS, D), F32),
         ),
-        us=15,
+        us=12,
     )
 
 
@@ -765,28 +798,20 @@
 
 
 def split_body(parts, chunk, weighted, total, *refs):
-    pieces, (grad_pack, row_totals), (whole,) = refs[:parts], refs[parts : parts + 2], refs[parts + 2 :]
+    pieces, grad_pack, whole = refs[:parts], refs[parts], refs[parts + 1]
     take_chunks(chunk[0], pieces, whole)
-    dctx = whole[...].astype(F32)
+    dctx = whole[...].astype(F32).T
     wide = HEADS * HS
-    each = total[...]
-    grad_pack[:, 0:wide] = (dctx / each).astype(BF16)
-    product = dctx * weighted[...]
-    cols = []
     for h in range(HEADS):
-        norm = each[:, h * HS : h * HS + 1]
-        inner = jnp.sum(product[:, h * HS : (h + 1) * HS], axis=1, keepdims=True)
-        cols.append((-inner / (norm * norm), norm))
-    lane = lax.broadcasted_iota(jnp.int32, (ROWS, 128), 1)
-    side = jnp.zeros((ROWS, 128), F32)
-    for h, (grad, norm) in enumerate(cols):
+        norm = total[h : h + 1, :]
+        rows = dctx[h * HS : (h + 1) * HS]
+        grad_pack[h * HS : (h + 1) * HS, :] = (rows / norm).astype(BF16)
+        inner = jnp.sum(rows * weighted[h * HS : (h + 1) * HS, :], axis=0, keepdims=True)
+        grad = -inner / (norm * norm)
         high = grad.astype(BF16).astype(F32)
-        side = jnp.where(lane == h, high, side)
-        side = jnp.where(lane == HEADS + h, norm, side)
-        side = jnp.where(lane == 2 * HEADS + h, grad - high, side)
-        side = jnp.where(lane == 64 + h, grad, side)
-    grad_pack[:, wide : wide + 64] = side[:, 0:64].astype(BF16)
-    row_totals[...] = side.T[64:72, :]
+        side = [high, grad - high, norm, jnp.zeros((GROUP - 3, ROWS), F32)]
+        base = wide + h * GROUP
+        grad_pack[base : base + GROUP, :] = jnp.concatenate(side, axis=0).astype(BF16)
 
 
 def feed_grads_body(place, slot, low_mine, low_got, down_mine, down_got, up, up_shift, down, half_mine, half_other, sums, low_all, down_all):
@@ -945,8 +970,11 @@
     out[...] = (mine[...].astype(F32) + other[...].astype(F32)).astype(BF16)
 
 
-def tokens_out_body(mine, other, out):
-    out[...] = mine[...].astype(F32) + other[...].astype(F32)
+def tokens_out_body(slot, mine, other, out):
+    half = mine.shape[0]
+    kept = slot[0] >> 1
+    out[pl.ds(pl.multiple_of(kept * half, 16), half), :] = mine[...].astype(F32)
+    out[pl.ds(pl.multiple_of((1 - kept) * half, 16), half), :] = other[...].astype(F32)
 
 
 def on_device(
@@ -997,12 +1025,13 @@
     raw_q, raw_k, tan_q, tan_k, pack = project(
         tokens, wq, query_shift, wk, key_shift, wv, value_shift, hyperplanes, choose
     )
-    far_mixer, pack = after(far_mixer, pack)
+    (far_mixer, taps, taps_back, planes_t), pack = after(
+        (far_mixer, taps, taps_back, planes_t), pack
+    )
     other_mixer = swap(far_mixer, "seq", 1)
     packs = over_seq(pack)
-    feat_q = local_feats(KEPT, pack)
-    context, near_half, far_half, weighted, total = forward(
-        doc_lengths, place, slot, feat_q, taps, packs
+    context, near_half, far_half, weighted, total, states = forward(
+        doc_lengths, place, slot, taps, packs
     )
     contexts = [
         near_half,
@@ -1010,7 +1039,7 @@
         hid_swap(far_half, 2),
         hid_swap(far_half, 3),
     ]
-    got, context = after(got, context)
+    got, contexts[1] = after(got, contexts[1])
     other = swap(got, "seq", 1)
     first_mine, normed_mine, inverse_mine, low, slope, keep, send, mixers = call(
         functools.partial(feed_body, parts),
@@ -1071,8 +1100,6 @@
         ),
         smem=1,
     )
-    pack_later, dh2 = after(pack, dh2)
-    feat_k, slope = after(local_feats(0, pack_later), slope)
     down_half, keep, send = call(
         feed_back_body,
         "feed_back",
@@ -1090,7 +1117,7 @@
         ),
         smem=2,
         scratch=(pltpu.VMEM((half, D), F32), pltpu.VMEM((2, D, units), BF16)),
-        us=4,
+        us=0.5,
     )
     token_blocks, mixers = after(token_blocks, mixers)
     first_back = call(
@@ -1126,10 +1153,10 @@
         us=6,
     )
     pieces, feed_other = after(pieces, feed_other)
-    grad_pack, row_totals = call(
+    grad_pack = call(
         functools.partial(split_body, parts),
         "split",
-        (bf16(ROWS, 4 * HS), f32(8, ROWS)),
+        bf16(HEADS * (HS + GROUP), ROWS),
         (slot, weighted, total, *pieces),
         smem=1,
         scratch=(pltpu.VMEM((ROWS, wide), BF16),),
@@ -1138,12 +1165,12 @@
     grad_blocks = cross_chips(grad_pack)
     feed_pieces = scatter_chips(feed_mine, swap(feed_other, "seq", 1), place, n)
     feed_got = [swap(feed_pieces[k], "seq", 2 * k) for k in range(1, n // 2)]
-    feed_own, row_totals = after(feed_pieces[0], row_totals)
+    feed_own, tan_q = after(feed_pieces[0], tan_q)
     query_turned, query_input, tap_rows = query_back(
         doc_lengths,
         place,
         grad_pack,
-        row_totals,
+        states,
         tan_q,
         raw_q,
         choose_back,
@@ -1172,7 +1199,6 @@
             doc_lengths,
             place,
             slot,
-            feat_k,
             tan_k,
             raw_k,
             taps_back,
@@ -1188,19 +1214,29 @@
         grad_packs,
     )
     last, (small_got, feed_chips) = after(last, (small_got, feed_chips))
-    near_tokens = hid_swap(last[1], 2)
+    near_tokens = hid_swap(last[2], 2)
     blocks = over_seq(last[0])
-    both = call(tokens_sum_body, "tokens_sum", bf16(ROWS, D), (last[1], near_tokens))
+
+    def tokens_sum(mine, other):
+        return call(tokens_sum_body, "tokens_sum", bf16(half, D), (mine, other), us=0.3)
+
+    both = tokens_sum(last[1], near_tokens)
+    token_blocks, both = after(token_blocks, both)
     small_chip = call(halve_all_body, "halve_small", bf16(*small_mine.shape), (small_mine, small_got))
     both, small_chip = after(both, small_chip)
     feed_full = call(
-        join_body, "join", bf16(feed_half, D), (place, settled, *feed_chips), smem=1
-    )
-    tokens_grad = call(tokens_out_body, "tokens_out", f32(ROWS, D), (both, hid_swap(both, 1)))
+        join_body, "join", bf16(feed_half, D), (place, settled, *feed_chips), smem=1, us=0.3
+    )
+    summed = tokens_sum(both, hid_swap(both, 1))
+    summed, tokens_first = after(summed, tokens_later)
+    tokens_grad = call(
+        tokens_out_body, "tokens_out", f32(ROWS, D), (slot, summed, hid_swap(summed, 2)), smem=1
+    )
     feed_sums = (feed_full, swap(feed_full, "seq", 1))
     small_full = total_chips(small_chip, chip_swaps(small_chip, n), place)
     small_sums = (small_full, swap(small_full, "seq", 1))
     token_blocks = from_partner(token_blocks)
+    token_blocks[0] = tokens_first
     down_grad, up_grad = call(
         finish_feed_body,
         "finish_feed",
@@ -1223,7 +1259,7 @@
         (*[f32(wide, D)] * 3, *[f32(wide)] * 3),
         (*blocks, *token_blocks),
         scratch=(pltpu.VMEM((3 * wide, n * ROWS), BF16), pltpu.VMEM((n * ROWS, D), BF16)),
-        us=4,
+        us=0.3,
     )
     return (
         layer_out,

time: 233 us -> 209 us (0.90)
  starting transfers between devices: 75.4 us -> 52.8 us
  Pallas kernels: 93.1 us -> 86.7 us
  waiting for transfers between devices: 47.1 us -> 51.3 us
    ppermute x60 -> x61, starting transfers between devices: 71.2 us -> 48.6 us  [swap(): return lax.ppermute(value, axis, [(i, i ^ k) for i in range(n)])]
    pallas_call x24 -> x23, Pallas kernels: 93.1 us -> 86.7 us  [call(): pl.pallas_call(body, out_shape=outs, in_specs=[SMEM] * smem + [VMEM] * (l...]
    ppermute x60 -> x61, waiting for transfers between devices: 41.7 us -> 48.1 us  [swap(): return lax.ppermute(value, axis, [(i, i ^ k) for i in range(n)])]
  transfers between devices with their start and end apart: 61 -> 62, of which waited for: 16 -> 25; matrix products, arithmetic and copies ran while one was open for 1% -> 1% of each run, Pallas kernels for 36% -> 37%
where the time goes in v4:
time: 209 us
  Pallas kernels  86.7 us (41%)
  starting transfers between devices  52.8 us (25%)
  waiting for transfers between devices  51.3 us (25%)
  local copies, waits for them, and re-layouts  16.5 us (8%)
    pallas_call x23, Pallas kernels, call(): pl.pallas_call(body, out_shape=outs, in_specs=[SMEM] * smem + [VMEM] * (l...  86.7 us
    ppermute x61, starting transfers between devices, swap(): return lax.ppermute(value, axis, [(i, i ^ k) for i in range(n)])  48.6 us
    ppermute x61, waiting for transfers between devices, swap(): return lax.ppermute(value, axis, [(i, i ^ k) for i in range(n)])  48.1 us
    unnamed x139, local copies, waits for them, and re-layouts  15 us
  transfers between devices with their start and end apart: 62, of which 25 were waited for; matrix products, arithmetic and copies ran while one was open for 1% of the time, Pallas kernels for 37%

profile of v4, /device:TPU:0, one launch (start us, length us, event | category | flops | bytes accessed | tf_op | source)
XLA Modules:
  0.0 209.1 jit_solution(9679425604747603938)
XLA Ops:
  0.7 4.1 %collective-permute-start = (bf16[192,768]{1,0:T(8,128)(2,1)}, bf16[192,768]{1,0:T(8,128)(2,1)S(1)}, u32[]{:S(2)}, u32[]{:S(2)}) collective-permute-start(bf16[192,768]{1,0:T(8,128)(2,1)} %refs_9_.1), channel_id=1, source_target_pairs={{0,2},{1,3},{2,0},{3,1},{4,7},{5,6},{6,5},{7,4},{8,10},{9,11},{10,... | collective-permute-start | bytes 884744 | tf_op jit(solution)/shard_map/ppermute | solution.py:607
  4.8 2.9 %bundle.1 = bf16[880,768]{1,0:T(8,128)(2,1)} custom-call(s32[1]{0:T(128)} %bitcast.place, bf16[768,768]{1,0:T(8,128)(2,1)} %up.5, bf16[768,768]{1,0:T(8,128)(2,1)} %down.5, bf16[192,768]{1,0:T(8,128)(2,1)} %refs_9_.1, f32[768]{0:T(1024)} %up_shift.1), custom_call_target="tpu_custom_call" | custom-call | flops 20000000000 | bytes 100000 | tf_op jit(solution)/shard_map/bundle/pallas_call | solution.py:218
  12.2 3.3 %project.1 = (f32[64,768]{1,0:T(8,128)}, f32[64,768]{1,0:T(8,128)}, f32[32,768]{1,0:T(8,128)}, f32[32,768]{1,0:T(8,128)}, bf16[128,768]{1,0:T(8,128)(2,1)}) custom-call(bf16[256,768]{1,0:T(8,128)(2,1)} %refs_8_, bf16[192,768]{1,0:T(8,128)(2,1)} %bitcast.9, f32[192]{0:T(256)} %bq.1, bf16[192,768]{1,0:T(8,128)(2,1)} %bitcast.11, f32[192]{0:T(256)} %bk.1, ...), custom_call_target="tpu_custom_call" | custom-call | flops 100000000 | bytes 100000 | tf_op jit(solution)/shard_map/project/pallas_call | solution.py:218
  15.4 3.2 %collective-permute-done.refs_10_ = bf16[192,768]{1,0:T(8,128)(2,1)S(1)} collective-permute-done((bf16[192,768]{1,0:T(8,128)(2,1)}, bf16[192,768]{1,0:T(8,128)(2,1)S(1)}, u32[]{:S(2)}, u32[]{:S(2)}) %collective-permute-start) | collective-permute-done | bytes 294944 | tf_op jit(solution)/shard_map/ppermute | solution.py:607
  18.6 2.4 %collective-permute-start.6 = (bf16[128,768]{1,0:T(8,128)(2,1)}, bf16[128,768]{1,0:T(8,128)(2,1)S(1)}, u32[]{:S(2)}, u32[]{:S(2)}) collective-permute-start(bf16[128,768]{1,0:T(8,128)(2,1)} %get-tuple-element.139.refs_0_), channel_id=1, source_target_pairs={{0,24},{4,28},{8,16},{12,20},{16,8},{20,12},{24,0},{28,4},{1,25},{... | collective-permute-start | bytes 589832 | tf_op jit(solution)/shard_map/ppermute | solution.py:572
  22.1 3.3 %collective-permute-done.6.refs_6_ = bf16[128,768]{1,0:T(8,128)(2,1)S(1)} collective-permute-done((bf16[128,768]{1,0:T(8,128)(2,1)}, bf16[128,768]{1,0:T(8,128)(2,1)S(1)}, u32[]{:S(2)}, u32[]{:S(2)}) %collective-permute-start.6) | collective-permute-done | bytes 196640 | tf_op jit(solution)/shard_map/ppermute | solution.py:572
  29.9 8.6 %attend.1 = (bf16[256,192]{1,0:T(8,128)(2,1)}, bf16[128,192]{1,0:T(8,128)(2,1)}, bf16[128,192]{1,0:T(8,128)(2,1)}, f32[192,256]{1,0:T(8,128)}, f32[8,256]{1,0:T(8,128)}, /*index=5*/bf16[2,3,1024,256]{3,2,1,0:T(8,128)(2,1)}) custom-call(s32[2]{0:T(128)} %lengths.5, s32[1]{0:T(128)} %bitcast.place, s32[1]{0:T(128)} %bitcast.1.slot.chunk, f32[8,512]{1,0:T(8,128)} %pad.7.taps, ...), custom_call_target="tpu_custom_call" | custom-call | flops 8999999488 | bytes 100000 | tf_op jit(solution)/shard_map/attend/pallas_call | solution.py:218
  38.5 2.9 %collective-permute-start.9 = (bf16[128,192]{1,0:T(8,128)(2,1)}, bf16[128,192]{1,0:T(8,128)(2,1)S(1)}, u32[]{:S(2)}, u32[]{:S(2)}) collective-permute-start(bf16[128,192]{1,0:T(8,128)(2,1)} %get-tuple-element.141.refs_12_), channel_id=1, source_target_pairs={{0,2},{1,3},{2,0},{3,1},{4,6},{5,7},{6,4},{7,5},{8,10},{9,11},{10,... | collective-permute-start | bytes 147464 | tf_op jit(solution)/shard_map/ppermute | solution.py:572
  41.4 2.8 %collective-permute-done.9.refs_13_ = bf16[128,192]{1,0:T(8,128)(2,1)S(1)} collective-permute-done((bf16[128,192]{1,0:T(8,128)(2,1)}, bf16[128,192]{1,0:T(8,128)(2,1)S(1)}, u32[]{:S(2)}, u32[]{:S(2)}) %collective-permute-start.9) | collective-permute-done | bytes 49184 | tf_op jit(solution)/shard_map/ppermute | solution.py:572
  45.4 3.3 %collective-permute-start.13 = (bf16[128,192]{1,0:T(8,128)(2,1)}, bf16[128,192]{1,0:T(8,128)(2,1)S(1)}, u32[]{:S(2)}, u32[]{:S(2)}) collective-permute-start(bf16[128,192]{1,0:T(8,128)(2,1)} %get-tuple-element.145), channel_id=1, source_target_pairs={{0,3},{1,2},{2,1},{3,0},{4,7},{5,6},{6,5},{7,4},{8,11},{9,10},{10,... | collective-permute-start | bytes 147464 | tf_op jit(solution)/shard_map/ppermute | solution.py:572
  48.7 3.5 %collective-permute-done.13.refs_15_ = bf16[128,192]{1,0:T(8,128)(2,1)S(1)} collective-permute-done((bf16[128,192]{1,0:T(8,128)(2,1)}, bf16[128,192]{1,0:T(8,128)(2,1)S(1)}, u32[]{:S(2)}, u32[]{:S(2)}) %collective-permute-start.13) | collective-permute-done | bytes 49184 | tf_op jit(solution)/shard_map/ppermute | solution.py:572
  54.9 5.7 %feed.1 = (f32[64,768]{1,0:T(8,128)}, f32[64,768]{1,0:T(8,128)}, f32[64,128]{1,0:T(8,128)}, bf16[128,768]{1,0:T(8,128)(2,1)}, f32[128,1536]{1,0:T(8,128)}, /*ind...) custom-call(s32[1]{0:T(128)} %bitcast.place, s32[1]{0:T(128)} %bitcast.1.slot.chunk, ...), custom_call_target="tpu_custom_call" | custom-call | flops 5000000000 | bytes 100000 | tf_op jit(solution)/shard_map/feed/pallas_call | solution.py:218
  61.1 2.4 %collective-permute-start.21 = (bf16[256,768]{1,0:T(8,128)(2,1)S(1)}, bf16[256,768]{1,0:T(8,128)(2,1)S(1)}, u32[]{:S(2)}, u32[]{:S(2)}) collective-permute-start(bf16[256,768]{1,0:T(8,128)(2,1)S(1)} %copy-done), channel_id=1, source_target_pairs={{0,24},{4,28},{8,16},{12,20},{16,8},{20,12},{24,0},{28,4},{1,25},{... | collective-permute-start | bytes 1179656 | tf_op jit(solution)/shard_map/ppermute | solution.py:572
  65.6 2.4 %collective-permute-done.15.got = bf16[64,768]{1,0:T(8,128)(2,1)S(1)} collective-permute-done((bf16[64,768]{1,0:T(8,128)(2,1)}, bf16[64,768]{1,0:T(8,128)(2,1)S(1)}, u32[]{:S(2)}, u32[]{:S(2)}) %collective-permute-start.15) | collective-permute-done | bytes 98336 | tf_op jit(solution)/shard_map/ppermute | solution.py:572
  68.6 2.4 %second_norm.1 = (bf16[80,768]{1,0:T(8,128)(2,1)}, f32[64,768]{1,0:T(8,128)}, bf16[64,768]{1,0:T(8,128)(2,1)}) custom-call(s32[1]{0:T(128)} %bitcast.1.slot.chunk, f32[64,768]{1,0:T(8,128)} %get-tuple-element.148.first, f32[256,768]{1,0:T(8,128)} %out_grad.1, f32[768]{0:T(1024)} %down_shift.1, f32[768]{0:T(1024)} %gain.2, f32[768]{0:T(1024)} %shift.3, ...), custom_call_target="tpu_custom_call" | custom-call | flops 2000000000 | bytes 100000 | tf_op jit(solution)/shard_map/second_norm/pallas_call | solution.py:218
  71.0 6.5 %collective-permute-done.16.low_got = bf16[64,768]{1,0:T(8,128)(2,1)S(1)} collective-permute-done((bf16[64,768]{1,0:T(8,128)(2,1)}, bf16[64,768]{1,0:T(8,128)(2,1)S(1)}, u32[]{:S(2)}, u32[]{:S(2)}) %collective-permute-start.16) | collective-permute-done | bytes 98336 | tf_op jit(solution)/shard_map/ppermute | solution.py:572
  78.1 5.4 %feed_back.1 = (bf16[128,768]{1,0:T(8,128)(2,1)}, f32[64,768]{1,0:T(8,128)}, bf16[64,768]{1,0:T(8,128)(2,1)}) custom-call(s32[1]{0:T(128)} %bitcast.place, s32[1]{0:T(128)} %bitcast.1.slot.chunk, f32[128,1536]{1,0:T(8,128)} %get-tuple-element.147.slope, bf16[768,768]{1,0:T(8,128)(2,1)} %up.5, bf16[768,768]{1,0:T(8,128)(2,1)} %down.5, ...), custom_call_target="tpu_custom_call" | custom-call | flops 500000000 | bytes 100000 | tf_op jit(solution)/shard_map/feed_back/pallas_call | solution.py:218
  83.5 2.8 %collective-permute-start.14 = (bf16[128,768]{1,0:T(8,128)(2,1)S(1)}, bf16[128,768]{1,0:T(8,128)(2,1)S(1)}, u32[]{:S(2)}, u32[]{:S(2)}) collective-permute-start(bf16[128,768]{1,0:T(8,128)(2,1)S(1)} %copy-done.41), channel_id=1, source_target_pairs={{0,1},{1,0},{2,3},{3,2},{4,5},{5,4},{6,7},{7,6},{8,9},{9,8},{10,11... | collective-permute-start | bytes 589832 | tf_op jit(solution)/shard_map/ppermute | solution.py:572
  86.4 4.6 %collective-permute-done.18.got = bf16[64,768]{1,0:T(8,128)(2,1)S(1)} collective-permute-done((bf16[64,768]{1,0:T(8,128)(2,1)}, bf16[64,768]{1,0:T(8,128)(2,1)S(1)}, u32[]{:S(2)}, u32[]{:S(2)}) %collective-permute-start.18) | collective-permute-done | bytes 98336 | tf_op jit(solution)/shard_map/ppermute | solution.py:572
  91.6 2.9 %first_norm_back.1 = (f32[64,768]{1,0:T(8,128)}, bf16[160,768]{1,0:T(8,128)(2,1)}, bf16[64,192]{1,0:T(8,128)(2,1)}, bf16[64,192]{1,0:T(8,128)(2,1)}, bf16[64,192]{1,0:T(8,128)(2,1)}, /*index=5*/bf16[64,192]{1,0:T(8,128)(2,1)}) custom-call(f32[64,768]{1,0:T(8,128)} %get-tuple-element.155.grad, f32[64,768]{1,0:T(8,128)} %get-tuple-element.156.normed, ...), custom_call_target="tpu_custom_call" | custom-call | flops 3000000000 | bytes 100000 | tf_op jit(solution)/shard_map/first_norm_back/pallas_call | solution.py:218
  96.4 2.5 %collective-permute-start.24 = (bf16[64,192]{1,0:T(8,128)(2,1)}, bf16[64,192]{1,0:T(8,128)(2,1)S(1)}, u32[]{:S(2)}, u32[]{:S(2)}) collective-permute-start(bf16[64,192]{1,0:T(8,128)(2,1)} %get-tuple-element.170), channel_id=1, source_target_pairs={{0,3},{1,2},{2,1},{3,0},{4,7},{5,6},{6,5},{7,4},{8,11},{9,10},{10,... | collective-permute-start | bytes 73736 | tf_op jit(solution)/shard_map/ppermute | solution.py:572
  100.3 5.2 %feed_grads.1 = (bf16[768,768]{1,0:T(8,128)(2,1)}, bf16[768,768]{1,0:T(8,128)(2,1)}, f32[8,768]{1,0:T(8,128)}) custom-call(s32[1]{0:T(128)} %bitcast.place, s32[1]{0:T(128)} %bitcast.1.slot.chunk, bf16[128,768]{1,0:T(8,128)(2,1)} %get-tuple-element.146.low_mine, bf16[128,768]{1,0:T(8,128)(2,1)} %copy-done.44, bf16[128,768]{1,0:T(8,128)(2,1)} %get-tuple-element.153.down_mine, ...), custom_call_target="tpu_custom_call" | custom-call | flops 6000000000 | bytes 100000 | tf_op jit(solution)/shard_map/feed_grads/pallas_call | solution.py:218
  110.0 2.7 %collective-permute-start.30 = (bf16[240,256]{1,0:T(8,128)(2,1)}, bf16[240,256]{1,0:T(8,128)(2,1)S(1)}, u32[]{:S(2)}, u32[]{:S(2)}) collective-permute-start(bf16[240,256]{1,0:T(8,128)(2,1)} %split.1.grads.refs_8_), channel_id=1, source_target_pairs={{0,16},{4,20},{8,24},{12,28},{16,0},{20,4},{24,8},{28,12},{1,17},{... | collective-permute-start | bytes 368648 | tf_op jit(solution)/shard_map/ppermute | solution.py:572
  115.2 2.7 %halve.1 = (bf16[192,768]{1,0:T(8,128)(2,1)}, bf16[192,768]{1,0:T(8,128)(2,1)}, bf16[192,768]{1,0:T(8,128)(2,1)}, bf16[192,768]{1,0:T(8,128)(2,1)}) custom-call(s32[1]{0:T(128)} %bitcast.place, bf16[768,768]{1,0:T(8,128)(2,1)} %get-tuple-element.178.mine, bf16[768,768]{1,0:T(8,128)(2,1)} %copy-done.24), custom_call_target="tpu_custom_call" | custom-call | flops 2000000000 | bytes 100000 | tf_op jit(solution)/shard_map/halve/pallas_call | solution.py:218
  123.2 6.8 %query_back.1 = (bf16[192,256]{1,0:T(8,128)(2,1)}, f32[256,768]{1,0:T(8,128)}, f32[8,512]{1,0:T(8,128)}) custom-call(s32[2]{0:T(128)} %lengths.5, s32[1]{0:T(128)} %bitcast.place, bf16[240,256]{1,0:T(8,128)(2,1)} %split.1.grads.refs_8_, bf16[2,3,1024,256]{3,2,1,0:T(8,128)(2,1)} %get-tuple-element.177.states, f32[32,768]{1,0:T(8,128)} %get-tuple-element.182.tan, ...), custom_call_target="tpu_custom_call" | custom-call | flops 6000000000 | bytes 100000 | tf_op jit(solution)/shard_map/query_back/pallas_call | solution.py:218
  131.9 2.6 %mixer_grads.1 = (bf16[112,768]{1,0:T(8,128)(2,1)}, bf16[112,768]{1,0:T(8,128)(2,1)}, bf16[256,768]{1,0:T(8,128)(2,1)}) custom-call(s32[1]{0:T(128)} %bitcast.place, s32[1]{0:T(128)} %bitcast.1.slot.chunk, bf16[256,192]{1,0:T(8,128)(2,1)} %get-tuple-element.140.context, f32[8,768]{1,0:T(8,128)} %get-tuple-element.154.up_sums, ...), custom_call_target="tpu_custom_call" | custom-call | flops 2000000000 | bytes 100000 | tf_op jit(solution)/shard_map/mixer_grads/pallas_call | solution.py:218
  142.3 10.8 %key_back.1 = (bf16[576,256]{1,0:T(8,128)(2,1)}, bf16[128,768]{1,0:T(8,128)(2,1)}, bf16[128,768]{1,0:T(8,128)(2,1)}) custom-call(s32[2]{0:T(128)} %lengths.5, s32[1]{0:T(128)} %bitcast.place, s32[1]{0:T(128)} %bitcast.1.slot.chunk, f32[32,768]{1,0:T(8,128)} %get-tuple-element.192.tan, f32[64,768]{1,0:T(8,128)} %get-tuple-element.193.raw, ...), custom_call_target="tpu_custom_call" | custom-call | flops 12000000000 | bytes 100000 | tf_op jit(solution)/shard_map/key_back/pallas_call | solution.py:218
  159.3 3.1 %collective-permute-done.43.other = bf16[128,768]{1,0:T(8,128)(2,1)S(1)} collective-permute-done((bf16[128,768]{1,0:T(8,128)(2,1)}, bf16[128,768]{1,0:T(8,128)(2,1)S(1)}, u32[]{:S(2)}, u32[]{:S(2)}) %collective-permute-start.43) | collective-permute-done | bytes 196640 | tf_op jit(solution)/shard_map/ppermute | solution.py:572
  171.7 2.4 %join.1.mine = bf16[768,768]{1,0:T(8,128)(2,1)} custom-call(s32[1]{0:T(128)} %bitcast.place, bf16[192,768]{1,0:T(8,128)(2,1)} %settle.1.refs_0_, bf16[192,768]{1,0:T(8,128)(2,1)} %copy-done.12, bf16[192,768]{1,0:T(8,128)(2,1)} %copy-done.11, bf16[192,768]{1,0:T(8,128)(2,1)} %copy-done.10), custom_call_target="tpu_custom_call" | custom-call | flops 300000000 | bytes 100000 | tf_op jit(solution)/shard_map/join/pallas_call | solution.py:218
  183.9 4.5 %collective-permute-done.44.other = bf16[128,768]{1,0:T(8,128)(2,1)S(1)} collective-permute-done((bf16[128,768]{1,0:T(8,128)(2,1)S(1)}, bf16[128,768]{1,0:T(8,128)(2,1)S(1)}, u32[]{:S(2)}, u32[]{:S(2)}) %collective-permute-start.44) | collective-permute-done | bytes 196640 | tf_op jit(solution)/shard_map/ppermute | solution.py:572
  196.4 5.9 %weight_grads.1 = (f32[192,768]{1,0:T(8,128)}, f32[192,768]{1,0:T(8,128)}, f32[192,768]{1,0:T(8,128)}, f32[192]{0:T(256)}, f32[192]{0:T(256)}, /*index=5*/f32[192]{0:T(256)}) custom-call(bf16[576,256]{1,0:T(8,128)(2,1)} %get-tuple-element.228.refs_0_, bf16[576,256]{1,0:T(8,128)(2,1)} %copy-done.17, bf16[576,256]{1,0:T(8,128)(2,1)} %copy-done.16, ...), custom_call_target="tpu_custom_call" | custom-call | flops 300000000 | bytes 100000 | tf_op jit(solution)/shard_map/weight_grads/pallas_call | solution.py:218
  205.0 4.1 %finish_feed.1 = (f32[768,768]{1,0:T(8,128)}, f32[768,768]{1,0:T(8,128)}) custom-call(s32[1]{0:T(128)} %bitcast.place, bf16[768,768]{1,0:T(8,128)(2,1)} %join.1.mine, bf16[768,768]{1,0:T(8,128)(2,1)} %collective-permute-done.61.other), custom_call_target="tpu_custom_call" | custom-call | flops 4000000000 | bytes 100000 | tf_op jit(solution)/shard_map/finish_feed/pallas_call | solution.py:218
  (259 shorter events, 79.3 us)
Async XLA Ops:
  0.7 17.9 %collective-permute-start = (bf16[192,768]{1,0:T(8,128)(2,1)}, bf16[192,768]{1,0:T(8,128)(2,1)S(1)}, u32[]{:S(2)}, u32[]{:S(2)}) collective-permute-start(bf16[192,768]{1,0:T(8,128)(2,1)} %refs_9_.1), channel_id=1, source_target_pairs={{0,2},{1,3},{2,0},{3,1},{4,7},{5,6},{6,5},{7,4},{8,10},{9,11},{10,... | collective-permute-start | bytes 884744 | tf_op jit(solution)/shard_map/ppermute | solution.py:607
  7.7 37.2 %collective-permute-start.8 = (bf16[880,768]{1,0:T(8,128)(2,1)}, bf16[880,768]{1,0:T(8,128)(2,1)S(1)}, u32[]{:S(2)}, u32[]{:S(2)}) collective-permute-start(bf16[880,768]{1,0:T(8,128)(2,1)} %bundle.1), channel_id=1, source_target_pairs={{0,1},{1,0},{2,3},{3,2},{4,5},{5,4},{6,7},{7,6},{8,9},{9,8},{10,11... | collective-permute-start | bytes 4055048 | tf_op jit(solution)/shard_map/ppermute | solution.py:572
  61.1 25.2 %collective-permute-start.21 = (bf16[256,768]{1,0:T(8,128)(2,1)S(1)}, bf16[256,768]{1,0:T(8,128)(2,1)S(1)}, u32[]{:S(2)}, u32[]{:S(2)}) collective-permute-start(bf16[256,768]{1,0:T(8,128)(2,1)S(1)} %copy-done), channel_id=1, source_target_pairs={{0,24},{4,28},{8,16},{12,20},{16,8},{20,12},{24,0},{28,4},{1,25},{... | collective-permute-start | bytes 1179656 | tf_op jit(solution)/shard_map/ppermute | solution.py:572
  63.5 22.9 %collective-permute-start.20 = (bf16[256,768]{1,0:T(8,128)(2,1)S(1)}, bf16[256,768]{1,0:T(8,128)(2,1)S(1)}, u32[]{:S(2)}, u32[]{:S(2)}) collective-permute-start(bf16[256,768]{1,0:T(8,128)(2,1)S(1)} %copy-done), channel_id=1, source_target_pairs={{0,16},{4,20},{8,24},{12,28},{16,0},{20,4},{24,8},{28,12},{1,17},{... | collective-permute-start | bytes 1179656 | tf_op jit(solution)/shard_map/ppermute | solution.py:572
  64.1 22.3 %collective-permute-start.19 = (bf16[256,768]{1,0:T(8,128)(2,1)S(1)}, bf16[256,768]{1,0:T(8,128)(2,1)S(1)}, u32[]{:S(2)}, u32[]{:S(2)}) collective-permute-start(bf16[256,768]{1,0:T(8,128)(2,1)S(1)} %copy-done), channel_id=1, source_target_pairs={{0,8},{4,12},{8,0},{12,4},{16,24},{20,28},{24,16},{28,20},{1,9},{5... | collective-permute-start | bytes 1179656 | tf_op jit(solution)/shard_map/ppermute | solution.py:572
  83.5 15.4 %collective-permute-start.14 = (bf16[128,768]{1,0:T(8,128)(2,1)S(1)}, bf16[128,768]{1,0:T(8,128)(2,1)S(1)}, u32[]{:S(2)}, u32[]{:S(2)}) collective-permute-start(bf16[128,768]{1,0:T(8,128)(2,1)S(1)} %copy-done.41), channel_id=1, source_target_pairs={{0,1},{1,0},{2,3},{3,2},{4,5},{5,4},{6,7},{7,6},{8,9},{9,8},{10,11... | collective-permute-start | bytes 589832 | tf_op jit(solution)/shard_map/ppermute | solution.py:572
  86.3 12.6 %collective-permute-start.17 = (bf16[128,768]{1,0:T(8,128)(2,1)}, bf16[128,768]{1,0:T(8,128)(2,1)S(1)}, u32[]{:S(2)}, u32[]{:S(2)}) collective-permute-start(bf16[128,768]{1,0:T(8,128)(2,1)} %get-tuple-element.153.down_mine), channel_id=1, source_target_pairs={{0,1},{1,0},{2,3},{3,2},{4,5},{5,4},{6,7},{7,6},{8,9},{9,8},{10,11... | collective-permute-start | bytes 589832 | tf_op jit(solution)/shard_map/ppermute | solution.py:572
  94.5 11.0 %collective-permute-start.22 = (bf16[64,192]{1,0:T(8,128)(2,1)}, bf16[64,192]{1,0:T(8,128)(2,1)S(1)}, u32[]{:S(2)}, u32[]{:S(2)}) collective-permute-start(bf16[64,192]{1,0:T(8,128)(2,1)} %get-tuple-element.168), channel_id=1, source_target_pairs={{0,2},{1,3},{2,0},{3,1},{4,6},{5,7},{6,4},{7,5},{8,10},{9,11},{10,... | collective-permute-start | bytes 73736 | tf_op jit(solution)/shard_map/ppermute | solution.py:572
  94.5 11.0 %collective-permute-start.23 = (bf16[64,192]{1,0:T(8,128)(2,1)}, bf16[64,192]{1,0:T(8,128)(2,1)S(1)}, u32[]{:S(2)}, u32[]{:S(2)}) collective-permute-start(bf16[64,192]{1,0:T(8,128)(2,1)} %get-tuple-element.169), channel_id=1, source_target_pairs={{0,1},{1,0},{2,3},{3,2},{4,5},{5,4},{6,7},{7,6},{8,9},{9,8},{10,11... | collective-permute-start | bytes 73736 | tf_op jit(solution)/shard_map/ppermute | solution.py:572
  96.4 9.1 %collective-permute-start.24 = (bf16[64,192]{1,0:T(8,128)(2,1)}, bf16[64,192]{1,0:T(8,128)(2,1)S(1)}, u32[]{:S(2)}, u32[]{:S(2)}) collective-permute-start(bf16[64,192]{1,0:T(8,128)(2,1)} %get-tuple-element.170), channel_id=1, source_target_pairs={{0,3},{1,2},{2,1},{3,0},{4,7},{5,6},{6,5},{7,4},{8,11},{9,10},{10,... | collective-permute-start | bytes 73736 | tf_op jit(solution)/shard_map/ppermute | solution.py:572
  105.5 8.6 %collective-permute-start.25 = (bf16[768,768]{1,0:T(8,128)(2,1)}, bf16[768,768]{1,0:T(8,128)(2,1)S(1)}, u32[]{:S(2)}, u32[]{:S(2)}) collective-permute-start(bf16[768,768]{1,0:T(8,128)(2,1)} %get-tuple-element.179), channel_id=1, source_target_pairs={{0,4},{4,0},{8,12},{12,8},{16,20},{20,16},{24,28},{28,24},{1,5},{5... | collective-permute-start | bytes 3538952 | tf_op jit(solution)/shard_map/ppermute | solution.py:572
  108.0 13.8 %collective-permute-start.28 = (bf16[160,768]{1,0:T(8,128)(2,1)S(1)}, bf16[160,768]{1,0:T(8,128)(2,1)S(1)}, u32[]{:S(2)}, u32[]{:S(2)}) collective-permute-start(bf16[160,768]{1,0:T(8,128)(2,1)S(1)} %copy-done.30), channel_id=1, source_target_pairs={{0,3},{1,2},{2,1},{3,0},{4,7},{5,6},{6,5},{7,4},{8,11},{9,10},{10,... | collective-permute-start | bytes 737288 | tf_op jit(solution)/shard_map/ppermute | solution.py:572
  109.3 8.6 %collective-permute-start.31 = (bf16[240,256]{1,0:T(8,128)(2,1)}, bf16[240,256]{1,0:T(8,128)(2,1)S(1)}, u32[]{:S(2)}, u32[]{:S(2)}) collective-permute-start(bf16[240,256]{1,0:T(8,128)(2,1)} %split.1.grads.refs_8_), channel_id=1, source_target_pairs={{0,24},{4,28},{8,16},{12,20},{16,8},{20,12},{24,0},{28,4},{1,25},{... | collective-permute-start | bytes 368648 | tf_op jit(solution)/shard_map/ppermute | solution.py:572
  110.0 9.6 %collective-permute-start.30 = (bf16[240,256]{1,0:T(8,128)(2,1)}, bf16[240,256]{1,0:T(8,128)(2,1)S(1)}, u32[]{:S(2)}, u32[]{:S(2)}) collective-permute-start(bf16[240,256]{1,0:T(8,128)(2,1)} %split.1.grads.refs_8_), channel_id=1, source_target_pairs={{0,16},{4,20},{8,24},{12,28},{16,0},{20,4},{24,8},{28,12},{1,17},{... | collective-permute-start | bytes 368648 | tf_op jit(solution)/shard_map/ppermute | solution.py:572
  114.2 15.8 %collective-permute-start.27 = (bf16[160,768]{1,0:T(8,128)(2,1)S(1)}, bf16[160,768]{1,0:T(8,128)(2,1)S(1)}, u32[]{:S(2)}, u32[]{:S(2)}) collective-permute-start(bf16[160,768]{1,0:T(8,128)(2,1)S(1)} %copy-done.30), channel_id=1, source_target_pairs={{0,1},{1,0},{2,3},{3,2},{4,5},{5,4},{6,7},{7,6},{8,9},{9,8},{10,11... | collective-permute-start | bytes 737288 | tf_op jit(solution)/shard_map/ppermute | solution.py:572
  117.9 13.3 %collective-permute-start.26 = (bf16[160,768]{1,0:T(8,128)(2,1)S(1)}, bf16[160,768]{1,0:T(8,128)(2,1)S(1)}, u32[]{:S(2)}, u32[]{:S(2)}) collective-permute-start(bf16[160,768]{1,0:T(8,128)(2,1)S(1)} %copy-done.30), channel_id=1, source_target_pairs={{0,2},{1,3},{2,0},{3,1},{4,6},{5,7},{6,4},{7,5},{8,10},{9,11},{10,... | collective-permute-start | bytes 737288 | tf_op jit(solution)/shard_map/ppermute | solution.py:572
  119.6 14.8 %collective-permute-start.32 = (bf16[192,768]{1,0:T(8,128)(2,1)}, bf16[192,768]{1,0:T(8,128)(2,1)S(1)}, u32[]{:S(2)}, u32[]{:S(2)}) collective-permute-start(bf16[192,768]{1,0:T(8,128)(2,1)} %get-tuple-element.200), channel_id=1, source_target_pairs={{0,8},{4,12},{8,0},{12,4},{16,24},{20,28},{24,16},{28,20},{1,9},{5... | collective-permute-start | bytes 884744 | tf_op jit(solution)/shard_map/ppermute | solution.py:572
  120.2 14.9 %collective-permute-start.33 = (bf16[192,768]{1,0:T(8,128)(2,1)}, bf16[192,768]{1,0:T(8,128)(2,1)S(1)}, u32[]{:S(2)}, u32[]{:S(2)}) collective-permute-start(bf16[192,768]{1,0:T(8,128)(2,1)} %get-tuple-element.201), channel_id=1, source_target_pairs={{0,16},{4,20},{8,24},{12,28},{16,0},{20,4},{24,8},{28,12},{1,17},{... | collective-permute-start | bytes 884744 | tf_op jit(solution)/shard_map/ppermute | solution.py:572
  121.8 13.4 %collective-permute-start.34 = (bf16[192,768]{1,0:T(8,128)(2,1)}, bf16[192,768]{1,0:T(8,128)(2,1)S(1)}, u32[]{:S(2)}, u32[]{:S(2)}) collective-permute-start(bf16[192,768]{1,0:T(8,128)(2,1)} %get-tuple-element.202), channel_id=1, source_target_pairs={{0,24},{4,28},{8,16},{12,20},{16,8},{20,12},{24,0},{28,4},{1,25},{... | collective-permute-start | bytes 884744 | tf_op jit(solution)/shard_map/ppermute | solution.py:572
  138.7 14.4 %collective-permute-start.42 = (bf16[192,768]{1,0:T(8,128)(2,1)}, bf16[192,768]{1,0:T(8,128)(2,1)S(1)}, u32[]{:S(2)}, u32[]{:S(2)}) collective-permute-start(bf16[192,768]{1,0:T(8,128)(2,1)} %settle.1.refs_0_), channel_id=1, source_target_pairs={{0,24},{4,28},{8,16},{12,20},{16,8},{20,12},{24,0},{28,4},{1,25},{... | collective-permute-start | bytes 884744 | tf_op jit(solution)/shard_map/ppermute | solution.py:572
  140.3 14.8 %collective-permute-start.41 = (bf16[192,768]{1,0:T(8,128)(2,1)}, bf16[192,768]{1,0:T(8,128)(2,1)S(1)}, u32[]{:S(2)}, u32[]{:S(2)}) collective-permute-start(bf16[192,768]{1,0:T(8,128)(2,1)} %settle.1.refs_0_), channel_id=1, source_target_pairs={{0,16},{4,20},{8,24},{12,28},{16,0},{20,4},{24,8},{28,12},{1,17},{... | collective-permute-start | bytes 884744 | tf_op jit(solution)/shard_map/ppermute | solution.py:572
  140.9 14.8 %collective-permute-start.40 = (bf16[192,768]{1,0:T(8,128)(2,1)}, bf16[192,768]{1,0:T(8,128)(2,1)S(1)}, u32[]{:S(2)}, u32[]{:S(2)}) collective-permute-start(bf16[192,768]{1,0:T(8,128)(2,1)} %settle.1.refs_0_), channel_id=1, source_target_pairs={{0,8},{4,12},{8,0},{12,4},{16,24},{20,28},{24,16},{28,20},{1,9},{5... | collective-permute-start | bytes 884744 | tf_op jit(solution)/shard_map/ppermute | solution.py:572
  142.3 10.8 %collective-permute-start.39 = (bf16[112,768]{1,0:T(8,128)(2,1)S(1)}, bf16[112,768]{1,0:T(8,128)(2,1)S(1)}, u32[]{:S(2)}, u32[]{:S(2)}) collective-permute-start(bf16[112,768]{1,0:T(8,128)(2,1)S(1)} %copy-done.48), channel_id=1, source_target_pairs={{0,4},{4,0},{8,12},{12,8},{16,20},{20,16},{24,28},{28,24},{1,5},{5... | collective-permute-start | bytes 516104 | tf_op jit(solution)/shard_map/ppermute | solution.py:572
  155.7 14.8 %collective-permute-start.51 = (bf16[576,256]{1,0:T(8,128)(2,1)}, bf16[576,256]{1,0:T(8,128)(2,1)S(1)}, u32[]{:S(2)}, u32[]{:S(2)}) collective-permute-start(bf16[576,256]{1,0:T(8,128)(2,1)} %get-tuple-element.228.refs_0_), channel_id=1, source_target_pairs={{0,24},{4,28},{8,16},{12,20},{16,8},{20,12},{24,0},{28,4},{1,25},{... | collective-permute-start | bytes 884744 | tf_op jit(solution)/shard_map/ppermute | solution.py:572
  166.0 9.8 %collective-permute-start.58 = (bf16[112,768]{1,0:T(8,128)(2,1)}, bf16[112,768]{1,0:T(8,128)(2,1)S(1)}, u32[]{:S(2)}, u32[]{:S(2)}) collective-permute-start(bf16[112,768]{1,0:T(8,128)(2,1)} %halve_small.1.refs_0_), channel_id=1, source_target_pairs={{0,16},{4,20},{8,24},{12,28},{16,0},{20,4},{24,8},{28,12},{1,17},{... | collective-permute-start | bytes 516104 | tf_op jit(solution)/shard_map/ppermute | solution.py:572
  167.0 10.6 %collective-permute-start.57 = (bf16[112,768]{1,0:T(8,128)(2,1)}, bf16[112,768]{1,0:T(8,128)(2,1)S(1)}, u32[]{:S(2)}, u32[]{:S(2)}) collective-permute-start(bf16[112,768]{1,0:T(8,128)(2,1)} %halve_small.1.refs_0_), channel_id=1, source_target_pairs={{0,8},{4,12},{8,0},{12,4},{16,24},{20,28},{24,16},{28,20},{1,9},{5... | collective-permute-start | bytes 516104 | tf_op jit(solution)/shard_map/ppermute | solution.py:572
  168.4 13.0 %collective-permute-start.49 = (bf16[576,256]{1,0:T(8,128)(2,1)S(1)}, bf16[576,256]{1,0:T(8,128)(2,1)S(1)}, u32[]{:S(2)}, u32[]{:S(2)}) collective-permute-start(bf16[576,256]{1,0:T(8,128)(2,1)S(1)} %copy-done.13), channel_id=1, source_target_pairs={{0,16},{4,20},{8,24},{12,28},{16,0},{20,4},{24,8},{28,12},{1,17},{... | collective-permute-start | bytes 884744 | tf_op jit(solution)/shard_map/ppermute | solution.py:572
  170.5 13.0 %collective-permute-start.47 = (bf16[576,256]{1,0:T(8,128)(2,1)S(1)}, bf16[576,256]{1,0:T(8,128)(2,1)S(1)}, u32[]{:S(2)}, u32[]{:S(2)}) collective-permute-start(bf16[576,256]{1,0:T(8,128)(2,1)S(1)} %copy-done.13), channel_id=1, source_target_pairs={{0,8},{4,12},{8,0},{12,4},{16,24},{20,28},{24,16},{28,20},{1,9},{5... | collective-permute-start | bytes 884744 | tf_op jit(solution)/shard_map/ppermute | solution.py:572
  171.6 11.8 %collective-permute-start.46 = (bf16[576,256]{1,0:T(8,128)(2,1)S(1)}, bf16[576,256]{1,0:T(8,128)(2,1)S(1)}, u32[]{:S(2)}, u32[]{:S(2)}) collective-permute-start(bf16[576,256]{1,0:T(8,128)(2,1)S(1)} %copy-done.13), channel_id=1, source_target_pairs={{0,4},{4,0},{8,12},{12,8},{16,20},{20,16},{24,28},{28,24},{1,5},{5... | collective-permute-start | bytes 884744 | tf_op jit(solution)/shard_map/ppermute | solution.py:572
  175.7 29.2 %collective-permute-start.61 = (bf16[768,768]{1,0:T(8,128)(2,1)}, bf16[768,768]{1,0:T(8,128)(2,1)}, u32[]{:S(2)}, u32[]{:S(2)}) collective-permute-start(bf16[768,768]{1,0:T(8,128)(2,1)} %join.1.mine), channel_id=1, source_target_pairs={{0,4},{4,0},{8,12},{12,8},{16,20},{20,16},{24,28},{28,24},{1,5},{5... | collective-permute-start | bytes 3538952 | tf_op jit(solution)/shard_map/ppermute | solution.py:572
  177.6 10.8 %collective-permute-start.44 = (bf16[128,768]{1,0:T(8,128)(2,1)S(1)}, bf16[128,768]{1,0:T(8,128)(2,1)S(1)}, u32[]{:S(2)}, u32[]{:S(2)}) collective-permute-start(bf16[128,768]{1,0:T(8,128)(2,1)S(1)} %copy-done.42), channel_id=1, source_target_pairs={{0,2},{1,3},{2,0},{3,1},{4,6},{5,7},{6,4},{7,5},{8,10},{9,11},{10,... | collective-permute-start | bytes 589832 | tf_op jit(solution)/shard_map/ppermute | solution.py:572
  192.7 9.7 %collective-permute-start.45 = (bf16[128,768]{1,0:T(8,128)(2,1)}, bf16[128,768]{1,0:T(8,128)(2,1)S(1)}, u32[]{:S(2)}, u32[]{:S(2)}) collective-permute-start(bf16[128,768]{1,0:T(8,128)(2,1)} %tokens_sum.3.mine), channel_id=1, source_target_pairs={{0,1},{1,0},{2,3},{3,2},{4,5},{5,4},{6,7},{7,6},{8,9},{9,8},{10,11... | collective-permute-start | bytes 589832 | tf_op jit(solution)/shard_map/ppermute | solution.py:572
  (99 other events, 762.0 us)

commit v5 on v4

--- a/solution.py
+++ b/solution.py
@@ -390,6 +390,18 @@
     return unit_back(code_grad, tan[...], raw[...], planes_t[...])
 
 
+def diagonal_sums(rows):
+    lanes = rows.shape[1]
+    total = rows[0:8]
+    for i in range(8, rows.shape[0], 8):
+        total = total + pltpu.roll(rows[i : i + 8], lanes - i, 1)
+    at = lax.broadcasted_iota(jnp.int32, (8, lanes), 0)
+    out = jnp.where(at == 0, total, 0.0)
+    for b in range(1, 8):
+        out = out + jnp.where(at == b, pltpu.roll(total, lanes - b, 1), 0.0)
+    return jnp.sum(out, axis=0, keepdims=True)
+
+
 def query_back_body(
     n, lengths, place, grads, states, tan, raw, choose_back, planes_t, weight, *refs
 ):
@@ -413,23 +425,16 @@
     turned = stacked(raw_grad).astype(BF16)
     grad_out[...] = turned
     input_out[...] = dot(turned.astype(F32).T.astype(BF16), weight[...])
-    near_rev = same_doc(mine * ROWS, ROWS, mine * ROWS - 128, 512, lengths, reverse=True)
-    turn = lax.broadcasted_iota(jnp.int32, (512, 512), 0) + lax.broadcasted_iota(
-        jnp.int32, (512, 512), 1
-    )
-    flip = (turn == 511).astype(F32)
-    flip_low = flip.astype(BF16)
+    near = same_doc(mine * ROWS, ROWS, mine * ROWS - 128, 512, lengths)
     ext = window(packs, mine, 0, HS, n)
     tap_rows = []
     for h in range(HEADS):
         rows, side = grad_rows(grads[...], h)
         context_grad = (rows * side[2:3]).astype(BF16)
-        flipped = dot(ext(h), flip_low).astype(BF16)
-        cross = jnp.where(near_rev, dot_tn(context_grad, flipped), 0.0)
-        cross = pltpu.roll(cross, 0, 1, stride=1, stride_axis=0)
-        tap_rows.append(jnp.sum(cross, axis=0, keepdims=True))
+        cross = jnp.where(near, dot_tn(context_grad, ext(h)), 0.0)
+        tap_rows.append(diagonal_sums(cross))
     tap_rows.append(jnp.zeros((8 - HEADS, 512), F32))
-    taps_out[...] = dot_exact(jnp.concatenate(tap_rows, axis=0), flip)
+    taps_out[...] = jnp.concatenate(tap_rows, axis=0)
 
 
 def query_back(*ins):

time: 209 us -> 208 us (level)
  starting transfers between devices: 52.8 us -> 55.2 us
    ppermute x61, starting transfers between devices: 48.6 us -> 51 us  [swap(): return lax.ppermute(value, axis, [(i, i ^ k) for i in range(n)])]
  transfers between devices with their start and end apart: 62 -> 62, of which waited for: 25 -> 24; matrix products, arithmetic and copies ran while one was open for 1% -> 1% of each run, Pallas kernels for 37% -> 36%
where the time goes in v5:
time: 208 us; the launch traced here: 207 us
  Pallas kernels  85 us (41%)
  starting transfers between devices  55.2 us (27%)
  waiting for transfers between devices  49.5 us (24%)
  local copies, waits for them, and re-layouts  15.9 us (8%)
    pallas_call x23, Pallas kernels, call(): pl.pallas_call(body, out_shape=outs, in_specs=[SMEM] * smem + [VMEM] * (l...  85 us
    ppermute x61, starting transfers between devices, swap(): return lax.ppermute(value, axis, [(i, i ^ k) for i in range(n)])  51 us
    ppermute x61, waiting for transfers between devices, swap(): return lax.ppermute(value, axis, [(i, i ^ k) for i in range(n)])  46.4 us
    unnamed x139, local copies, waits for them, and re-layouts  14.4 us
  transfers between devices with their start and end apart: 62, of which 24 were waited for; matrix products, arithmetic and copies ran while one was open for 1% of the time, Pallas kernels for 36%

profile of v5, /device:TPU:0, one launch (start us, length us, event | category | flops | bytes accessed | tf_op | source)
XLA Modules:
  0.0 207.5 jit_solution(12367049680749281961)
XLA Ops:
  0.7 4.1 %collective-permute-start = (bf16[192,768]{1,0:T(8,128)(2,1)}, bf16[192,768]{1,0:T(8,128)(2,1)S(1)}, u32[]{:S(2)}, u32[]{:S(2)}) collective-permute-start(bf16[192,768]{1,0:T(8,128)(2,1)} %refs_9_.1), channel_id=1, source_target_pairs={{0,2},{1,3},{2,0},{3,1},{4,7},{5,6},{6,5},{7,4},{8,10},{9,11},{10,... | collective-permute-start | bytes 884744 | tf_op jit(solution)/shard_map/ppermute | solution.py:612
  4.8 2.9 %bundle.1 = bf16[880,768]{1,0:T(8,128)(2,1)} custom-call(s32[1]{0:T(128)} %bitcast.place, bf16[768,768]{1,0:T(8,128)(2,1)} %up.5, bf16[768,768]{1,0:T(8,128)(2,1)} %down.5, bf16[192,768]{1,0:T(8,128)(2,1)} %refs_9_.1, f32[768]{0:T(1024)} %up_shift.1), custom_call_target="tpu_custom_call" | custom-call | flops 20000000000 | bytes 100000 | tf_op jit(solution)/shard_map/bundle/pallas_call | solution.py:218
  12.2 3.3 %project.1 = (f32[64,768]{1,0:T(8,128)}, f32[64,768]{1,0:T(8,128)}, f32[32,768]{1,0:T(8,128)}, f32[32,768]{1,0:T(8,128)}, bf16[128,768]{1,0:T(8,128)(2,1)}) custom-call(bf16[256,768]{1,0:T(8,128)(2,1)} %refs_8_, bf16[192,768]{1,0:T(8,128)(2,1)} %bitcast.9, f32[192]{0:T(256)} %bq.1, bf16[192,768]{1,0:T(8,128)(2,1)} %bitcast.11, f32[192]{0:T(256)} %bk.1, ...), custom_call_target="tpu_custom_call" | custom-call | flops 100000000 | bytes 100000 | tf_op jit(solution)/shard_map/project/pallas_call | solution.py:218
  15.4 3.2 %collective-permute-done.refs_10_ = bf16[192,768]{1,0:T(8,128)(2,1)S(1)} collective-permute-done((bf16[192,768]{1,0:T(8,128)(2,1)}, bf16[192,768]{1,0:T(8,128)(2,1)S(1)}, u32[]{:S(2)}, u32[]{:S(2)}) %collective-permute-start) | collective-permute-done | bytes 294944 | tf_op jit(solution)/shard_map/ppermute | solution.py:612
  18.6 2.4 %collective-permute-start.6 = (bf16[128,768]{1,0:T(8,128)(2,1)}, bf16[128,768]{1,0:T(8,128)(2,1)S(1)}, u32[]{:S(2)}, u32[]{:S(2)}) collective-permute-start(bf16[128,768]{1,0:T(8,128)(2,1)} %get-tuple-element.139.refs_0_), channel_id=1, source_target_pairs={{0,24},{4,28},{8,16},{12,20},{16,8},{20,12},{24,0},{28,4},{1,25},{... | collective-permute-start | bytes 589832 | tf_op jit(solution)/shard_map/ppermute | solution.py:577
  22.1 3.3 %collective-permute-done.6.refs_6_ = bf16[128,768]{1,0:T(8,128)(2,1)S(1)} collective-permute-done((bf16[128,768]{1,0:T(8,128)(2,1)}, bf16[128,768]{1,0:T(8,128)(2,1)S(1)}, u32[]{:S(2)}, u32[]{:S(2)}) %collective-permute-start.6) | collective-permute-done | bytes 196640 | tf_op jit(solution)/shard_map/ppermute | solution.py:577
  29.9 8.1 %attend.1 = (bf16[256,192]{1,0:T(8,128)(2,1)}, bf16[128,192]{1,0:T(8,128)(2,1)}, bf16[128,192]{1,0:T(8,128)(2,1)}, f32[192,256]{1,0:T(8,128)}, f32[8,256]{1,0:T(8,128)}, /*index=5*/bf16[2,3,1024,256]{3,2,1,0:T(8,128)(2,1)}) custom-call(s32[2]{0:T(128)} %lengths.5, s32[1]{0:T(128)} %bitcast.place, s32[1]{0:T(128)} %bitcast.1.slot.chunk, f32[8,512]{1,0:T(8,128)} %pad.7.taps, ...), custom_call_target="tpu_custom_call" | custom-call | flops 8999999488 | bytes 100000 | tf_op jit(solution)/shard_map/attend/pallas_call | solution.py:218
  37.9 2.9 %collective-permute-start.9 = (bf16[128,192]{1,0:T(8,128)(2,1)}, bf16[128,192]{1,0:T(8,128)(2,1)S(1)}, u32[]{:S(2)}, u32[]{:S(2)}) collective-permute-start(bf16[128,192]{1,0:T(8,128)(2,1)} %get-tuple-element.141.refs_12_), channel_id=1, source_target_pairs={{0,2},{1,3},{2,0},{3,1},{4,6},{5,7},{6,4},{7,5},{8,10},{9,11},{10,... | collective-permute-start | bytes 147464 | tf_op jit(solution)/shard_map/ppermute | solution.py:577
  40.8 2.8 %collective-permute-done.9.refs_13_ = bf16[128,192]{1,0:T(8,128)(2,1)S(1)} collective-permute-done((bf16[128,192]{1,0:T(8,128)(2,1)}, bf16[128,192]{1,0:T(8,128)(2,1)S(1)}, u32[]{:S(2)}, u32[]{:S(2)}) %collective-permute-start.9) | collective-permute-done | bytes 49184 | tf_op jit(solution)/shard_map/ppermute | solution.py:577
  45.4 2.7 %collective-permute-start.13 = (bf16[128,192]{1,0:T(8,128)(2,1)}, bf16[128,192]{1,0:T(8,128)(2,1)S(1)}, u32[]{:S(2)}, u32[]{:S(2)}) collective-permute-start(bf16[128,192]{1,0:T(8,128)(2,1)} %get-tuple-element.145), channel_id=1, source_target_pairs={{0,3},{1,2},{2,1},{3,0},{4,7},{5,6},{6,5},{7,4},{8,11},{9,10},{10,... | collective-permute-start | bytes 147464 | tf_op jit(solution)/shard_map/ppermute | solution.py:577
  48.4 3.8 %collective-permute-done.13.refs_15_ = bf16[128,192]{1,0:T(8,128)(2,1)S(1)} collective-permute-done((bf16[128,192]{1,0:T(8,128)(2,1)}, bf16[128,192]{1,0:T(8,128)(2,1)S(1)}, u32[]{:S(2)}, u32[]{:S(2)}) %collective-permute-start.13) | collective-permute-done | bytes 49184 | tf_op jit(solution)/shard_map/ppermute | solution.py:577
  54.7 5.7 %feed.1 = (f32[64,768]{1,0:T(8,128)}, f32[64,768]{1,0:T(8,128)}, f32[64,128]{1,0:T(8,128)}, bf16[128,768]{1,0:T(8,128)(2,1)}, f32[128,1536]{1,0:T(8,128)}, /*ind...) custom-call(s32[1]{0:T(128)} %bitcast.place, s32[1]{0:T(128)} %bitcast.1.slot.chunk, ...), custom_call_target="tpu_custom_call" | custom-call | flops 5000000000 | bytes 100000 | tf_op jit(solution)/shard_map/feed/pallas_call | solution.py:218
  60.9 2.6 %collective-permute-start.21 = (bf16[256,768]{1,0:T(8,128)(2,1)S(1)}, bf16[256,768]{1,0:T(8,128)(2,1)S(1)}, u32[]{:S(2)}, u32[]{:S(2)}) collective-permute-start(bf16[256,768]{1,0:T(8,128)(2,1)S(1)} %copy-done), channel_id=1, source_target_pairs={{0,24},{4,28},{8,16},{12,20},{16,8},{20,12},{24,0},{28,4},{1,25},{... | collective-permute-start | bytes 1179656 | tf_op jit(solution)/shard_map/ppermute | solution.py:577
  68.2 2.4 %second_norm.1 = (bf16[80,768]{1,0:T(8,128)(2,1)}, f32[64,768]{1,0:T(8,128)}, bf16[64,768]{1,0:T(8,128)(2,1)}) custom-call(s32[1]{0:T(128)} %bitcast.1.slot.chunk, f32[64,768]{1,0:T(8,128)} %get-tuple-element.148.first, f32[256,768]{1,0:T(8,128)} %out_grad.1, f32[768]{0:T(1024)} %down_shift.1, f32[768]{0:T(1024)} %gain.2, f32[768]{0:T(1024)} %shift.3, ...), custom_call_target="tpu_custom_call" | custom-call | flops 2000000000 | bytes 100000 | tf_op jit(solution)/shard_map/second_norm/pallas_call | solution.py:218
  71.1 5.8 %collective-permute-done.16.low_got = bf16[64,768]{1,0:T(8,128)(2,1)S(1)} collective-permute-done((bf16[64,768]{1,0:T(8,128)(2,1)}, bf16[64,768]{1,0:T(8,128)(2,1)S(1)}, u32[]{:S(2)}, u32[]{:S(2)}) %collective-permute-start.16) | collective-permute-done | bytes 98336 | tf_op jit(solution)/shard_map/ppermute | solution.py:577
  77.5 5.4 %feed_back.1 = (bf16[128,768]{1,0:T(8,128)(2,1)}, f32[64,768]{1,0:T(8,128)}, bf16[64,768]{1,0:T(8,128)(2,1)}) custom-call(s32[1]{0:T(128)} %bitcast.place, s32[1]{0:T(128)} %bitcast.1.slot.chunk, f32[128,1536]{1,0:T(8,128)} %get-tuple-element.147.slope, bf16[768,768]{1,0:T(8,128)(2,1)} %up.5, bf16[768,768]{1,0:T(8,128)(2,1)} %down.5, ...), custom_call_target="tpu_custom_call" | custom-call | flops 500000000 | bytes 100000 | tf_op jit(solution)/shard_map/feed_back/pallas_call | solution.py:218
  83.0 2.5 %collective-permute-start.14 = (bf16[128,768]{1,0:T(8,128)(2,1)S(1)}, bf16[128,768]{1,0:T(8,128)(2,1)S(1)}, u32[]{:S(2)}, u32[]{:S(2)}) collective-permute-start(bf16[128,768]{1,0:T(8,128)(2,1)S(1)} %copy-done.41), channel_id=1, source_target_pairs={{0,1},{1,0},{2,3},{3,2},{4,5},{5,4},{6,7},{7,6},{8,9},{9,8},{10,11... | collective-permute-start | bytes 589832 | tf_op jit(solution)/shard_map/ppermute | solution.py:577
  85.6 3.8 %collective-permute-done.18.got = bf16[64,768]{1,0:T(8,128)(2,1)S(1)} collective-permute-done((bf16[64,768]{1,0:T(8,128)(2,1)}, bf16[64,768]{1,0:T(8,128)(2,1)S(1)}, u32[]{:S(2)}, u32[]{:S(2)}) %collective-permute-start.18) | collective-permute-done | bytes 98336 | tf_op jit(solution)/shard_map/ppermute | solution.py:577
  90.0 2.9 %first_norm_back.1 = (f32[64,768]{1,0:T(8,128)}, bf16[160,768]{1,0:T(8,128)(2,1)}, bf16[64,192]{1,0:T(8,128)(2,1)}, bf16[64,192]{1,0:T(8,128)(2,1)}, bf16[64,192]{1,0:T(8,128)(2,1)}, /*index=5*/bf16[64,192]{1,0:T(8,128)(2,1)}) custom-call(f32[64,768]{1,0:T(8,128)} %get-tuple-element.155.grad, f32[64,768]{1,0:T(8,128)} %get-tuple-element.156.normed, ...), custom_call_target="tpu_custom_call" | custom-call | flops 3000000000 | bytes 100000 | tf_op jit(solution)/shard_map/first_norm_back/pallas_call | solution.py:218
  92.9 2.3 %collective-permute-start.23 = (bf16[64,192]{1,0:T(8,128)(2,1)}, bf16[64,192]{1,0:T(8,128)(2,1)S(1)}, u32[]{:S(2)}, u32[]{:S(2)}) collective-permute-start(bf16[64,192]{1,0:T(8,128)(2,1)} %get-tuple-element.169), channel_id=1, source_target_pairs={{0,1},{1,0},{2,3},{3,2},{4,5},{5,4},{6,7},{7,6},{8,9},{9,8},{10,11... | collective-permute-start | bytes 73736 | tf_op jit(solution)/shard_map/ppermute | solution.py:577
  98.6 5.2 %feed_grads.1 = (bf16[768,768]{1,0:T(8,128)(2,1)}, bf16[768,768]{1,0:T(8,128)(2,1)}, f32[8,768]{1,0:T(8,128)}) custom-call(s32[1]{0:T(128)} %bitcast.place, s32[1]{0:T(128)} %bitcast.1.slot.chunk, bf16[128,768]{1,0:T(8,128)(2,1)} %get-tuple-element.146.low_mine, bf16[128,768]{1,0:T(8,128)(2,1)} %copy-done.44, bf16[128,768]{1,0:T(8,128)(2,1)} %get-tuple-element.153.down_mine, ...), custom_call_target="tpu_custom_call" | custom-call | flops 6000000000 | bytes 100000 | tf_op jit(solution)/shard_map/feed_grads/pallas_call | solution.py:218
  114.4 2.7 %halve.1 = (bf16[192,768]{1,0:T(8,128)(2,1)}, bf16[192,768]{1,0:T(8,128)(2,1)}, bf16[192,768]{1,0:T(8,128)(2,1)}, bf16[192,768]{1,0:T(8,128)(2,1)}) custom-call(s32[1]{0:T(128)} %bitcast.place, bf16[768,768]{1,0:T(8,128)(2,1)} %get-tuple-element.178.mine, bf16[768,768]{1,0:T(8,128)(2,1)} %copy-done.24), custom_call_target="tpu_custom_call" | custom-call | flops 2000000000 | bytes 100000 | tf_op jit(solution)/shard_map/halve/pallas_call | solution.py:218
  121.9 6.2 %query_back.1 = (bf16[192,256]{1,0:T(8,128)(2,1)}, f32[256,768]{1,0:T(8,128)}, f32[8,512]{1,0:T(8,128)}) custom-call(s32[2]{0:T(128)} %lengths.5, s32[1]{0:T(128)} %bitcast.place, bf16[240,256]{1,0:T(8,128)(2,1)} %split.1.grads.refs_8_, bf16[2,3,1024,256]{3,2,1,0:T(8,128)(2,1)} %get-tuple-element.177.states, f32[32,768]{1,0:T(8,128)} %get-tuple-element.182.tan, ...), custom_call_target="tpu_custom_call" | custom-call | flops 6000000000 | bytes 100000 | tf_op jit(solution)/shard_map/query_back/pallas_call | solution.py:218
  131.0 2.6 %mixer_grads.1 = (bf16[112,768]{1,0:T(8,128)(2,1)}, bf16[112,768]{1,0:T(8,128)(2,1)}, bf16[256,768]{1,0:T(8,128)(2,1)}) custom-call(s32[1]{0:T(128)} %bitcast.place, s32[1]{0:T(128)} %bitcast.1.slot.chunk, bf16[256,192]{1,0:T(8,128)(2,1)} %get-tuple-element.140.context, f32[8,768]{1,0:T(8,128)} %get-tuple-element.154.up_sums, ...), custom_call_target="tpu_custom_call" | custom-call | flops 2000000000 | bytes 100000 | tf_op jit(solution)/shard_map/mixer_grads/pallas_call | solution.py:218
  141.5 10.2 %key_back.1 = (bf16[576,256]{1,0:T(8,128)(2,1)}, bf16[128,768]{1,0:T(8,128)(2,1)}, bf16[128,768]{1,0:T(8,128)(2,1)}) custom-call(s32[2]{0:T(128)} %lengths.5, s32[1]{0:T(128)} %bitcast.place, s32[1]{0:T(128)} %bitcast.1.slot.chunk, f32[32,768]{1,0:T(8,128)} %get-tuple-element.192.tan, f32[64,768]{1,0:T(8,128)} %get-tuple-element.193.raw, ...), custom_call_target="tpu_custom_call" | custom-call | flops 12000000000 | bytes 100000 | tf_op jit(solution)/shard_map/key_back/pallas_call | solution.py:218
  151.7 2.4 %collective-permute-done.41.refs_2_ = bf16[192,768]{1,0:T(8,128)(2,1)S(1)} collective-permute-done((bf16[192,768]{1,0:T(8,128)(2,1)}, bf16[192,768]{1,0:T(8,128)(2,1)S(1)}, u32[]{:S(2)}, u32[]{:S(2)}) %collective-permute-start.41) | collective-permute-done | bytes 294944 | tf_op jit(solution)/shard_map/ppermute | solution.py:577
  157.9 3.4 %collective-permute-done.43.other = bf16[128,768]{1,0:T(8,128)(2,1)S(1)} collective-permute-done((bf16[128,768]{1,0:T(8,128)(2,1)}, bf16[128,768]{1,0:T(8,128)(2,1)S(1)}, u32[]{:S(2)}, u32[]{:S(2)}) %collective-permute-start.43) | collective-permute-done | bytes 196640 | tf_op jit(solution)/shard_map/ppermute | solution.py:577
  169.2 2.9 %collective-permute-done.59.refs_3_ = bf16[112,768]{1,0:T(8,128)(2,1)S(1)} collective-permute-done((bf16[112,768]{1,0:T(8,128)(2,1)}, bf16[112,768]{1,0:T(8,128)(2,1)S(1)}, u32[]{:S(2)}, u32[]{:S(2)}) %collective-permute-start.59) | collective-permute-done | bytes 172064 | tf_op jit(solution)/shard_map/ppermute | solution.py:577
  172.1 2.4 %join.1.mine = bf16[768,768]{1,0:T(8,128)(2,1)} custom-call(s32[1]{0:T(128)} %bitcast.place, bf16[192,768]{1,0:T(8,128)(2,1)} %settle.1.refs_0_, bf16[192,768]{1,0:T(8,128)(2,1)} %copy-done.12, bf16[192,768]{1,0:T(8,128)(2,1)} %copy-done.11, bf16[192,768]{1,0:T(8,128)(2,1)} %copy-done.10), custom_call_target="tpu_custom_call" | custom-call | flops 300000000 | bytes 100000 | tf_op jit(solution)/shard_map/join/pallas_call | solution.py:218
  180.7 6.1 %collective-permute-done.44.other = bf16[128,768]{1,0:T(8,128)(2,1)S(1)} collective-permute-done((bf16[128,768]{1,0:T(8,128)(2,1)S(1)}, bf16[128,768]{1,0:T(8,128)(2,1)S(1)}, u32[]{:S(2)}, u32[]{:S(2)}) %collective-permute-start.44) | collective-permute-done | bytes 196640 | tf_op jit(solution)/shard_map/ppermute | solution.py:577
  194.8 5.9 %weight_grads.1 = (f32[192,768]{1,0:T(8,128)}, f32[192,768]{1,0:T(8,128)}, f32[192,768]{1,0:T(8,128)}, f32[192]{0:T(256)}, f32[192]{0:T(256)}, /*index=5*/f32[192]{0:T(256)}) custom-call(bf16[576,256]{1,0:T(8,128)(2,1)} %get-tuple-element.228.refs_0_, bf16[576,256]{1,0:T(8,128)(2,1)} %copy-done.17, bf16[576,256]{1,0:T(8,128)(2,1)} %copy-done.16, ...), custom_call_target="tpu_custom_call" | custom-call | flops 300000000 | bytes 100000 | tf_op jit(solution)/shard_map/weight_grads/pallas_call | solution.py:218
  203.3 4.1 %finish_feed.1 = (f32[768,768]{1,0:T(8,128)}, f32[768,768]{1,0:T(8,128)}) custom-call(s32[1]{0:T(128)} %bitcast.place, bf16[768,768]{1,0:T(8,128)(2,1)} %join.1.mine, bf16[768,768]{1,0:T(8,128)(2,1)} %collective-permute-done.61.other), custom_call_target="tpu_custom_call" | custom-call | flops 4000000000 | bytes 100000 | tf_op jit(solution)/shard_map/finish_feed/pallas_call | solution.py:218
  (259 shorter events, 79.3 us)
Async XLA Ops:
  0.7 17.9 %collective-permute-start = (bf16[192,768]{1,0:T(8,128)(2,1)}, bf16[192,768]{1,0:T(8,128)(2,1)S(1)}, u32[]{:S(2)}, u32[]{:S(2)}) collective-permute-start(bf16[192,768]{1,0:T(8,128)(2,1)} %refs_9_.1), channel_id=1, source_target_pairs={{0,2},{1,3},{2,0},{3,1},{4,7},{5,6},{6,5},{7,4},{8,10},{9,11},{10,... | collective-permute-start | bytes 884744 | tf_op jit(solution)/shard_map/ppermute | solution.py:612
  7.7 37.2 %collective-permute-start.8 = (bf16[880,768]{1,0:T(8,128)(2,1)}, bf16[880,768]{1,0:T(8,128)(2,1)S(1)}, u32[]{:S(2)}, u32[]{:S(2)}) collective-permute-start(bf16[880,768]{1,0:T(8,128)(2,1)} %bundle.1), channel_id=1, source_target_pairs={{0,1},{1,0},{2,3},{3,2},{4,5},{5,4},{6,7},{7,6},{8,9},{9,8},{10,11... | collective-permute-start | bytes 4055048 | tf_op jit(solution)/shard_map/ppermute | solution.py:577
  60.9 24.6 %collective-permute-start.21 = (bf16[256,768]{1,0:T(8,128)(2,1)S(1)}, bf16[256,768]{1,0:T(8,128)(2,1)S(1)}, u32[]{:S(2)}, u32[]{:S(2)}) collective-permute-start(bf16[256,768]{1,0:T(8,128)(2,1)S(1)} %copy-done), channel_id=1, source_target_pairs={{0,24},{4,28},{8,16},{12,20},{16,8},{20,12},{24,0},{28,4},{1,25},{... | collective-permute-start | bytes 1179656 | tf_op jit(solution)/shard_map/ppermute | solution.py:577
  63.5 22.1 %collective-permute-start.20 = (bf16[256,768]{1,0:T(8,128)(2,1)S(1)}, bf16[256,768]{1,0:T(8,128)(2,1)S(1)}, u32[]{:S(2)}, u32[]{:S(2)}) collective-permute-start(bf16[256,768]{1,0:T(8,128)(2,1)S(1)} %copy-done), channel_id=1, source_target_pairs={{0,16},{4,20},{8,24},{12,28},{16,0},{20,4},{24,8},{28,12},{1,17},{... | collective-permute-start | bytes 1179656 | tf_op jit(solution)/shard_map/ppermute | solution.py:577
  65.0 20.6 %collective-permute-start.19 = (bf16[256,768]{1,0:T(8,128)(2,1)S(1)}, bf16[256,768]{1,0:T(8,128)(2,1)S(1)}, u32[]{:S(2)}, u32[]{:S(2)}) collective-permute-start(bf16[256,768]{1,0:T(8,128)(2,1)S(1)} %copy-done), channel_id=1, source_target_pairs={{0,8},{4,12},{8,0},{12,4},{16,24},{20,28},{24,16},{28,20},{1,9},{5... | collective-permute-start | bytes 1179656 | tf_op jit(solution)/shard_map/ppermute | solution.py:577
  83.0 14.3 %collective-permute-start.14 = (bf16[128,768]{1,0:T(8,128)(2,1)S(1)}, bf16[128,768]{1,0:T(8,128)(2,1)S(1)}, u32[]{:S(2)}, u32[]{:S(2)}) collective-permute-start(bf16[128,768]{1,0:T(8,128)(2,1)S(1)} %copy-done.41), channel_id=1, source_target_pairs={{0,1},{1,0},{2,3},{3,2},{4,5},{5,4},{6,7},{7,6},{8,9},{9,8},{10,11... | collective-permute-start | bytes 589832 | tf_op jit(solution)/shard_map/ppermute | solution.py:577
  85.5 11.8 %collective-permute-start.17 = (bf16[128,768]{1,0:T(8,128)(2,1)}, bf16[128,768]{1,0:T(8,128)(2,1)S(1)}, u32[]{:S(2)}, u32[]{:S(2)}) collective-permute-start(bf16[128,768]{1,0:T(8,128)(2,1)} %get-tuple-element.153.down_mine), channel_id=1, source_target_pairs={{0,1},{1,0},{2,3},{3,2},{4,5},{5,4},{6,7},{7,6},{8,9},{9,8},{10,11... | collective-permute-start | bytes 589832 | tf_op jit(solution)/shard_map/ppermute | solution.py:577
  92.9 11.0 %collective-permute-start.22 = (bf16[64,192]{1,0:T(8,128)(2,1)}, bf16[64,192]{1,0:T(8,128)(2,1)S(1)}, u32[]{:S(2)}, u32[]{:S(2)}) collective-permute-start(bf16[64,192]{1,0:T(8,128)(2,1)} %get-tuple-element.168), channel_id=1, source_target_pairs={{0,2},{1,3},{2,0},{3,1},{4,6},{5,7},{6,4},{7,5},{8,10},{9,11},{10,... | collective-permute-start | bytes 73736 | tf_op jit(solution)/shard_map/ppermute | solution.py:577
  92.9 11.0 %collective-permute-start.23 = (bf16[64,192]{1,0:T(8,128)(2,1)}, bf16[64,192]{1,0:T(8,128)(2,1)S(1)}, u32[]{:S(2)}, u32[]{:S(2)}) collective-permute-start(bf16[64,192]{1,0:T(8,128)(2,1)} %get-tuple-element.169), channel_id=1, source_target_pairs={{0,1},{1,0},{2,3},{3,2},{4,5},{5,4},{6,7},{7,6},{8,9},{9,8},{10,11... | collective-permute-start | bytes 73736 | tf_op jit(solution)/shard_map/ppermute | solution.py:577
  95.2 8.7 %collective-permute-start.24 = (bf16[64,192]{1,0:T(8,128)(2,1)}, bf16[64,192]{1,0:T(8,128)(2,1)S(1)}, u32[]{:S(2)}, u32[]{:S(2)}) collective-permute-start(bf16[64,192]{1,0:T(8,128)(2,1)} %get-tuple-element.170), channel_id=1, source_target_pairs={{0,3},{1,2},{2,1},{3,0},{4,7},{5,6},{6,5},{7,4},{8,11},{9,10},{10,... | collective-permute-start | bytes 73736 | tf_op jit(solution)/shard_map/ppermute | solution.py:577
  103.9 9.5 %collective-permute-start.25 = (bf16[768,768]{1,0:T(8,128)(2,1)}, bf16[768,768]{1,0:T(8,128)(2,1)S(1)}, u32[]{:S(2)}, u32[]{:S(2)}) collective-permute-start(bf16[768,768]{1,0:T(8,128)(2,1)} %get-tuple-element.179), channel_id=1, source_target_pairs={{0,4},{4,0},{8,12},{12,8},{16,20},{20,16},{24,28},{28,24},{1,5},{5... | collective-permute-start | bytes 3538952 | tf_op jit(solution)/shard_map/ppermute | solution.py:577
  106.3 14.1 %collective-permute-start.28 = (bf16[160,768]{1,0:T(8,128)(2,1)S(1)}, bf16[160,768]{1,0:T(8,128)(2,1)S(1)}, u32[]{:S(2)}, u32[]{:S(2)}) collective-permute-start(bf16[160,768]{1,0:T(8,128)(2,1)S(1)} %copy-done.30), channel_id=1, source_target_pairs={{0,3},{1,2},{2,1},{3,0},{4,7},{5,6},{6,5},{7,4},{8,11},{9,10},{10,... | collective-permute-start | bytes 737288 | tf_op jit(solution)/shard_map/ppermute | solution.py:577
  108.1 9.0 %collective-permute-start.31 = (bf16[240,256]{1,0:T(8,128)(2,1)}, bf16[240,256]{1,0:T(8,128)(2,1)S(1)}, u32[]{:S(2)}, u32[]{:S(2)}) collective-permute-start(bf16[240,256]{1,0:T(8,128)(2,1)} %split.1.grads.refs_8_), channel_id=1, source_target_pairs={{0,24},{4,28},{8,16},{12,20},{16,8},{20,12},{24,0},{28,4},{1,25},{... | collective-permute-start | bytes 368648 | tf_op jit(solution)/shard_map/ppermute | solution.py:577
  113.4 14.8 %collective-permute-start.27 = (bf16[160,768]{1,0:T(8,128)(2,1)S(1)}, bf16[160,768]{1,0:T(8,128)(2,1)S(1)}, u32[]{:S(2)}, u32[]{:S(2)}) collective-permute-start(bf16[160,768]{1,0:T(8,128)(2,1)S(1)} %copy-done.30), channel_id=1, source_target_pairs={{0,1},{1,0},{2,3},{3,2},{4,5},{5,4},{6,7},{7,6},{8,9},{9,8},{10,11... | collective-permute-start | bytes 737288 | tf_op jit(solution)/shard_map/ppermute | solution.py:577
  117.1 13.2 %collective-permute-start.26 = (bf16[160,768]{1,0:T(8,128)(2,1)S(1)}, bf16[160,768]{1,0:T(8,128)(2,1)S(1)}, u32[]{:S(2)}, u32[]{:S(2)}) collective-permute-start(bf16[160,768]{1,0:T(8,128)(2,1)S(1)} %copy-done.30), channel_id=1, source_target_pairs={{0,2},{1,3},{2,0},{3,1},{4,6},{5,7},{6,4},{7,5},{8,10},{9,11},{10,... | collective-permute-start | bytes 737288 | tf_op jit(solution)/shard_map/ppermute | solution.py:577
  118.3 15.3 %collective-permute-start.32 = (bf16[192,768]{1,0:T(8,128)(2,1)}, bf16[192,768]{1,0:T(8,128)(2,1)S(1)}, u32[]{:S(2)}, u32[]{:S(2)}) collective-permute-start(bf16[192,768]{1,0:T(8,128)(2,1)} %get-tuple-element.200), channel_id=1, source_target_pairs={{0,8},{4,12},{8,0},{12,4},{16,24},{20,28},{24,16},{28,20},{1,9},{5... | collective-permute-start | bytes 884744 | tf_op jit(solution)/shard_map/ppermute | solution.py:577
  119.4 14.9 %collective-permute-start.33 = (bf16[192,768]{1,0:T(8,128)(2,1)}, bf16[192,768]{1,0:T(8,128)(2,1)S(1)}, u32[]{:S(2)}, u32[]{:S(2)}) collective-permute-start(bf16[192,768]{1,0:T(8,128)(2,1)} %get-tuple-element.201), channel_id=1, source_target_pairs={{0,16},{4,20},{8,24},{12,28},{16,0},{20,4},{24,8},{28,12},{1,17},{... | collective-permute-start | bytes 884744 | tf_op jit(solution)/shard_map/ppermute | solution.py:577
  120.4 13.9 %collective-permute-start.34 = (bf16[192,768]{1,0:T(8,128)(2,1)}, bf16[192,768]{1,0:T(8,128)(2,1)S(1)}, u32[]{:S(2)}, u32[]{:S(2)}) collective-permute-start(bf16[192,768]{1,0:T(8,128)(2,1)} %get-tuple-element.202), channel_id=1, source_target_pairs={{0,24},{4,28},{8,16},{12,20},{16,8},{20,12},{24,0},{28,4},{1,25},{... | collective-permute-start | bytes 884744 | tf_op jit(solution)/shard_map/ppermute | solution.py:577
  128.2 9.7 %collective-permute-start.35 = (bf16[240,256]{1,0:T(8,128)(2,1)S(1)}, bf16[240,256]{1,0:T(8,128)(2,1)S(1)}, u32[]{:S(2)}, u32[]{:S(2)}) collective-permute-start(bf16[240,256]{1,0:T(8,128)(2,1)S(1)} %copy-done.53), channel_id=1, source_target_pairs={{0,4},{4,0},{8,12},{12,8},{16,20},{20,16},{24,28},{28,24},{1,5},{5... | collective-permute-start | bytes 368648 | tf_op jit(solution)/shard_map/ppermute | solution.py:577
  137.9 13.8 %collective-permute-start.42 = (bf16[192,768]{1,0:T(8,128)(2,1)}, bf16[192,768]{1,0:T(8,128)(2,1)S(1)}, u32[]{:S(2)}, u32[]{:S(2)}) collective-permute-start(bf16[192,768]{1,0:T(8,128)(2,1)} %settle.1.refs_0_), channel_id=1, source_target_pairs={{0,24},{4,28},{8,16},{12,20},{16,8},{20,12},{24,0},{28,4},{1,25},{... | collective-permute-start | bytes 884744 | tf_op jit(solution)/shard_map/ppermute | solution.py:577
  138.8 15.4 %collective-permute-start.41 = (bf16[192,768]{1,0:T(8,128)(2,1)}, bf16[192,768]{1,0:T(8,128)(2,1)S(1)}, u32[]{:S(2)}, u32[]{:S(2)}) collective-permute-start(bf16[192,768]{1,0:T(8,128)(2,1)} %settle.1.refs_0_), channel_id=1, source_target_pairs={{0,16},{4,20},{8,24},{12,28},{16,0},{20,4},{24,8},{28,12},{1,17},{... | collective-permute-start | bytes 884744 | tf_op jit(solution)/shard_map/ppermute | solution.py:577
  139.8 14.7 %collective-permute-start.40 = (bf16[192,768]{1,0:T(8,128)(2,1)}, bf16[192,768]{1,0:T(8,128)(2,1)S(1)}, u32[]{:S(2)}, u32[]{:S(2)}) collective-permute-start(bf16[192,768]{1,0:T(8,128)(2,1)} %settle.1.refs_0_), channel_id=1, source_target_pairs={{0,8},{4,12},{8,0},{12,4},{16,24},{20,28},{24,16},{28,20},{1,9},{5... | collective-permute-start | bytes 884744 | tf_op jit(solution)/shard_map/ppermute | solution.py:577
  141.5 10.2 %collective-permute-start.39 = (bf16[112,768]{1,0:T(8,128)(2,1)S(1)}, bf16[112,768]{1,0:T(8,128)(2,1)S(1)}, u32[]{:S(2)}, u32[]{:S(2)}) collective-permute-start(bf16[112,768]{1,0:T(8,128)(2,1)S(1)} %copy-done.48), channel_id=1, source_target_pairs={{0,4},{4,0},{8,12},{12,8},{16,20},{20,16},{24,28},{28,24},{1,5},{5... | collective-permute-start | bytes 516104 | tf_op jit(solution)/shard_map/ppermute | solution.py:577
  154.5 13.9 %collective-permute-start.51 = (bf16[576,256]{1,0:T(8,128)(2,1)}, bf16[576,256]{1,0:T(8,128)(2,1)S(1)}, u32[]{:S(2)}, u32[]{:S(2)}) collective-permute-start(bf16[576,256]{1,0:T(8,128)(2,1)} %get-tuple-element.228.refs_0_), channel_id=1, source_target_pairs={{0,24},{4,28},{8,16},{12,20},{16,8},{20,12},{24,0},{28,4},{1,25},{... | collective-permute-start | bytes 884744 | tf_op jit(solution)/shard_map/ppermute | solution.py:577
  165.2 9.3 %collective-permute-start.58 = (bf16[112,768]{1,0:T(8,128)(2,1)}, bf16[112,768]{1,0:T(8,128)(2,1)S(1)}, u32[]{:S(2)}, u32[]{:S(2)}) collective-permute-start(bf16[112,768]{1,0:T(8,128)(2,1)} %halve_small.1.refs_0_), channel_id=1, source_target_pairs={{0,16},{4,20},{8,24},{12,28},{16,0},{20,4},{24,8},{28,12},{1,17},{... | collective-permute-start | bytes 516104 | tf_op jit(solution)/shard_map/ppermute | solution.py:577
  165.8 9.7 %collective-permute-start.57 = (bf16[112,768]{1,0:T(8,128)(2,1)}, bf16[112,768]{1,0:T(8,128)(2,1)S(1)}, u32[]{:S(2)}, u32[]{:S(2)}) collective-permute-start(bf16[112,768]{1,0:T(8,128)(2,1)} %halve_small.1.refs_0_), channel_id=1, source_target_pairs={{0,8},{4,12},{8,0},{12,4},{16,24},{20,28},{24,16},{28,20},{1,9},{5... | collective-permute-start | bytes 516104 | tf_op jit(solution)/shard_map/ppermute | solution.py:577
  167.2 12.8 %collective-permute-start.49 = (bf16[576,256]{1,0:T(8,128)(2,1)S(1)}, bf16[576,256]{1,0:T(8,128)(2,1)S(1)}, u32[]{:S(2)}, u32[]{:S(2)}) collective-permute-start(bf16[576,256]{1,0:T(8,128)(2,1)S(1)} %copy-done.13), channel_id=1, source_target_pairs={{0,16},{4,20},{8,24},{12,28},{16,0},{20,4},{24,8},{28,12},{1,17},{... | collective-permute-start | bytes 884744 | tf_op jit(solution)/shard_map/ppermute | solution.py:577
  168.5 11.6 %collective-permute-start.47 = (bf16[576,256]{1,0:T(8,128)(2,1)S(1)}, bf16[576,256]{1,0:T(8,128)(2,1)S(1)}, u32[]{:S(2)}, u32[]{:S(2)}) collective-permute-start(bf16[576,256]{1,0:T(8,128)(2,1)S(1)} %copy-done.13), channel_id=1, source_target_pairs={{0,8},{4,12},{8,0},{12,4},{16,24},{20,28},{24,16},{28,20},{1,9},{5... | collective-permute-start | bytes 884744 | tf_op jit(solution)/shard_map/ppermute | solution.py:577
  172.1 8.5 %collective-permute-start.46 = (bf16[576,256]{1,0:T(8,128)(2,1)S(1)}, bf16[576,256]{1,0:T(8,128)(2,1)S(1)}, u32[]{:S(2)}, u32[]{:S(2)}) collective-permute-start(bf16[576,256]{1,0:T(8,128)(2,1)S(1)} %copy-done.13), channel_id=1, source_target_pairs={{0,4},{4,0},{8,12},{12,8},{16,20},{20,16},{24,28},{28,24},{1,5},{5... | collective-permute-start | bytes 884744 | tf_op jit(solution)/shard_map/ppermute | solution.py:577
  174.5 28.8 %collective-permute-start.61 = (bf16[768,768]{1,0:T(8,128)(2,1)}, bf16[768,768]{1,0:T(8,128)(2,1)}, u32[]{:S(2)}, u32[]{:S(2)}) collective-permute-start(bf16[768,768]{1,0:T(8,128)(2,1)} %join.1.mine), channel_id=1, source_target_pairs={{0,4},{4,0},{8,12},{12,8},{16,20},{20,16},{24,28},{28,24},{1,5},{5... | collective-permute-start | bytes 3538952 | tf_op jit(solution)/shard_map/ppermute | solution.py:577
  175.5 11.3 %collective-permute-start.44 = (bf16[128,768]{1,0:T(8,128)(2,1)S(1)}, bf16[128,768]{1,0:T(8,128)(2,1)S(1)}, u32[]{:S(2)}, u32[]{:S(2)}) collective-permute-start(bf16[128,768]{1,0:T(8,128)(2,1)S(1)} %copy-done.42), channel_id=1, source_target_pairs={{0,2},{1,3},{2,0},{3,1},{4,6},{5,7},{6,4},{7,5},{8,10},{9,11},{10,... | collective-permute-start | bytes 589832 | tf_op jit(solution)/shard_map/ppermute | solution.py:577
  191.1 9.7 %collective-permute-start.45 = (bf16[128,768]{1,0:T(8,128)(2,1)}, bf16[128,768]{1,0:T(8,128)(2,1)S(1)}, u32[]{:S(2)}, u32[]{:S(2)}) collective-permute-start(bf16[128,768]{1,0:T(8,128)(2,1)} %tokens_sum.3.mine), channel_id=1, source_target_pairs={{0,1},{1,0},{2,3},{3,2},{4,5},{5,4},{6,7},{7,6},{8,9},{9,8},{10,11... | collective-permute-start | bytes 589832 | tf_op jit(solution)/shard_map/ppermute | solution.py:577
  (99 other events, 762.2 us)
